TPU v7x, 32 devices: a whole 2x2x4 slice. The times are simulated.
32 devices in a mesh: seq: 4 (over z), tm: 8 (over y, x, core).
Axes of the slice: x: 2, y: 2, z: 4, core: 2. Of those that a mesh axis runs over, the one named last changes fastest.
Arguments:
- inputs: bfloat16 [8, 1024, 2304], P('seq', 'tm'), may hold values from -6 to 6
- weight_one: bfloat16 [2, 3, 2304, 2304], P(None, None, 'tm'), may hold values from -0.09375 to 0.09375
- fbias_one: float32 [2304], P('tm'), may hold values from 2 to 9, as said below
- weight_two: bfloat16 [2, 3, 2304, 2304], P(None, None, 'tm'), may hold values from -0.09375 to 0.09375
- fbias_two: float32 [2304], P('tm'), may hold values from 2 to 9, as said below
- cotangent: bfloat16 [8, 1024, 2304], P('seq', 'tm'), may hold values from -6 to 6
- cluster_starts: int32 [8, 4], P('seq'), may hold values from 512 to 992
Outputs:
- hidden_two: bfloat16 [8, 1024, 2304], P('seq', 'tm')
- input_grad: bfloat16 [8, 1024, 2304], P('seq', 'tm')
- grad_weight_one: float32 [2, 3, 2304, 2304], P(None, None, 'tm')
- grad_fbias_one: float32 [2304], P('tm')
- grad_weight_two: float32 [2, 3, 2304, 2304], P(None, None, 'tm')
- grad_fbias_two: float32 [2304], P('tm')
Inputs may be any that keep to these rules, and one draw needn't show every extreme that they name: `fbias_one`: forget gate biases, spread between fast and slow forgetting over the hidden units. `fbias_two`: forget gate biases, spread between fast and slow forgetting over the hidden units. `cluster_starts`: each start lies in the second half of its sequence, with room for a whole cluster; clusters may intersect.
All inputs are finite; a program needn't handle non-finite values.
Results may differ from a plain program's by a relative error of at most 0.011.
Values may be sent and summed in bfloat16 or wider, within the bound.
A program may use at most 320 MiB of HBM per device.

v0:
```python
import jax
import jax.numpy as jnp
from jax import lax
from jax.sharding import PartitionSpec as P

CLUSTER = 32


def entering(value, axis, join, neutral, backward):
    count, mine = (lax.axis_size(axis), lax.axis_index(axis))
    pieces = jax.tree.map(lambda part: lax.all_gather(part, axis), value)
    if backward:
        pieces = jax.tree.map(lambda part: part[::-1], pieces)
        mine = count - 1 - mine
    subtotal = jax.tree.map(
        lambda part, zero: jnp.full_like(part, 0) + jnp.asarray(zero, part.dtype), value, neutral
    )

    def lap(position, subtotal):
        longer = join(subtotal, jax.tree.map(lambda part: part[position], pieces))
        return jax.tree.map(lambda new, old: jnp.where(position < mine, new, old), longer, subtotal)

    return lax.fori_loop(0, count - 1, lap, subtotal)


def affine_chain(earlier, later):
    return (earlier[0] * later[0], later[0] * earlier[1] + later[1])


def activate(preact):
    values = preact.astype(jnp.float32)
    return (
        jnp.tanh(values[:, :, 0]),
        jax.nn.sigmoid(values[:, :, 1]),
        jax.nn.sigmoid(values[:, :, 2]),
    )


def shift_down(values):
    return jnp.concatenate([jnp.zeros_like(values[:, :1]), values[:, :-1]], axis=1)


def shift_up(values):
    return jnp.concatenate([values[:, 1:], jnp.zeros_like(values[:, :1])], axis=1)


def forward_layer(layer_in, weight, fbias):
    gathered = lax.all_gather(layer_in, "tm", axis=1, tiled=True)
    seq_count, length, width = gathered.shape
    hidden = weight.shape[2]
    flat_now = weight[0].reshape(3 * hidden, width)
    flat_past = weight[1].reshape(3 * hidden, width)
    preact = jnp.einsum("btd,kd->btk", gathered, flat_now, preferred_element_type=jnp.float32)
    preact = preact + jnp.einsum(
        "btd,kd->btk", shift_down(gathered), flat_past, preferred_element_type=jnp.float32
    )
    zero_row = jnp.zeros_like(fbias)
    preact = preact + jnp.concatenate([zero_row, fbias, zero_row])
    preact = preact.astype(jnp.bfloat16).reshape(seq_count, length, 3, hidden)
    local_pre = lax.all_to_all(preact, "tm", split_axis=1, concat_axis=3, tiled=True)
    candidate, forget, outgate = activate(local_pre)
    products, cell_state = lax.associative_scan(
        affine_chain, (forget, (1.0 - forget) * candidate), axis=1
    )
    carry_in = entering(
        (products[:, -1], cell_state[:, -1]),
        "tm",
        affine_chain,
        (jnp.ones_like(products[:, -1]), jnp.zeros_like(cell_state[:, -1])),
        False,
    )[1]
    cell_state = cell_state + products * carry_in[:, None]
    layer_out = (outgate * cell_state).astype(jnp.bfloat16)
    kept = (gathered, local_pre, cell_state, carry_in)
    return (layer_out, kept)


def pool_backward(grad_hidden, preact, cell_state, carry_in):
    candidate, forget, outgate = activate(preact)
    before = jnp.concatenate([carry_in[:, None], cell_state[:, :-1]], axis=1)
    factor = jnp.concatenate([forget[:, 1:], jnp.ones_like(forget[:, :1])], axis=1)
    products, partial_value = lax.associative_scan(
        affine_chain, (factor, grad_hidden * outgate), reverse=True, axis=1
    )
    incoming = entering(
        (forget[:, 0] * products[:, 0], forget[:, 0] * partial_value[:, 0]),
        "tm",
        affine_chain,
        (jnp.ones_like(partial_value[:, 0]), jnp.zeros_like(partial_value[:, 0])),
        True,
    )[1]
    partial_value = partial_value + products * incoming[:, None]
    grad_cand = partial_value * (1.0 - forget) * (1.0 - candidate * candidate)
    grad_forget = partial_value * (before - candidate) * forget * (1.0 - forget)
    grad_outgate = grad_hidden * cell_state * outgate * (1.0 - outgate)
    return jnp.stack([grad_cand, grad_forget, grad_outgate], axis=2).astype(jnp.bfloat16)


def backward_layer(grad_out, weight, kept):
    gathered, preact, cell_state, carry_in = kept
    local_grad = pool_backward(grad_out.astype(jnp.float32), preact, cell_state, carry_in)
    grad_rows = lax.all_to_all(local_grad, "tm", split_axis=3, concat_axis=1, tiled=True)
    seq_count, length, width = gathered.shape
    hidden = weight.shape[2]
    flat_grad = grad_rows.reshape(seq_count, length, 3 * hidden)
    grad_now = jnp.einsum("btk,btd->kd", flat_grad, gathered, preferred_element_type=jnp.float32)
    grad_past = jnp.einsum(
        "btk,btd->kd", flat_grad, shift_down(gathered), preferred_element_type=jnp.float32
    )
    grad_weight = jnp.stack([grad_now, grad_past]).reshape(2, 3, hidden, width)
    grad_bias = jnp.sum(grad_rows[:, :, 1, :].astype(jnp.float32), axis=(0, 1))
    flat_now = weight[0].reshape(3 * hidden, width)
    flat_past = weight[1].reshape(3 * hidden, width)
    part_grad = jnp.einsum("btk,kd->btd", flat_grad, flat_now, preferred_element_type=jnp.float32)
    part_grad = part_grad + shift_up(
        jnp.einsum("btk,kd->btd", flat_grad, flat_past, preferred_element_type=jnp.float32)
    )
    grad_in = lax.psum_scatter(part_grad, "tm", scatter_dimension=1, tiled=True)
    return (grad_in, grad_weight, grad_bias)


def per_device(inputs, weight_one, fbias_one, weight_two, fbias_two, cotangent, cluster_starts):
    layer_first, kept_first = forward_layer(inputs, weight_one, fbias_one)
    layer_second, kept_second = forward_layer(layer_first, weight_two, fbias_two)
    span_len = inputs.shape[1]
    steps_here = lax.axis_index("tm") * span_len + jnp.arange(span_len, dtype=jnp.int32)
    inside = (steps_here[None, None, :] >= cluster_starts[:, :, None]) & (
        steps_here[None, None, :] < cluster_starts[:, :, None] + CLUSTER
    )
    keep_mask = jnp.any(inside, axis=1)
    grad_seed = jnp.where(keep_mask[:, :, None], cotangent, jnp.zeros_like(cotangent))
    back_second, gweight_second, gbias_second = backward_layer(grad_seed, weight_two, kept_second)
    back_first, gweight_first, gbias_first = backward_layer(
        back_second.astype(jnp.bfloat16), weight_one, kept_first
    )
    summed = lax.psum((gweight_first, gbias_first, gweight_second, gbias_second), "seq")
    return (
        layer_second,
        back_first.astype(jnp.bfloat16),
        summed[0],
        summed[1],
        summed[2],
        summed[3],
    )


def solution(mesh):
    placed = (
        P("seq", "tm", None),
        P(None, None, "tm", None),
        P("tm"),
        P(None, None, "tm", None),
        P("tm"),
        P("seq", "tm", None),
        P("seq", None),
    )
    return jax.shard_map(
        per_device,
        mesh=mesh,
        in_specs=placed,
        out_specs=(
            P("seq", "tm", None),
            P("seq", "tm", None),
            P(None, None, "tm", None),
            P("tm"),
            P(None, None, "tm", None),
            P("tm"),
        ),
        check_vma=False,
    )
```

profile of v0, /device:TPU:0, one launch (start us, length us, event | category | flops | bytes accessed | tf_op | source)
XLA Modules:
  0.0 2914.4 jit_solution(7773878995228876392)
XLA Ops:
  14.3 57.1 %all-gather.11.cloned.1.call-done = bf16[2,1024,2304]{2,1,0:T(8,128)(2,1)} async-done(((bf16[2,128,2304]{2,1,0:T(8,128)(2,1)}), bf16[2,1024,2304]{2,1,0:T(8,128)(2,1)}) %all-gather.11.cloned.1.call-update) | async-done | bytes 9437200 | tf_op jit(solution)/shard_map/all_gather | solution.py:48
  71.5 14.1 fusion.128
  85.6 10.7 add_convert_fusion.1
  109.5 54.5 %all-to-all-done = bf16[2,1024,3,288]{3,0,2,1:T(2,128)(2,1)} async-done(((bf16[2,1024,3,288]{3,0,2,1:T(2,128)(2,1)}), bf16[2,1024,3,288]{3,0,2,1:T(2,128)(2,1)}, u32[]{:S(2)}, u32[]{:S(2)}) %all-to-all-start) | async-done | bytes 3538976 | tf_op jit(solution)/shard_map/all_to_all | solution.py:60
  163.9 10.7 copy.112
  413.6 53.4 %all-gather.13.cloned.1.call-done = bf16[2,1024,2304]{2,1,0:T(8,128)(2,1)} async-done(((bf16[2,128,2304]{2,1,0:T(8,128)(2,1)}), bf16[2,1024,2304]{2,1,0:T(8,128)(2,1)}) %all-gather.13.cloned.1.call-update) | async-done | bytes 9437200 | tf_op jit(solution)/shard_map/all_gather | solution.py:48
  467.0 14.1 fusion.129
  481.1 10.7 add_convert_fusion
  505.1 54.5 %all-to-all-done.1 = bf16[2,1024,3,288]{3,0,2,1:T(2,128)(2,1)} async-done(((bf16[2,1024,3,288]{3,0,2,1:T(2,128)(2,1)}), bf16[2,1024,3,288]{3,0,2,1:T(2,128)(2,1)}, u32[]{:S(2)}, u32[]{:S(2)}) %all-to-all-start.1) | async-done | bytes 3538976 | tf_op jit(solution)/shard_map/all_to_all | solution.py:60
  559.6 10.7 copy.118
  810.5 10.2 all-gather.3
  824.2 10.1 while.57
  1062.2 18.6 rev.28
  1080.8 18.8 rev.29
  1130.7 45.8 %all_to_all.54 = bf16[2,128,3,2304]{1,0,2,3:T(2,128)(2,1)S(1)} all-to-all(bf16[2,128,3,2304]{1,0,2,3:T(2,128)(2,1)} %copy.123), channel_id=1, replica_groups=mesh['seq'=4,'tm'=8] {'tm'}, dimensions={3} | all-to-all | bytes 7077888 | tf_op jit(solution)/shard_map/all_to_all | solution.py:102
  1183.6 17.2 fusion.32
  1200.8 19.0 pad_add_fusion.1
  1240.4 9.9 slice.1161
  1266.1 79.1 %reduce-scatter.3.cloned.1.call-done = f32[2,128,2304]{2,1,0:T(8,128)} async-done(((f32[2,1024,2304]{2,1,0:T(8,128)}), f32[2,128,2304]{2,1,0:T(8,128)}) %reduce-scatter.3.cloned.1.call-update) | async-done | bytes 2359312 | tf_op jit(solution)/shard_map/reduce_scatter | solution.py:118
  1543.2 18.8 rev.32
  1562.0 18.9 rev.33
  1612.4 45.8 %all_to_all.55 = bf16[2,128,3,2304]{1,0,2,3:T(2,128)(2,1)S(1)} all-to-all(bf16[2,128,3,2304]{1,0,2,3:T(2,128)(2,1)} %copy.126), channel_id=1, replica_groups=mesh['seq'=4,'tm'=8] {'tm'}, dimensions={3} | all-to-all | bytes 7077888 | tf_op jit(solution)/shard_map/all_to_all | solution.py:102
  1668.5 17.2 fusion.30
  1685.6 20.0 pad_add_fusion
  1706.0 13.2 fusion.21
  1719.2 12.9 fusion.27
  1738.4 12.0 fusion.18
  1750.4 12.2 fusion.24
  1775.4 12.4 all-reduce.120
  1787.8 43.2 %reduce-scatter.5.cloned.1.call-done = f32[2,128,2304]{2,1,0:T(8,128)} async-done(((f32[2,1024,2304]{2,1,0:T(8,128)}), f32[2,128,2304]{2,1,0:T(8,128)}) %reduce-scatter.5.cloned.1.call-update) | async-done | bytes 2359312 | tf_op jit(solution)/shard_map/reduce_scatter | solution.py:118
  1833.8 1051.8 %all-reduce.124.cloned.1.call-done = (f32[2,3,288,2304]{3,2,1,0:T(8,128)}, f32[2,3,288,2304]{3,2,1,0:T(8,128)}) async-done(((f32[2,3,288,2304]{3,2,1,0:T(8,128)}, f32[2,3,288,2304]{3,2,1,0:T(8,128)}), (f32[2,3,288,2304]{3,2,1,0:T(8,128)}, f32[2,3,288,2304]{3,2,1,0:T(8,128)})) %all-reduce.124.cloned.1.call-update) | async-done | bytes 31850512 | tf_op jit(solution)/shard_map/psum | solution.py:136
  2885.7 12.0 copy.183
  (810 shorter events, 1103.8 us)
Async XLA Ops:
  7.2 64.3 %all-gather.11.cloned.1.call-start = ((), (), s32[]{:S(2)}) async-start(), calls=%async_computation.6 | async-start | bytes 10616832 | tf_op jit(solution)/shard_map/all_gather | solution.py:48
  71.5 14.1 copy-start.50
  71.5 14.1 copy-start.119
  104.6 59.4 %all-to-all-start = ((bf16[2,1024,3,288]{3,0,2,1:T(2,128)(2,1)}), bf16[2,1024,3,288]{3,0,2,1:T(2,128)(2,1)}, u32[]{:S(2)}, u32[]{:S(2)}) async-start(bf16[2,1024,3,288]{3,0,2,1:T(2,128)(2,1)} %copy.111), calls=%async_computation | async-start | bytes 9437184 | tf_op jit(solution)/shard_map/all_to_all | solution.py:60
  109.2 357.8 %all-gather.13.cloned.1.call-start = ((), (), s32[]{:S(2)}) async-start(), calls=%async_computation.7 | async-start | bytes 10616832 | tf_op jit(solution)/shard_map/all_gather | solution.py:48
  190.9 11.1 copy-start.4
  297.9 103.8 %copy-start.7 = (f32[2,128,1,2304]{3,1,0,2:T(8,128)}, f32[2,128,1,2304]{3,1,0,2:T(8,128)S(1)}, u32[]{:S(2)}) copy-start(f32[2,128,1,2304]{3,1,0,2:T(8,128)S(1)} %copy.143) | copy-start | bytes 7077892
  358.3 19.6 copy-start.41
  379.7 16.5 copy-start.62
  467.0 14.1 copy-start.52
  467.0 14.1 copy-start.120
  500.1 59.5 %all-to-all-start.1 = ((bf16[2,1024,3,288]{3,0,2,1:T(2,128)(2,1)}), bf16[2,1024,3,288]{3,0,2,1:T(2,128)(2,1)}, u32[]{:S(2)}, u32[]{:S(2)}) async-start(bf16[2,1024,3,288]{3,0,2,1:T(2,128)(2,1)} %copy.117), calls=%async_computation.1 | async-start | bytes 9437184 | tf_op jit(solution)/shard_map/all_to_all | solution.py:60
  504.9 840.2 %reduce-scatter.3.cloned.1.call-start = ((), (), s32[]{:S(2)}) async-start(), calls=%async_computation.8 | async-start | bytes 21233664 | tf_op jit(solution)/shard_map/reduce_scatter | solution.py:118
  782.5 19.6 copy-start.42
  803.9 30.4 %copy-start.60 = (bf16[2,128,2304]{2,1,0:T(8,128)(2,1)S(1)}, bf16[2,128,2304]{2,1,0:T(8,128)(2,1)}, u32[]{:S(2)}) copy-start(bf16[2,128,2304]{2,1,0:T(8,128)(2,1)} %param.20) | copy-start | bytes 3538948
  848.0 15.4 copy-start.45
  869.2 9.9 copy-start.48
  1080.8 37.2 %copy-start.64 = (f32[2,2304]{1,0:T(2,128)S(1)}, f32[2,2304]{1,0:T(2,128)}, u32[]{:S(2)}) copy-start(f32[2,2304]{1,0:T(2,128)} %custom-call.2) | copy-start | bytes 55300
  1183.6 17.2 copy-start.51
  1183.6 17.2 copy-start.53
  1219.8 611.3 %reduce-scatter.5.cloned.1.call-start = ((), (), s32[]{:S(2)}) async-start(), calls=%async_computation.9 | async-start | bytes 21233664 | tf_op jit(solution)/shard_map/reduce_scatter | solution.py:118
  1452.3 9.2 copy-start.72
  1452.3 9.2 copy-start.75
  1452.3 9.3 copy-start.109
  1452.3 9.6 copy-start.107
  1562.0 37.5 %copy-start.65 = (f32[2,2304]{1,0:T(2,128)S(1)}, f32[2,2304]{1,0:T(2,128)}, u32[]{:S(2)}) copy-start(f32[2,2304]{1,0:T(2,128)} %custom-call.3) | copy-start | bytes 55300
  1562.0 37.9 %copy-start.1 = (f32[2,128,1,2304]{3,1,0,2:T(8,128)S(1)}, f32[2,128,1,2304]{3,1,0,2:T(8,128)}, u32[]{:S(2)}) copy-start(f32[2,128,1,2304]{3,1,0,2:T(8,128)} %copy-done) | copy-start | bytes 7077892
  1580.9 19.0 copy-start.84
  1668.5 17.2 copy-start.49
  1705.7 1180.0 %all-reduce.124.cloned.1.call-start = ((), (), s32[]{:S(2)}) async-start(), calls=%async_computation.10 | async-start | bytes 63700992 | tf_op jit(solution)/shard_map/psum | solution.py:136
  1705.9 13.2 copy-start.54
  2885.7 15.9 copy-start.9
  (96 other events, 339.7 us)
Sparse Core Ops, SparseCore 0:
  9.9 61.5 all-gather.10
  408.1 58.8 all-gather.12
  1219.9 125.1 reduce-scatter.2
  1705.8 125.1 reduce-scatter.4
  1834.1 1051.5 all-reduce.123
where the time goes:
time: 2940 us; the launch traced here: 2910 us
  waiting for transfers between devices  1390 us (47%)
  local copies, waits for them, and re-layouts  869 us (30%)
  other arithmetic  273 us (9%)
  blocking collectives  177 us (6%)
  matrix products  173 us (6%)
    psum x1, waiting for transfers between devices, per_device(): lax.psum((gweight_first, gbias_first, gweight_second, gbias_second), 'seq')  1050 us
    slice x98, local copies, waits for them, and re-layouts, pool_backward(): lax.associative_scan(affine_chain, (factor, grad_hidden * outgate), rever...  289 us
    slice x88, local copies, waits for them, and re-layouts, forward_layer(): lax.associative_scan(affine_chain, (forget, (1.0 - forget) * candidate),...  187 us
    reduce_scatter x2, waiting for transfers between devices, backward_layer(): grad_in = lax.psum_scatter(part_grad, 'tm', scatter_dimension=1, tiled=True)  122 us
    all_gather x2, waiting for transfers between devices, forward_layer(): gathered = lax.all_gather(layer_in, 'tm', axis=1, tiled=True)  111 us
    all_to_all x2, waiting for transfers between devices, forward_layer(): lax.all_to_all(preact, 'tm', split_axis=1, concat_axis=3, tiled=True)  109 us
    all_to_all x2, blocking collectives, backward_layer(): lax.all_to_all(local_grad, 'tm', split_axis=3, concat_axis=1, tiled=True)  91.6 us
    pad x48, local copies, waits for them, and re-layouts, forward_layer(): lax.associative_scan(affine_chain, (forget, (1.0 - forget) * candidate),...  89.2 us
  transfers between devices with their start and end apart: 7, of which 7 were waited for; matrix products, arithmetic and copies ran while one was open for 4% of the time, Pallas kernels for 0%

commit v1 on v0

v1 whole, which is shorter than its diff:
```python
import functools

import jax
import jax.numpy as jnp
from jax import lax
from jax.experimental import pallas as pl
from jax.experimental.pallas import tpu as pltpu
from jax.sharding import PartitionSpec as P

CLUSTER = 32
LANES = 128
ROWS = 16
F32 = jnp.float32
BF16 = jnp.bfloat16


def sigmoid(v):
    return 0.5 * jnp.tanh(0.5 * v) + 0.5


def shift_lanes(v, amount, lane, fill):
    moved = pltpu.roll(v, amount % LANES, axis=1)
    gone = lane < amount if amount > 0 else lane >= LANES + amount
    return jnp.where(gone, fill, moved)


def lane_chain(factor, value, lane, sign):
    step = 1
    while step < LANES:
        value = value + factor * shift_lanes(value, sign * step, lane, 0.0)
        factor = factor * shift_lanes(factor, sign * step, lane, 1.0)
        step *= 2
    return value


def pool_forward(seq, p_ref, b_ref, pre_ref, cell_ref, h_ref, hidden, groups):
    lane = lax.broadcasted_iota(jnp.int32, (ROWS, LANES), 1)

    def tile(r, carry):
        rows = pl.ds(pl.multiple_of(r * ROWS, ROWS), ROWS)
        bias = b_ref[rows, :]

        def gate(g, j):
            cols = pl.ds(j * LANES, LANES)
            now = p_ref[g, rows, cols]
            if j:
                past = p_ref[3 + g, rows, pl.ds((j - 1) * LANES, LANES)]
            else:
                past = shift_lanes(p_ref[3 + g, rows, pl.ds((groups - 1) * LANES, LANES)], 1, lane, 0.0)
            total = now + past
            if g == 1:
                total = total + bias
            total = total.astype(BF16)
            pre_ref[seq, g, rows, cols] = total
            return total.astype(F32)

        factors, values = [], []
        for j in range(groups):
            candidate = jnp.tanh(gate(0, j))
            forget = sigmoid(gate(1, j))
            fresh = (1.0 - forget) * candidate
            if j:
                values.append(forget * values[-1] + fresh)
                factors.append(forget * factors[-1])
            else:
                values.append(fresh)
                factors.append(forget)
        entering = shift_lanes(lane_chain(factors[-1], values[-1], lane, 1), 1, lane, 0.0)
        for j in range(groups):
            cols = pl.ds(j * LANES, LANES)
            cell = values[j] + factors[j] * entering
            cell_ref[seq, rows, cols] = cell
            h_ref[seq, rows, cols] = (sigmoid(gate(2, j)) * cell).astype(BF16)
        return carry

    lax.fori_loop(0, hidden // ROWS, tile, 0)


def pool_backward(seq, g_ref, pre_ref, cell_ref, d_ref, db_ref, hidden, groups):
    lane = lax.broadcasted_iota(jnp.int32, (ROWS, LANES), 1)

    def tile(r, carry):
        rows = pl.ds(pl.multiple_of(r * ROWS, ROWS), ROWS)

        def at(j):
            return pl.ds(j * LANES, LANES)

        def put(g, j, v):
            v = v.astype(BF16)
            d_ref[seq, g, rows, at(j)] = v
            if j:
                d_ref[seq, 3 + g, rows, at(j - 1)] = v
            else:
                d_ref[seq, 3 + g, rows, at(groups - 1)] = shift_lanes(v.astype(F32), -1, lane, 0.0).astype(BF16)
            return v

        factors, values = [None] * groups, [None] * groups
        later = None
        for j in reversed(range(groups)):
            grad = g_ref[seq, rows, at(j)].astype(F32)
            own = grad * sigmoid(pre_ref[seq, 2, rows, at(j)].astype(F32))
            if later is None:
                values[j] = own
                factors[j] = jnp.ones_like(own)
            else:
                values[j] = own + later * values[j + 1]
                factors[j] = later * factors[j + 1]
            later = sigmoid(pre_ref[seq, 1, rows, at(j)].astype(F32))
        chain = lane_chain(later * factors[0], later * values[0], lane, -1)
        entering = shift_lanes(chain, -1, lane, 0.0)
        total = jnp.zeros((ROWS, LANES), F32)
        for j in range(groups):
            grad = g_ref[seq, rows, at(j)].astype(F32)
            carried = values[j] + factors[j] * entering
            candidate = jnp.tanh(pre_ref[seq, 0, rows, at(j)].astype(F32))
            forget = sigmoid(pre_ref[seq, 1, rows, at(j)].astype(F32))
            outgate = sigmoid(pre_ref[seq, 2, rows, at(j)].astype(F32))
            cell = cell_ref[seq, rows, at(j)]
            if j:
                before = cell_ref[seq, rows, at(j - 1)]
            else:
                before = shift_lanes(cell_ref[seq, rows, at(groups - 1)], 1, lane, 0.0)
            put(0, j, carried * (1.0 - forget) * (1.0 - candidate * candidate))
            total = total + put(1, j, carried * (before - candidate) * forget * (1.0 - forget)).astype(F32)
            put(2, j, grad * cell * outgate * (1.0 - outgate))
        db_ref[seq, rows, :] = jnp.sum(total, axis=1, keepdims=True)
        return carry

    lax.fori_loop(0, hidden // ROWS, tile, 0)


def products(w_ref, x_ref, p_ref, hidden, length, token_major):
    wide = 256

    def strip(c, carry):
        cols = pl.ds(pl.multiple_of(c * wide, wide), wide)
        if token_major:
            rhs, dims = x_ref[0, cols, :], (((1,), (1,)), ((), ()))
        else:
            rhs, dims = x_ref[0, :, cols], (((1,), (0,)), ((), ()))
        for k in range(6):
            p_ref[k, :, cols] = lax.dot_general(w_ref[k], rhs, dims, preferred_element_type=F32)
        return carry

    lax.fori_loop(0, length // wide, strip, 0)


def first_kernel(hidden, length, w_ref, b_ref, x_ref, pre_ref, cell_ref, h_ref, p_ref):
    products(w_ref, x_ref, p_ref, hidden, length, True)
    pool_forward(0, p_ref, b_ref, pre_ref, cell_ref, h_ref, hidden, length // LANES)


def second_kernel(hidden, length, w_ref, b_ref, x_ref, g_ref, h_ref, d_ref, db_ref, p_ref, pre_ref, cell_ref):
    products(w_ref, x_ref, p_ref, hidden, length, False)
    groups = length // LANES
    pool_forward(0, p_ref, b_ref, pre_ref, cell_ref, h_ref, hidden, groups)
    pool_backward(0, g_ref, pre_ref, cell_ref, d_ref, db_ref, hidden, groups)


def back_kernel(hidden, length, g_ref, pre_ref, cell_ref, d_ref, db_ref):
    pool_backward(0, g_ref, pre_ref, cell_ref, d_ref, db_ref, hidden, length // LANES)


def per_seq(*dims):
    return pl.BlockSpec((1,) + dims, lambda s: (s,) + (0,) * len(dims))


def whole(*dims):
    return pl.BlockSpec(dims, lambda s: (0,) * len(dims), pipeline_mode=pl.Buffered(1))


PARAMS = pltpu.CompilerParams(vmem_limit_bytes=62 * 1024 * 1024, dimension_semantics=("arbitrary",))


def run_first(weight, bias, gathered):
    seqs, length, width = gathered.shape
    hidden = weight.shape[1]
    shape = jax.ShapeDtypeStruct
    return pl.pallas_call(
        functools.partial(first_kernel, hidden, length),
        name="layer_one_forward",
        grid=(seqs,),
        in_specs=[whole(6, hidden, width), whole(hidden, 1), per_seq(length, width)],
        out_specs=[per_seq(3, hidden, length), per_seq(hidden, length), per_seq(hidden, length)],
        out_shape=[
            shape((seqs, 3, hidden, length), BF16),
            shape((seqs, hidden, length), F32),
            shape((seqs, hidden, length), BF16),
        ],
        scratch_shapes=[pltpu.VMEM((6, hidden, length), F32)],
        compiler_params=PARAMS,
    )(weight, bias, gathered)


def run_second(weight, bias, gathered, grad):
    seqs, width, length = gathered.shape
    hidden = weight.shape[1]
    shape = jax.ShapeDtypeStruct
    return pl.pallas_call(
        functools.partial(second_kernel, hidden, length),
        name="layer_two_forward_and_pool_backward",
        grid=(seqs,),
        in_specs=[whole(6, hidden, width), whole(hidden, 1), per_seq(width, length), per_seq(hidden, length)],
        out_specs=[per_seq(hidden, length), per_seq(6, hidden, length), per_seq(hidden, 1)],
        out_shape=[
            shape((seqs, hidden, length), BF16),
            shape((seqs, 6, hidden, length), BF16),
            shape((seqs, hidden, 1), F32),
        ],
        scratch_shapes=[
            pltpu.VMEM((6, hidden, length), F32),
            pltpu.VMEM((1, 3, hidden, length), BF16),
            pltpu.VMEM((1, hidden, length), F32),
        ],
        compiler_params=PARAMS,
    )(weight, bias, gathered, grad)


def run_back(grad, pre, cell):
    seqs, hidden, length = grad.shape
    shape = jax.ShapeDtypeStruct
    return pl.pallas_call(
        functools.partial(back_kernel, hidden, length),
        name="layer_one_pool_backward",
        grid=(seqs,),
        in_specs=[per_seq(hidden, length), per_seq(3, hidden, length), per_seq(hidden, length)],
        out_specs=[per_seq(6, hidden, length), per_seq(hidden, 1)],
        out_shape=[shape((seqs, 6, hidden, length), BF16), shape((seqs, hidden, 1), F32)],
        compiler_params=PARAMS,
    )(grad, pre, cell)


def per_device(inputs, weight_one, fbias_one, weight_two, fbias_two, cotangent, cluster_starts):
    seqs, span, width = inputs.shape
    count = lax.axis_size("tm")
    length = span * count
    groups = length // LANES
    part = LANES // count
    hidden = weight_one.shape[2]
    w1 = weight_one.reshape(6, hidden, width)
    w2 = weight_two.reshape(6, hidden, width)

    def to_columns(v):
        return v.reshape(seqs, part, groups, width).transpose(0, 2, 1, 3)

    steps = lax.axis_index("tm") * span + jnp.arange(span, dtype=jnp.int32)
    starts = cluster_starts[:, :, None]
    keep = jnp.any((steps >= starts) & (steps < starts + CLUSTER), axis=1)
    seed = jnp.where(keep[:, :, None], cotangent, jnp.zeros_like(cotangent))
    seed = seed.reshape(seqs, part, groups, count, hidden)
    seed = lax.all_to_all(seed, "tm", split_axis=3, concat_axis=1, tiled=True)
    seed = seed.reshape(seqs, LANES, groups, hidden).transpose(0, 3, 2, 1).reshape(seqs, hidden, length)

    x = lax.all_gather(to_columns(inputs), "tm", axis=2, tiled=True).reshape(seqs, length, width)
    pre1, cell1, h1 = run_first(w1, fbias_one[:, None], x)
    h1 = lax.all_gather(h1, "tm", axis=1, tiled=True)
    h2, d2, db2 = run_second(w2, fbias_two[:, None], h1, seed)

    out = h2.reshape(seqs, hidden, groups, count, part)
    out = lax.all_to_all(out, "tm", split_axis=3, concat_axis=1, tiled=True)
    out = out.reshape(seqs, width, groups, part).transpose(0, 3, 2, 1).reshape(seqs, span, width)

    d2 = d2.reshape(seqs, 6 * hidden, length)
    flat2 = w2.reshape(6 * hidden, width)
    gw2 = jnp.einsum("skt,sdt->kd", d2, h1, preferred_element_type=F32).astype(BF16)
    gw2 = lax.psum(gw2, "seq")
    gx2 = jnp.einsum("kd,skt->sdt", flat2, d2, preferred_element_type=F32).astype(BF16)
    gx2 = lax.psum_scatter(gx2, "tm", scatter_dimension=1, tiled=True)

    d1, db1 = run_back(gx2, pre1, cell1)
    d1 = d1.reshape(seqs, 6 * hidden, length)
    flat1 = w1.reshape(6 * hidden, width)
    gw1 = jnp.einsum("skt,std->kd", d1, x, preferred_element_type=F32).astype(BF16)
    gw1 = lax.psum(gw1, "seq")
    gx1 = jnp.einsum("kd,skt->std", flat1, d1, preferred_element_type=F32).astype(BF16)
    gx1 = gx1.reshape(seqs, groups, LANES, width)
    gx1 = lax.psum_scatter(gx1, "tm", scatter_dimension=2, tiled=True)
    gx1 = gx1.transpose(0, 2, 1, 3).reshape(seqs, span, width)

    db = lax.psum(jnp.stack([db1, db2]).sum(axis=(1, 3)), "seq")
    shape = weight_one.shape
    return (out, gx1, gw1.astype(F32).reshape(shape), db[0], gw2.astype(F32).reshape(shape), db[1])


def solution(mesh):
    placed = (
        P("seq", "tm", None),
        P(None, None, "tm", None),
        P("tm"),
        P(None, None, "tm", None),
        P("tm"),
        P("seq", "tm", None),
        P("seq", None),
    )
    return jax.shard_map(
        per_device,
        mesh=mesh,
        in_specs=placed,
        out_specs=(
            P("seq", "tm", None),
            P("seq", "tm", None),
            P(None, None, "tm", None),
            P("tm"),
            P(None, None, "tm", None),
            P("tm"),
        ),
        check_vma=False,
    )
```

time: 2940 us -> 1070 us (0.36); the launches traced: 2910 us -> 1070 us
  local copies, waits for them, and re-layouts: 869 us -> 21.7 us
  waiting for transfers between devices: 1390 us -> 754 us
  other arithmetic: 273 us -> 19.9 us
  blocking collectives: 177 us -> 11.2 us
  Pallas kernels: 0 us -> 153 us
  matrix products: 173 us -> 92.6 us
    psum x1, waiting for transfers between devices: 1050 us -> 522 us  [per_device(): gw1 = lax.psum(gw1, 'seq')]
    slice x192 -> x1, local copies, waits for them, and re-layouts: 495 us -> 0.6 us  [per_device(): db[1]]
    pad x96 -> x0, local copies, waits for them, and re-layouts: 167 us -> none  [the longest x48 89.2 us: forward_layer(): lax.associative_scan(affine_chain, (forget, (1.0 - forget) * candidate),...]
    pallas_call x0 -> x3, Pallas kernels: none -> 153 us  [the longest x1 74.8 us: run_second(): pl.pallas_call(functools.partial(second_kernel, hidden, length), name='la...]
    add x79 -> x2, other arithmetic: 104 us -> 0.01 us  [the longest x1 0.01 us: per_device(): keep = jnp.any((steps >= starts) & (steps < starts + CLUSTER), axis=1)]
    all_to_all x2 -> x0, blocking collectives: 91.6 us -> none  [backward_layer(): lax.all_to_all(local_grad, 'tm', split_axis=3, concat_axis=1, tiled=True)]
    dot_general x12 -> x4, matrix products: 173 us -> 92.6 us  [the longest x1 23.3 us: per_device(): jnp.einsum('skt,std->kd', d1, x, preferred_element_type=F32).astype(BF16)]
    rev x8 -> x0, local copies, waits for them, and re-layouts: 75.1 us -> none  [the longest x4 75.1 us: pool_backward(): lax.associative_scan(affine_chain, (factor, grad_hidden * outgate), rever...]
  transfers between devices with their start and end apart: 7 -> 7, of which waited for: 7 -> 6; matrix products, arithmetic and copies ran while one was open for 4% -> 6% of each run, Pallas kernels for 0% -> 0%
where the time goes in v1:
time: 1070 us
  waiting for transfers between devices  754 us (70%)
  Pallas kernels  153 us (14%)
  matrix products  92.6 us (9%)
  local copies, waits for them, and re-layouts  21.7 us (2%)
  other arithmetic  19.9 us (2%)
  between operations  13.9 us (1%)
  blocking collectives  11.2 us (1%)
    psum x1, waiting for transfers between devices, per_device(): gw1 = lax.psum(gw1, 'seq')  522 us
    reduce_scatter x1, waiting for transfers between devices, per_device(): gx2 = lax.psum_scatter(gx2, 'tm', scatter_dimension=1, tiled=True)  76.4 us
    pallas_call x1, Pallas kernels, run_second(): pl.pallas_call(functools.partial(second_kernel, hidden, length), name='la...  74.8 us
    all_gather x1, waiting for transfers between devices, per_device(): lax.all_gather(to_columns(inputs), 'tm', axis=2, tiled=True)  60.8 us
    pallas_call x1, Pallas kernels, run_first(): pl.pallas_call(functools.partial(first_kernel, hidden, length), name='lay...  48.9 us
    all_to_all x1, waiting for transfers between devices, per_device(): out = lax.all_to_all(out, 'tm', split_axis=3, concat_axis=1, tiled=True)  31.9 us
    all_gather x1, waiting for transfers between devices, per_device(): h1 = lax.all_gather(h1, 'tm', axis=1, tiled=True)  31.7 us
    all_to_all x1, waiting for transfers between devices, per_device(): seed = lax.all_to_all(seed, 'tm', split_axis=3, concat_axis=1, tiled=True)  31.3 us
  transfers between devices with their start and end apart: 7, of which 6 were waited for; matrix products, arithmetic and copies ran while one was open for 6% of the time, Pallas kernels for 0%

profile of v1, /device:TPU:0, one launch (start us, length us, event | category | flops | bytes accessed | tf_op | source)
XLA Modules:
  0.0 1074.5 jit_solution(9070547174080304193)
XLA Ops:
  7.2 2.5 copy.77
  9.8 1.4 broadcast_in_dim.26.b_ref
  11.2 60.8 %all-gather.3.cloned.1.call-done = bf16[2,8,128,2304]{3,2,1,0:T(8,128)(2,1)} async-done(((bf16[2,8,16,2304]{3,2,1,0:T(8,128)(2,1)}), bf16[2,8,128,2304]{3,2,1,0:T(8,128)(2,1)}) %all-gather.3.cloned.1.call-update) | async-done | bytes 9437200 | tf_op jit(solution)/shard_map/all_gather | solution.py:254
  72.0 48.9 %layer_one_forward.1 = (bf16[2,3,288,1024]{3,2,1,0:T(8,128)(2,1)}, f32[2,288,1024]{2,1,0:T(8,128)}, bf16[2,288,1024]{2,1,0:T(8,128)(2,1)}) custom-call(bf16[6,288,2304]{2,1,0:T(8,128)(2,1)} %bitcast.63, f32[288,1]{1,0:T(8,128)} %broadcast_in_dim.26.b_ref, bf16[2,1024,2304]{2,1,0:T(8,128)(2,1)} %bitcast.58), custom_call_target="tpu_custom_call" | custom-call | tf_op jit(solution)/shard_map/layer_one_forward/pallas_call | solution.py:179
  121.1 1.4 broadcast_select_fusion
  122.5 2.5 reshape.80
  125.0 1.4 copy.61
  126.4 3.6 all-to-all-start
  130.8 31.3 %all-to-all-done = bf16[2,16,8,8,288]{4,2,1,0,3:T(8,128)(2,1)S(1)} async-done(((bf16[2,16,8,8,288]{4,2,1,0,3:T(8,128)(2,1)}), bf16[2,16,8,8,288]{4,2,1,0,3:T(8,128)(2,1)S(1)}, u32[]{:S(2)}, u32[]{:S(2)}) %all-to-all-start) | async-done | bytes 1179680 | tf_op jit(solution)/shard_map/all_to_all | solution.py:251
  162.4 1.4 copy.63
  163.8 1.4 reshape.82.g_ref
  165.1 31.7 %all-gather.5.cloned.1.call-done.x_ref = bf16[2,2304,1024]{2,1,0:T(8,128)(2,1)} async-done(((bf16[2,288,1024]{2,1,0:T(8,128)(2,1)}), bf16[2,2304,1024]{2,1,0:T(8,128)(2,1)}) %all-gather.5.cloned.1.call-update) | async-done | bytes 9437200 | tf_op jit(solution)/shard_map/all_gather | solution.py:256
  196.8 74.8 %layer_two_forward_and_pool_backward.1 = (bf16[2,288,1024]{2,1,0:T(8,128)(2,1)}, bf16[2,6,288,1024]{3,2,1,0:T(8,128)(2,1)}, f32[2,288,1]{2,1,0:T(8,128)}) custom-call(bf16[6,288,2304]{2,1,0:T(8,128)(2,1)} %bitcast.61, f32[288,1]{1,0:T(8,128)} %broadcast_in_dim.25.b_ref, bf16[2,2304,1024]{2,1,0:T(8,128)(2,1)} %all-gather.5.cloned.1.call-done.x_ref, ...), custom_call_target="tpu_custom_call" | custom-call | tf_op jit(solution)/shard_map/layer_two_forward_and_pool_backward/pallas_call | solution.py:199
  271.6 23.2 %convert_bitcast_fusion = bf16[2,2304,1024]{2,1,0:T(8,128)(2,1)} fusion(bf16[2,1728,1024]{2,1,0:T(8,128)(2,1)} %bitcast.79, bf16[1728,2304,1]{1,0,2:T(8,128)(2,1)} %bitcast.62), kind=kOutput, calls=%fused_computation.2 | convolution fusion | flops 16312172544 | bytes 24477696 | tf_op jit(solution)/shard_map/kd,skt->sdt/dot_general | solution.py:267
  295.1 76.4 %reduce-scatter.3.cloned.1.call-done.g_ref = bf16[2,288,1024]{2,1,0:T(8,128)(2,1)} async-done(((bf16[2,2304,1024]{2,1,0:T(8,128)(2,1)}), bf16[2,288,1024]{2,1,0:T(8,128)(2,1)}) %reduce-scatter.3.cloned.1.call-update) | async-done | bytes 1179664 | tf_op jit(solution)/shard_map/reduce_scatter | solution.py:268
  371.5 29.6 %layer_one_pool_backward.1 = (bf16[2,6,288,1024]{3,2,1,0:T(8,128)(2,1)}, f32[2,288,1]{2,1,0:T(8,128)}) custom-call(bf16[2,288,1024]{2,1,0:T(8,128)(2,1)} %reduce-scatter.3.cloned.1.call-done.g_ref, bf16[2,3,288,1024]{3,2,1,0:T(8,128)(2,1)} %get-tuple-element.17.pre_ref, f32[2,288,1024]{2,1,0:T(8,128)} %get-tuple-element.18.cell_ref), custom_call_target="tpu_custom_call" | custom-call | tf_op jit(solution)/shard_map/layer_one_pool_backward/pallas_call | solution.py:222
  401.1 23.2 %convolution_convert_fusion = bf16[2,1024,2304]{2,1,0:T(8,128)(2,1)} fusion(bf16[2,1728,1024]{2,1,0:T(8,128)(2,1)} %bitcast.81, bf16[1728,2304,1]{1,0,2:T(8,128)(2,1)} %bitcast.64), kind=kOutput, calls=%fused_computation.3 | convolution fusion | flops 16312172544 | bytes 24477696 | tf_op jit(solution)/shard_map/kd,skt->std/dot_general | solution.py:275
  424.4 22.8 %bitcast_convert_fusion = bf16[1728,2304]{1,0:T(8,128)(2,1)} fusion(bf16[2,1728,1024]{2,1,0:T(8,128)(2,1)} %bitcast.80, bf16[2,2304,1024]{2,1,0:T(8,128)(2,1)} %all-gather.5.cloned.1.call-done.x_ref), kind=kOutput, calls=%fused_computation | convolution fusion | flops 16311435264 | bytes 24477696 | tf_op jit(solution)/shard_map/skt,sdt->kd/dot_general | solution.py:265
  447.3 23.3 %bitcast_convert_fusion.1 = bf16[1728,2304]{1,0:T(8,128)(2,1)} fusion(bf16[2,1728,1024]{2,1,0:T(8,128)(2,1)} %bitcast.82, bf16[2,1024,2304]{2,1,0:T(8,128)(2,1)} %bitcast.59), kind=kOutput, calls=%fused_computation.1 | convolution fusion | flops 16311435264 | bytes 24477696 | tf_op jit(solution)/shard_map/skt,std->kd/dot_general | solution.py:273
  470.6 1.2 copy-done.1
  471.8 0.8 copy.65
  472.7 1.4 copy.66
  474.1 3.8 all-to-all-start.1
  478.1 31.9 %all-to-all-done.1 = bf16[2,288,8,8,16]{1,4,2,0,3:T(8,128)(2,1)S(1)} async-done(((bf16[2,288,8,8,16]{1,4,2,0,3:T(8,128)(2,1)}), bf16[2,288,8,8,16]{1,4,2,0,3:T(8,128)(2,1)S(1)}, u32[]{:S(2)}, u32[]{:S(2)}) %all-to-all-start.1) | async-done | bytes 1179680 | tf_op jit(solution)/shard_map/all_to_all | solution.py:260
  509.9 0.9 copy.67
  510.8 1.2 reshape.84
  512.1 1.4 copy.76
  513.7 11.2 %psum.22 = f32[2,288]{1,0:T(2,128)S(1)} all-reduce(f32[2,288]{1,0:T(2,128)S(1)} %maximum_reduce_fusion), channel_id=1, replica_groups=mesh['seq'=4,'tm'=8] {'seq'}, use_global_device_ids=true, to_apply=%region_5.6 | all-reduce | flops 576 | bytes 4608 | tf_op jit(solution)/shard_map/psum | solution.py:280
  525.4 2.6 copy.75
  528.1 522.0 %all-reduce.3.cloned.1.call-done = (bf16[2,3,288,2304]{3,2,1,0:T(8,128)(2,1)}, bf16[2,3,288,2304]{3,2,1,0:T(8,128)(2,1)}) async-done(((bf16[2,3,288,2304]{3,2,1,0:T(8,128)(2,1)}, bf16[2,3,288,2304]{3,2,1,0:T(8,128)(2,1)}), (bf16[2,3,288,2304]{3,2,1,0:T(8,128)(2,1)}, bf16[2,3,288,2304]{3,2,1,0:T(8,128)(2,1)})) %all-reduce.3.cloned.1.call-update) | async-done | bytes 15925264 | tf_op jit(solution)/shard_map/psum | solution.py:274
  1050.0 10.7 reshape.91
  1060.7 7.3 reshape.93
  (31 shorter events, 2.5 us)
Async XLA Ops:
  7.2 64.9 %all-gather.3.cloned.1.call-start = ((), (), s32[]{:S(2)}) async-start(), calls=%async_computation.4 | async-start | bytes 10616832 | tf_op jit(solution)/shard_map/all_gather | solution.py:254
  9.7 187.1 %all-gather.5.cloned.1.call-start = ((), (), s32[]{:S(2)}) async-start(), calls=%async_computation.5 | async-start | bytes 10616832 | tf_op jit(solution)/shard_map/all_gather | solution.py:256
  72.0 48.9 %copy-start.4 = (s32[2,4]{1,0:T(2,128)S(1)}, s32[2,4]{1,0:T(2,128)}, u32[]{:S(2)}) copy-start(s32[2,4]{1,0:T(2,128)} %param.13) | copy-start | bytes 100
  120.9 9.1 copy-start.5
  126.4 35.8 %all-to-all-start = ((bf16[2,16,8,8,288]{4,2,1,0,3:T(8,128)(2,1)}), bf16[2,16,8,8,288]{4,2,1,0,3:T(8,128)(2,1)S(1)}, u32[]{:S(2)}, u32[]{:S(2)}) async-start(bf16[2,16,8,8,288]{4,2,1,0,3:T(8,128)(2,1)} %copy.61), calls=%async_computation | async-start | bytes 3145728 | tf_op jit(solution)/shard_map/all_to_all | solution.py:251
  130.0 241.5 %reduce-scatter.3.cloned.1.call-start = ((), (), s32[]{:S(2)}) async-start(), calls=%async_computation.6 | async-start | bytes 10616832 | tf_op jit(solution)/shard_map/reduce_scatter | solution.py:268
  294.9 230.6 %reduce-scatter.5.cloned.1.call-start = ((), (), s32[]{:S(2)}) async-start(), calls=%async_computation.7 | async-start | bytes 10616832 | tf_op jit(solution)/shard_map/reduce_scatter | solution.py:277
  424.4 625.6 %all-reduce.3.cloned.1.call-start = ((), (), s32[]{:S(2)}) async-start(), calls=%async_computation.8 | async-start | bytes 31850496 | tf_op jit(solution)/shard_map/psum | solution.py:274
  470.6 1.3 copy-start.1
  470.6 7.3 copy-start.2
  472.7 40.8 %copy-start.3 = (f32[2,288,1]{2,1,0:T(8,128)S(1)}, f32[2,288,1]{2,1,0:T(8,128)}, u32[]{:S(2)}) copy-start(f32[2,288,1]{2,1,0:T(8,128)} %get-tuple-element.20) | copy-start | bytes 6916
  474.1 35.9 %all-to-all-start.1 = ((bf16[2,288,8,8,16]{1,4,2,0,3:T(8,128)(2,1)}), bf16[2,288,8,8,16]{1,4,2,0,3:T(8,128)(2,1)S(1)}, u32[]{:S(2)}, u32[]{:S(2)}) async-start(bf16[2,288,8,8,16]{1,4,2,0,3:T(8,128)(2,1)} %copy.66), calls=%async_computation.1 | async-start | bytes 3145728 | tf_op jit(solution)/shard_map/all_to_all | solution.py:260
  1050.0 10.7 copy-start
Sparse Core Ops, SparseCore 0:
  10.5 61.5 all-gather.2
  121.1 75.6 all-gather.4
  295.0 76.4 reduce-scatter.2
  424.5 87.3 reduce-scatter.4
  515.0 534.9 all-reduce.2

commit v2 on v1

v2 whole, which is shorter than its diff:
```python
import functools

import jax
import jax.numpy as jnp
from jax import lax
from jax.experimental import pallas as pl
from jax.experimental.pallas import tpu as pltpu
from jax.sharding import PartitionSpec as P

CLUSTER = 32
LANES = 128
ROWS = 48
F32 = jnp.float32
BF16 = jnp.bfloat16
ANY = pl.BlockSpec(memory_space=pl.ANY)
MESH = pl.DeviceIdType.MESH
NN = (((1,), (0,)), ((), ()))
NT = (((1,), (1,)), ((), ()))
TN = (((0,), (0,)), ((), ()))


def dot(a, b, dims):
    return lax.dot_general(a, b, dims, preferred_element_type=F32)


def sigmoid(v):
    return 1.0 / (1.0 + jnp.exp(-v))


def tiles(count, rows, body):
    def step(r, carry):
        body(pl.multiple_of(r * rows, rows))
        return carry

    lax.fori_loop(0, count // rows, step, 0)


def shift_lanes(v, amount, lane, fill):
    moved = pltpu.roll(v, amount % LANES, axis=1)
    gone = lane < amount if amount > 0 else lane >= LANES + amount
    return jnp.where(gone, fill, moved)


def lane_chain(factor, value, lane, sign):
    step = 1
    while step < LANES:
        value = value + factor * shift_lanes(value, sign * step, lane, 0.0)
        factor = factor * shift_lanes(factor, sign * step, lane, 1.0)
        step *= 2
    return value


def pool_forward(first, p_ref, b_ref, pre_ref, cell_ref, h_ref, factor_ref, edge_ref, hidden, groups):
    lane = lax.broadcasted_iota(jnp.int32, (ROWS, LANES), 1)

    def at(j, start=0):
        return pl.ds(start + j * LANES, LANES)

    def gates(r):
        rows = pl.ds(r, ROWS)
        value = factor = None
        for j in range(groups):
            got = []
            for g in range(3):
                now = p_ref[pl.ds(g * hidden + r, ROWS), at(j)]
                tap = pl.ds((3 + g) * hidden + r, ROWS)
                if j:
                    past = p_ref[tap, at(j - 1)]
                else:
                    past = shift_lanes(p_ref[tap, at(groups - 1)], 1, lane, 0.0)
                total = now + past
                if g == 1:
                    total = total + b_ref[rows, :]
                total = total.astype(BF16)
                pre_ref[pl.ds(g * hidden + r, ROWS), at(j, first)] = total
                got.append(total.astype(F32))
            forget = sigmoid(got[1])
            fresh = (1.0 - forget) * jnp.tanh(got[0])
            if j:
                value = forget * value + fresh
                factor = forget * factor
            else:
                value, factor = fresh, forget
            cell_ref[rows, at(j, first)] = value
            factor_ref[rows, at(j)] = factor

    tiles(hidden, ROWS, gates)

    def chain(r):
        rows = pl.ds(r, ROWS)
        value = lane_chain(factor_ref[rows, at(groups - 1)], cell_ref[rows, at(groups - 1, first)], lane, 1)
        edge_ref[rows, :] = shift_lanes(value, 1, lane, 0.0)

    tiles(hidden, ROWS, chain)

    def finish(r):
        rows = pl.ds(r, ROWS)
        edge = edge_ref[rows, :]
        for j in range(groups):
            cell = cell_ref[rows, at(j, first)] + factor_ref[rows, at(j)] * edge
            cell_ref[rows, at(j, first)] = cell
            outgate = sigmoid(pre_ref[pl.ds(2 * hidden + r, ROWS), at(j, first)].astype(F32))
            h_ref[rows, at(j, first)] = (outgate * cell).astype(BF16)

    tiles(hidden, ROWS, finish)


def pool_backward(first, g_ref, pre_ref, cell_ref, target, d_ref, db_ref, work_ref, edge_ref, hidden, groups):
    lane = lax.broadcasted_iota(jnp.int32, (ROWS, LANES), 1)

    def at(j, start=0):
        return pl.ds(start + j * LANES, LANES)

    def gate(g, r, j):
        return pre_ref[pl.ds(g * hidden + r, ROWS), at(j, first)].astype(F32)

    def start(r):
        rows = pl.ds(r, ROWS)
        later = value = factor = None
        for j in reversed(range(groups)):
            own = g_ref[rows, at(j, first)].astype(F32) * sigmoid(gate(2, r, j))
            if later is None:
                value, factor = own, jnp.ones_like(own)
            else:
                value = own + later * value
                factor = later * factor
            work_ref[0, rows, at(j)] = value
            work_ref[1, rows, at(j)] = factor
            later = sigmoid(gate(1, r, j))
        edge_ref[0, rows, :] = later * value
        edge_ref[1, rows, :] = later * factor

    tiles(hidden, ROWS, start)

    def chain(r):
        rows = pl.ds(r, ROWS)
        value = lane_chain(edge_ref[1, rows, :], edge_ref[0, rows, :], lane, -1)
        edge_ref[0, rows, :] = shift_lanes(value, -1, lane, 0.0)

    tiles(hidden, ROWS, chain)

    def finish(r):
        rows = pl.ds(r, ROWS)
        edge = edge_ref[0, rows, :]
        total = jnp.zeros((ROWS, LANES), F32)
        before = shift_lanes(cell_ref[rows, at(groups - 1, first)], 1, lane, 0.0)
        for j in range(groups):
            carried = work_ref[0, rows, at(j)] + work_ref[1, rows, at(j)] * edge
            candidate = jnp.tanh(gate(0, r, j))
            forget = sigmoid(gate(1, r, j))
            outgate = sigmoid(gate(2, r, j))
            cell = cell_ref[rows, at(j, first)]
            keep = carried * (1.0 - forget)
            got = (
                keep * (1.0 - candidate * candidate),
                keep * forget * (before - candidate),
                g_ref[rows, at(j, first)].astype(F32) * cell * outgate * (1.0 - outgate),
            )
            before = cell
            for g, v in enumerate(got):
                v = v.astype(BF16)
                if g == 1:
                    total = total + v.astype(F32)
                d_ref[pl.ds(g * hidden + r, ROWS), at(j, target)] = v
                tap = pl.ds((3 + g) * hidden + r, ROWS)
                if j:
                    d_ref[tap, at(j - 1, target)] = v
                else:
                    d_ref[tap, at(groups - 1, target)] = shift_lanes(v.astype(F32), -1, lane, 0.0).astype(BF16)
        db_ref[rows, :] = jnp.sum(total, axis=1, keepdims=True)

    tiles(hidden, ROWS, finish)


def first_kernel(hidden, length, w_ref, b_ref, x_ref, pre_ref, cell_ref, h_ref, p_ref, work_ref, edge_ref):
    def strip(c):
        cols = pl.ds(c, 512)
        p_ref[:, cols] = dot(w_ref[...], x_ref[cols, :], NT)

    tiles(length, 512, strip)
    pool_forward(0, p_ref, b_ref, pre_ref, cell_ref, h_ref, work_ref, edge_ref, hidden, length // LANES)


def second_kernel(
    hidden, length, w_ref, b_ref, x_ref, g_ref, h_ref, d_ref, db_ref, p_ref, pre_ref, cell_ref, work_ref, edge_ref
):
    def strip(c):
        cols = pl.ds(c, 512)
        p_ref[:, cols] = dot(w_ref[...], x_ref[:, cols], NN)

    tiles(length, 512, strip)
    groups = length // LANES
    pool_forward(0, p_ref, b_ref, pre_ref, cell_ref, h_ref, work_ref.at[0], edge_ref.at[0], hidden, groups)
    pool_backward(0, g_ref, pre_ref, cell_ref, 0, d_ref, db_ref.at[0], work_ref, edge_ref, hidden, groups)


def back_kernel(hidden, length, g_ref, pre_ref, cell_ref, d_ref, db_ref, work_ref, edge_ref):
    pool_backward(0, g_ref, pre_ref, cell_ref, 0, d_ref, db_ref.at[0], work_ref, edge_ref, hidden, length // LANES)


def columns(rows, length):
    return pl.BlockSpec((rows, length), lambda s: (0, s))


def fixed(*dims):
    return pl.BlockSpec(dims, lambda s: (0,) * len(dims), pipeline_mode=pl.Buffered(1))


def params(**more):
    return pltpu.CompilerParams(vmem_limit_bytes=63 * 1024 * 1024, **more)


shape = jax.ShapeDtypeStruct


def run_first(seqs, weight, bias, gathered):
    (wide, width), total = weight.shape, gathered.shape[0]
    hidden, length = wide // 6, total // seqs
    return pl.pallas_call(
        functools.partial(first_kernel, hidden, length),
        name="layer_one_forward",
        grid=(seqs,),
        in_specs=[fixed(wide, width), fixed(hidden, 1), pl.BlockSpec((length, width), lambda s: (s, 0))],
        out_specs=[columns(3 * hidden, length), columns(hidden, length), columns(hidden, length)],
        out_shape=[shape((3 * hidden, total), BF16), shape((hidden, total), F32), shape((hidden, total), BF16)],
        scratch_shapes=[
            pltpu.VMEM((wide, length), F32),
            pltpu.VMEM((hidden, length), F32),
            pltpu.VMEM((hidden, LANES), F32),
        ],
        compiler_params=params(),
    )(weight, bias, gathered)


def run_second(seqs, weight, bias, gathered, grad):
    (wide, width), total = weight.shape, gathered.shape[1]
    hidden, length = wide // 6, total // seqs
    return pl.pallas_call(
        functools.partial(second_kernel, hidden, length),
        name="layer_two_forward_and_pool_backward",
        grid=(seqs,),
        in_specs=[fixed(wide, width), fixed(hidden, 1), columns(width, length), columns(hidden, length)],
        out_specs=[columns(hidden, length), columns(wide, length), pl.BlockSpec((1, hidden, 1), lambda s: (s, 0, 0))],
        out_shape=[shape((hidden, total), BF16), shape((wide, total), BF16), shape((seqs, hidden, 1), F32)],
        scratch_shapes=[
            pltpu.VMEM((wide, length), F32),
            pltpu.VMEM((3 * hidden, length), BF16),
            pltpu.VMEM((hidden, length), F32),
            pltpu.VMEM((2, hidden, length), F32),
            pltpu.VMEM((2, hidden, LANES), F32),
        ],
        compiler_params=params(),
    )(weight, bias, gathered, grad)


def run_back(seqs, grad, pre, cell):
    hidden, total = grad.shape
    length = total // seqs
    return pl.pallas_call(
        functools.partial(back_kernel, hidden, length),
        name="layer_one_pool_backward",
        grid=(seqs,),
        in_specs=[columns(hidden, length), columns(3 * hidden, length), columns(hidden, length)],
        out_specs=[columns(6 * hidden, length), pl.BlockSpec((1, hidden, 1), lambda s: (s, 0, 0))],
        out_shape=[shape((6 * hidden, total), BF16), shape((seqs, hidden, 1), F32)],
        scratch_shapes=[pltpu.VMEM((2, hidden, length), F32), pltpu.VMEM((2, hidden, LANES), F32)],
        compiler_params=params(),
    )(grad, pre, cell)


UNITS = 18
THIRDS = 3
SLOTS = 6
AHEAD = 4


class Here:
    def __init__(self):
        self.z = lax.axis_index("seq")
        self.b = lax.axis_index("tm")
        self.c = lax.rem(self.b, 2)
        self.x = lax.rem(self.b // 2, 2)
        self.y = self.b // 4
        self.core = dict(seq=self.z, tm=self.b + 1 - 2 * self.c)
        self.across_x = dict(seq=self.z, tm=self.b + 2 - 4 * self.x)
        self.across_y = dict(seq=self.z, tm=self.b + 4 - 8 * self.y)
        self.pair = dict(seq=self.z + 1 - 2 * lax.rem(self.z, 2), tm=self.b)
        self.middle = dict(seq=3 - self.z, tm=self.b)
        self.peers = [dict(seq=self.z, tm=lax.rem(self.b + d, 8)) for d in range(1, 8)]
        self.is_end = jnp.logical_or(self.z == 0, self.z == 3)
        self.is_centre = jnp.logical_and(self.z > 0, self.z < 3)


def remote(src, dst, send, recv, target):
    return pltpu.make_async_remote_copy(
        src_ref=src, dst_ref=dst, send_sem=send, recv_sem=recv, device_id=target, device_id_type=MESH
    )


def both(a, b):
    if isinstance(a, bool) and isinstance(b, bool):
        return a and b
    return jnp.logical_and(a, b)


def signal(sem, target):
    pl.semaphore_signal(sem, inc=1, device_id=target, device_id_type=MESH)


def meet(here, everyone):
    barrier = pltpu.get_barrier_semaphore()
    near = here.peers if everyone else [here.core, here.across_x, here.across_y]
    targets = near + [here.pair, here.middle]
    for target in targets:
        signal(barrier, target)
    pl.semaphore_wait(barrier, len(targets))


class SeqSum:
    def __init__(self, here, hidden, third, own, ring_in, ring_mid, total, out, sems, credits):
        self.here, self.hidden, self.third = here, hidden, third
        self.own, self.ring_in, self.ring_mid, self.total, self.out = own, ring_in, ring_mid, total, out
        self.sems = sems
        self.credit_in, self.credit_mid, self.credit_out = credits

    def inward(self, u):
        i = lax.rem(u, SLOTS)
        return remote(self.own.at[u], self.ring_in.at[i], self.sems.at[0, i], self.sems.at[1, i], self.here.pair)

    def across(self, u):
        i = lax.rem(u, SLOTS)
        return remote(self.own.at[u], self.ring_mid.at[i], self.sems.at[2, i], self.sems.at[3, i], self.here.middle)

    def outward(self, u):
        i = lax.rem(u, SLOTS)
        return remote(self.total.at[i], self.ring_in.at[i], self.sems.at[4, i], self.sems.at[5, i], self.here.pair)

    def store(self, u, ring):
        i = lax.rem(u, SLOTS)
        cols = pl.ds(pl.multiple_of((u // 6) * self.third, LANES), self.third)
        return pltpu.make_async_copy(ring.at[i], self.out.at[lax.rem(u, 6), :, cols], self.sems.at[6, i])

    def add(self, dst, i, a, ia, b, ib):
        def rows(r):
            at = pl.ds(r, ROWS)
            dst[i, at, :] = a[ia, at, :] + b[ib, at, :]

        tiles(self.hidden, ROWS, rows)

    def offer(self, u):
        @pl.when(self.here.is_end)
        def _():
            @pl.when(u >= SLOTS)
            def _():
                pl.semaphore_wait(self.credit_in, 1)
                self.inward(u - SLOTS).wait_send()

            self.inward(u).start()

    def gather(self, u):
        i = lax.rem(u, SLOTS)
        self.inward(u).wait_recv()
        self.add(self.own, u, self.own, u, self.ring_in, i)

        @pl.when(u + SLOTS < UNITS)
        def _():
            signal(self.credit_in, self.here.pair)

        @pl.when(u >= SLOTS)
        def _():
            pl.semaphore_wait(self.credit_mid, 1)
            self.across(u - SLOTS).wait_send()

        self.across(u).start()

    def finish(self, u):
        i = lax.rem(u, SLOTS)
        self.across(u).wait_recv()

        @pl.when(u >= SLOTS)
        def _():
            pl.semaphore_wait(self.credit_out, 1)
            self.outward(u - SLOTS).wait_send()
            self.store(u - SLOTS, self.total).wait()

        self.add(self.total, i, self.own, u, self.ring_mid, i)

        @pl.when(u + SLOTS < UNITS)
        def _():
            signal(self.credit_mid, self.here.middle)

        self.outward(u).start()
        self.store(u, self.total).start()

    def accept(self, u):
        self.outward(u).wait_recv()
        self.store(u, self.ring_in).start()

        @pl.when(u > 0)
        def _():
            self.store(u - 1, self.ring_in).wait()

            @pl.when(u - 1 + SLOTS < UNITS)
            def _():
                signal(self.credit_out, self.here.pair)

    def tick(self, n):
        @pl.when(self.here.is_centre)
        def _():
            @pl.when(n < UNITS)
            def _():
                self.gather(n)

            @pl.when(both(n >= 1, n <= UNITS))
            def _():
                self.finish(n - 1)

        @pl.when(n + AHEAD < UNITS)
        def _():
            self.offer(n + AHEAD)

        @pl.when(n >= 2)
        def _():
            @pl.when(self.here.is_end)
            def _():
                self.accept(n - 2)

    def drain(self):
        @pl.when(self.here.is_centre)
        def _():
            for u in range(UNITS - SLOTS, UNITS):
                self.across(u).wait_send()
                self.outward(u).wait_send()
                self.store(u, self.total).wait()

        @pl.when(self.here.is_end)
        def _():
            for u in range(UNITS - SLOTS, UNITS):
                self.inward(u).wait_send()
            self.store(UNITS - 1, self.ring_in).wait()


class RankSum:
    def __init__(self, here, part, pairs, wide_x, wide_y, last_x, last_y, sems):
        self.here, self.part, self.pairs = here, part, pairs
        self.wide_x, self.wide_y, self.last_x, self.last_y, self.sems = wide_x, wide_y, last_x, last_y, sems
        self.rows = part.shape[3]
        self.upper = pl.ds(0, self.rows // 2)
        self.lower = pl.ds(self.rows // 2, self.rows // 2)
        self.step = 16

    def copy(self, k, s, src, dst, target):
        return remote(src, dst, self.sems.at[s, k, 0], self.sems.at[s, k, 1], target)

    def swap(self, s):
        return self.copy(0, s, self.part.at[:, :, 1 - self.here.c], self.pairs.at[s], self.here.core)

    def wide(self, s):
        h = self.here
        return (
            self.copy(1, s, self.pairs.at[s, :, 1 - h.x, self.upper], self.wide_x.at[s], h.across_x),
            self.copy(2, s, self.pairs.at[s, 1 - h.y, :, self.lower], self.wide_y.at[s], h.across_y),
        )

    def last(self, s):
        h = self.here
        return (
            self.copy(3, s, self.pairs.at[s, 1 - h.y, h.x, self.upper], self.last_y.at[s], h.across_y),
            self.copy(4, s, self.pairs.at[s, h.y, 1 - h.x, self.lower], self.last_x.at[s], h.across_x),
        )

    def start(self, s):
        self.swap(s).start()

    def cross(self, s):
        h = self.here
        self.swap(s).wait()

        def rows(r):
            at = pl.ds(r, self.step)
            for y in range(2):
                for x in range(2):
                    self.pairs[s, y, x, at, :] = self.pairs[s, y, x, at, :] + self.part[y, x, h.c, at, :]

        tiles(self.rows, self.step, rows)
        for copy in self.wide(s):
            copy.start()

    def turn(self, s):
        h = self.here
        half = self.rows // 2
        for copy in self.wide(s):
            copy.wait()

        def rows(r):
            at, low = pl.ds(r, self.step), pl.ds(half + r, self.step)
            for k in range(2):
                self.pairs[s, k, h.x, at, :] = self.pairs[s, k, h.x, at, :] + self.wide_x[s, k, at, :]
                self.pairs[s, h.y, k, low, :] = self.pairs[s, h.y, k, low, :] + self.wide_y[s, k, at, :]

        tiles(half, self.step, rows)
        for copy in self.last(s):
            copy.start()

    def done(self, s, out):
        h = self.here
        half = self.rows // 2
        for copy in self.last(s):
            copy.wait()

        def rows(r):
            at, low = pl.ds(r, self.step), pl.ds(half + r, self.step)
            out[at, :] = self.pairs[s, h.y, h.x, at, :] + self.last_y[s, at, :]
            out[low, :] = self.pairs[s, h.y, h.x, low, :] + self.last_x[s, at, :]

        tiles(half, self.step, rows)


def sum_scratch(seqs, hidden, third, rows, cols):
    return [
        pltpu.VMEM((UNITS, hidden, third), BF16),
        pltpu.VMEM((SLOTS, hidden, third), BF16),
        pltpu.VMEM((SLOTS, hidden, third), BF16),
        pltpu.VMEM((SLOTS, hidden, third), BF16),
        pltpu.SemaphoreType.DMA((7, SLOTS)),
        pltpu.SemaphoreType.REGULAR,
        pltpu.SemaphoreType.REGULAR,
        pltpu.SemaphoreType.REGULAR,
        pltpu.VMEM((2, 2, 2, rows, cols), BF16),
        pltpu.VMEM((seqs, 2, 2, rows, cols), BF16),
        pltpu.VMEM((seqs, 2, rows // 2, cols), BF16),
        pltpu.VMEM((seqs, 2, rows // 2, cols), BF16),
        pltpu.VMEM((seqs, rows // 2, cols), BF16),
        pltpu.VMEM((seqs, rows // 2, cols), BF16),
        pltpu.SemaphoreType.DMA((seqs, 5, 2)),
        pltpu.SemaphoreType.DMA((8,)),
    ]


def backward_kernel(second, seqs, hidden, length, width, *refs):
    third = width // THIRDS
    if second:
        d_in, r_in, w_in, pre_in, cell_in, h_in, gw_out, d_out, db_out, h_out = refs[:10]
        dv, wv, rv, pre, cell, work, edge, grad, hsem = refs[10:19]
        rest = refs[19:]
    else:
        d_in, r_in, w_in, gw_out, gx_out = refs[:5]
        dv, wv, rv, gxv = refs[5:9]
        rest = refs[9:]
    own, ring_in, ring_mid, total, zsem, *credits = rest[:8]
    rank_refs, lsem = rest[8:15], rest[15]
    here = Here()
    ar = SeqSum(here, hidden, third, own, ring_in, ring_mid, total, gw_out, zsem, credits)
    rs = RankSum(here, *rank_refs)
    groups = length // LANES

    def columns_of(s):
        return pl.ds(s * length, length)

    def rhs(t):
        if second:
            src = r_in.at[pl.ds(t * third, third), :]
        else:
            src = r_in.at[:, pl.ds(t * third, third)]
        return pltpu.make_async_copy(src, rv.at[t % 2], lsem.at[t % 2])

    loads = [pltpu.make_async_copy(d_in, dv, lsem.at[2]), pltpu.make_async_copy(w_in, wv, lsem.at[3])]
    if second:
        loads.append(pltpu.make_async_copy(pre_in, pre, lsem.at[4]))
        loads.append(pltpu.make_async_copy(cell_in, cell, lsem.at[5]))
    loads[0].start()
    rhs(0).start()
    for copy in loads[1:]:
        copy.start()
    rhs(1).start()
    meet(here, second)
    spread = []
    if second:
        spread.append(pltpu.make_async_copy(h_in.at[here.b], h_out.at[here.b], hsem.at[0, 0]))
        for d, peer in enumerate(here.peers, 1):
            spread.append(remote(h_in.at[peer["tm"]], h_out.at[here.b], hsem.at[d, 0], hsem.at[d, 1], peer))
        for copy in spread:
            copy.start()

    def units(t, ks):
        for k in ks:
            rows = pl.ds(k * hidden, hidden)
            own[t * 6 + k] = dot(dv[rows, :], rv[t % 2], NT if second else NN).astype(BF16)
            if t * 6 + k < AHEAD:
                ar.offer(t * 6 + k)

    def part(s, piece):
        if second:
            i, start = piece // 2, piece % 2 * (length // 2)
            lhs = pl.ds(i * (width // 2), width // 2)

            def strip(c):
                cols = pl.ds(pl.multiple_of(start + c, 256), 256)
                src = pl.ds(pl.multiple_of(s * length + start + c, 256), 256)
                got = dot(wv[:, lhs], dv[:, src], TN).astype(BF16)
                rs.part[i, :, :, :, cols] = got.reshape(2, 2, hidden, 256)

            tiles(length // 2, 256, strip)
        else:
            rows = LANES // 8
            low, high = (width // 256 * q // 4 * 256 for q in (piece, piece + 1))

            def strip(c):
                cols = pl.ds(pl.multiple_of(low + c, 256), 256)
                got = dot(dv[:, columns_of(s)], wv[:, cols], TN).astype(BF16)
                for j in range(groups):
                    block = got[j * LANES : (j + 1) * LANES].reshape(2, 2, 2, rows, 256)
                    rs.part[:, :, :, pl.ds(j * rows, rows), cols] = block

            tiles(high - low, 256, strip)

    ticks = iter(range(UNITS + 2))

    def tick():
        ar.tick(next(ticks))

    def settle(s):
        rs.done(s, grad.at[:, columns_of(s)] if second else gxv.at[s])

    loads[0].wait()
    rhs(0).wait()
    units(0, range(6))
    rhs(2).start()
    loads[1].wait()
    part(0, 0)
    part(0, 1)
    tick()
    part(0, 2)
    part(0, 3)
    rs.start(0)
    tick()
    rhs(1).wait()
    units(1, range(3))
    rs.cross(0)
    tick()
    part(1, 0)
    part(1, 1)
    part(1, 2)
    tick()
    part(1, 3)
    rs.start(1)
    units(1, range(3, 6))
    tick()
    rs.turn(0)
    rhs(2).wait()
    units(2, range(2))
    rs.cross(1)
    units(2, range(2, 4))
    tick()
    units(2, range(4, 6))
    settle(0)
    if second:
        for copy in loads[2:]:
            copy.wait()
        stores = [
            pltpu.make_async_copy(dv.at[:, columns_of(s)], d_out.at[:, columns_of(s)], lsem.at[6 + s])
            for s in range(seqs)
        ]

        def pool(s):
            first = s * length
            pool_backward(first, grad, pre, cell, first, dv, db_out.at[s], work, edge, hidden, groups)
            stores[s].start()

        tick()
        pool(0)
    else:
        tick()
    rs.turn(1)
    tick()
    tick()
    settle(1)
    if second:
        pool(1)
    else:
        stores = [pltpu.make_async_copy(gxv, gx_out, lsem.at[6])]
        stores[0].start()

    def more(n, carry):
        ar.tick(n)
        return carry

    lax.fori_loop(next(ticks), UNITS + 2, more, 0)
    ar.drain()
    for copy in stores + spread:
        copy.wait()


def run_backward(seqs, d, rhs, weight, layer_one=None):
    second = layer_one is not None
    (wide, width), total = weight.shape, d.shape[1]
    hidden, length = wide // 6, total // seqs
    third, span = width // THIRDS, length // 8
    outs = [shape((6, hidden, width), BF16)]
    scratch = [pltpu.VMEM((wide, total), BF16), pltpu.VMEM((wide, width), BF16)]
    if second:
        outs += [shape((wide, total), BF16), shape((seqs, hidden, 1), F32), shape(layer_one[2].shape, BF16)]
        specs = [ANY, ANY, pl.BlockSpec(memory_space=pltpu.VMEM), ANY]
        rows, cols = hidden, length
        scratch += [
            pltpu.VMEM((2, third, total), BF16),
            pltpu.VMEM((3 * hidden, total), BF16),
            pltpu.VMEM((hidden, total), F32),
            pltpu.VMEM((2, hidden, length), F32),
            pltpu.VMEM((2, hidden, LANES), F32),
            pltpu.VMEM((hidden, total), BF16),
            pltpu.SemaphoreType.DMA((8, 2)),
        ]
    else:
        outs += [shape((seqs, span, width), BF16)]
        specs = [ANY, ANY]
        rows, cols = span, width
        scratch += [pltpu.VMEM((2, total, third), BF16), pltpu.VMEM((seqs, span, width), BF16)]
    operands = (d, rhs, weight) + (layer_one or ())
    return pl.pallas_call(
        functools.partial(backward_kernel, second, seqs, hidden, length, width),
        name="layer_two_backward" if second else "layer_one_backward",
        in_specs=[ANY] * len(operands),
        out_specs=specs,
        out_shape=outs,
        scratch_shapes=scratch + sum_scratch(seqs, hidden, third, rows, cols),
        compiler_params=params(collective_id=1 if second else 2, has_side_effects=True),
    )(*operands)


def per_device(line, inputs, weight_one, fbias_one, weight_two, fbias_two, cotangent, cluster_starts):
    seqs, span, width = inputs.shape
    count = lax.axis_size("tm")
    length = span * count
    groups = length // LANES
    piece = LANES // count
    hidden = weight_one.shape[2]
    total = seqs * length
    w1 = weight_one.reshape(6 * hidden, width)
    w2 = weight_two.reshape(6 * hidden, width)

    steps = lax.axis_index("tm") * span + jnp.arange(span, dtype=jnp.int32)
    starts = cluster_starts[:, :, None]
    keep = jnp.any((steps >= starts) & (steps < starts + CLUSTER), axis=1)
    seed = jnp.where(keep[:, :, None], cotangent, jnp.zeros_like(cotangent))
    seed = seed.reshape(seqs, piece, groups, count, hidden)
    seed = lax.all_to_all(seed, "tm", split_axis=3, concat_axis=1, tiled=True)
    seed = seed.reshape(seqs, LANES, groups, hidden).transpose(3, 0, 2, 1).reshape(hidden, total)

    x = inputs.reshape(seqs, piece, groups, width).transpose(0, 2, 1, 3)
    x = lax.all_gather(x, "tm", axis=2, tiled=True).reshape(total, width)
    pre1, cell1, h1 = run_first(seqs, w1, fbias_one[:, None], x)
    h1 = lax.all_gather(h1, "tm", axis=0, tiled=True)
    h2, d2, db2 = run_second(seqs, w2, fbias_two[:, None], h1, seed)

    h2 = h2.reshape(hidden, seqs, groups, count, piece)
    if line:
        h2 = h2.transpose(3, 1, 2, 4, 0).reshape(count, seqs * groups * piece, hidden)
        gw2, d1, db1, h2 = run_backward(seqs, d2, h1, w2, (pre1, cell1, h2))
        h2 = h2.reshape(count, seqs, groups, piece, hidden).transpose(1, 3, 2, 0, 4)
        gw1, gx1 = run_backward(seqs, d1, x, w1)
        gx1 = gx1.reshape(seqs, groups, piece, width)
    else:
        h2 = lax.all_to_all(h2, "tm", split_axis=3, concat_axis=0, tiled=True)
        h2 = h2.reshape(width, seqs, groups, piece).transpose(1, 3, 2, 0)
        gw2 = lax.psum(dot(d2, h1, NT).astype(BF16), "seq")
        gx2 = lax.psum_scatter(dot(w2, d2, TN).astype(BF16), "tm", scatter_dimension=0, tiled=True)
        d1, db1 = run_back(seqs, gx2, pre1, cell1)
        gw1 = lax.psum(dot(d1, x, NN).astype(BF16), "seq")
        gx1 = dot(d1, w1, TN).astype(BF16).reshape(seqs, groups, LANES, width)
        gx1 = lax.psum_scatter(gx1, "tm", scatter_dimension=2, tiled=True)
    out = h2.reshape(seqs, span, width)
    gx1 = gx1.transpose(0, 2, 1, 3).reshape(seqs, span, width)
    db = lax.psum(jnp.stack([db1, db2]).sum(axis=(1, 3)), "seq")
    dims = weight_one.shape
    return (out, gx1, gw1.astype(F32).reshape(dims), db[0], gw2.astype(F32).reshape(dims), db[1])


def solution(mesh):
    placed = (
        P("seq", "tm", None),
        P(None, None, "tm", None),
        P("tm"),
        P(None, None, "tm", None),
        P("tm"),
        P("seq", "tm", None),
        P("seq", None),
    )
    return jax.shard_map(
        functools.partial(per_device, dict(mesh.shape) == {"seq": 4, "tm": 8}),
        mesh=mesh,
        in_specs=placed,
        out_specs=(
            P("seq", "tm", None),
            P("seq", "tm", None),
            P(None, None, "tm", None),
            P("tm"),
            P(None, None, "tm", None),
            P("tm"),
        ),
        check_vma=False,
    )
```

time: 1070 us -> 681 us (0.64)
  waiting for transfers between devices: 754 us -> 124 us
  Pallas kernels: 153 us -> 483 us
  matrix products: 92.6 us -> 0 us
    psum x1 -> x0, waiting for transfers between devices: 522 us -> none  [per_device(): gw1 = lax.psum(gw1, 'seq')]
    pallas_call x1 -> x2, Pallas kernels: 29.6 us -> 402 us  [run_backward(): pl.pallas_call(functools.partial(backward_kernel, second, seqs, hidden, l...]
    dot_general x4 -> x0, matrix products: 92.6 us -> none  [the longest x1 23.3 us: per_device(): jnp.einsum('skt,std->kd', d1, x, preferred_element_type=F32).astype(BF16)]
    reduce_scatter x2 -> x0, waiting for transfers between devices: 76.4 us -> none  [the longest x1 76.4 us: per_device(): gx2 = lax.psum_scatter(gx2, 'tm', scatter_dimension=1, tiled=True)]
    all_to_all x1 -> x0, waiting for transfers between devices: 31.9 us -> none  [per_device(): out = lax.all_to_all(out, 'tm', split_axis=3, concat_axis=1, tiled=True)]
    pallas_call x1, Pallas kernels: 74.8 us -> 46.5 us  [run_second(): pl.pallas_call(functools.partial(second_kernel, hidden, length), name='la...]
    pallas_call x1, Pallas kernels: 48.9 us -> 34.2 us  [run_first(): pl.pallas_call(functools.partial(first_kernel, hidden, length), name='lay...]
  transfers between devices with their start and end apart: 7 -> 3, of which waited for: 6 -> 3; matrix products, arithmetic and copies ran while one was open for 6% -> 1% of each run, Pallas kernels for 0% -> 0%
where the time goes in v2:
time: 681 us; the launch traced here: 676 us
  Pallas kernels  483 us (71%)
  waiting for transfers between devices  124 us (18%)
  local copies, waits for them, and re-layouts  21.5 us (3%)
  other arithmetic  18.6 us (3%)
  between operations  14.4 us (2%)
  blocking collectives  9.9 us (1%)
    pallas_call x2, Pallas kernels, run_backward(): pl.pallas_call(functools.partial(backward_kernel, second, seqs, hidden, l...  402 us
    all_gather x1, waiting for transfers between devices, per_device(): x = lax.all_gather(x, 'tm', axis=2, tiled=True).reshape(total, width)  61.5 us
    pallas_call x1, Pallas kernels, run_second(): pl.pallas_call(functools.partial(second_kernel, hidden, length), name='la...  46.5 us
    pallas_call x1, Pallas kernels, run_first(): pl.pallas_call(functools.partial(first_kernel, hidden, length), name='lay...  34.2 us
    all_gather x1, waiting for transfers between devices, per_device(): h1 = lax.all_gather(h1, 'tm', axis=0, tiled=True)  31.6 us
    all_to_all x1, waiting for transfers between devices, per_device(): seed = lax.all_to_all(seed, 'tm', split_axis=3, concat_axis=1, tiled=True)  31.1 us
  transfers between devices with their start and end apart: 3, of which 3 were waited for; matrix products, arithmetic and copies ran while one was open for 1% of the time, Pallas kernels for 0%

profile of v2, /device:TPU:0, one launch (start us, length us, event | category | flops | bytes accessed | tf_op | source)
XLA Modules:
  0.0 675.7 jit_solution(18083077188136392532)
XLA Ops:
  7.2 0.0 all-gather.3.cloned.1.call-start
  7.2 2.5 copy.62
  9.7 0.0 all-gather.5.cloned.1.call-start
  9.8 0.8 broadcast_in_dim.26.b_ref
  10.6 61.5 %all-gather.3.cloned.1.call-done = bf16[2,8,128,2304]{3,2,1,0:T(8,128)(2,1)} async-done(((bf16[2,8,16,2304]{3,2,1,0:T(8,128)(2,1)}), bf16[2,8,128,2304]{3,2,1,0:T(8,128)(2,1)}) %all-gather.3.cloned.1.call-update) | async-done | bytes 9437200 | tf_op jit(solution)/shard_map/all_gather | solution.py:751
  72.0 34.2 %layer_one_forward.1 = (bf16[864,2048]{1,0:T(8,128)(2,1)}, f32[288,2048]{1,0:T(8,128)}, bf16[288,2048]{1,0:T(8,128)(2,1)}) custom-call(bf16[1728,2304]{1,0:T(8,128)(2,1)} %bitcast.43, f32[288,1]{1,0:T(8,128)} %broadcast_in_dim.26.b_ref, bf16[2048,2304]{1,0:T(8,128)(2,1)} %bitcast.39), custom_call_target="tpu_custom_call" | custom-call | tf_op jit(solution)/shard_map/layer_one_forward/pallas_call | solution.py:219
  106.3 0.1 and_reduce_fusion
  106.4 1.1 copy-done
  107.5 0.1 broadcast_select_fusion
  107.7 2.5 reshape.76
  110.2 1.4 copy.48
  111.6 4.1 all-to-all-start
  115.6 0.8 broadcast_in_dim.25.b_ref
  116.4 31.1 %all-to-all-done = bf16[2,16,8,8,288]{4,2,1,0,3:T(8,128)(2,1)S(1)} async-done(((bf16[2,16,8,8,288]{4,2,1,0,3:T(8,128)(2,1)}), bf16[2,16,8,8,288]{4,2,1,0,3:T(8,128)(2,1)S(1)}, u32[]{:S(2)}, u32[]{:S(2)}) %all-to-all-start) | async-done | bytes 1179680 | tf_op jit(solution)/shard_map/all_to_all | solution.py:747
  147.5 0.2 copy.49
  147.7 1.5 copy.50
  149.2 1.3 copy.60
  150.5 31.6 %all-gather.5.cloned.1.call-done.x_ref.refs_1_ = bf16[2304,2048]{1,0:T(8,128)(2,1)} async-done(((bf16[288,2048]{1,0:T(8,128)(2,1)}), bf16[2304,2048]{1,0:T(8,128)(2,1)}) %all-gather.5.cloned.1.call-update) | async-done | bytes 9437200 | tf_op jit(solution)/shard_map/all_gather | solution.py:753
  182.1 46.5 %layer_two_forward_and_pool_backward.1 = (bf16[288,2048]{1,0:T(8,128)(2,1)}, bf16[1728,2048]{1,0:T(8,128)(2,1)}, f32[2,288,1]{2,1,0:T(8,128)}) custom-call(bf16[1728,2304]{1,0:T(8,128)(2,1)} %bitcast.41, f32[288,1]{1,0:T(8,128)} %broadcast_in_dim.25.b_ref, bf16[2304,2048]{1,0:T(8,128)(2,1)} %all-gather.5.cloned.1.call-done.x_ref.refs_1_, ...), custom_call_target="tpu_custom_call" | custom-call | tf_op jit(solution)/shard_map/layer_two_forward_and_pool_backward/pallas_call | solution.py:238
  228.7 1.8 copy.52
  230.5 1.4 copy.53
  231.8 204.5 %layer_two_backward.1 = (bf16[6,288,2304]{2,1,0:T(8,128)(2,1)}, bf16[1728,2048]{1,0:T(8,128)(2,1)}, f32[2,288,1]{2,1,0:T(8,128)}, bf16[8,256,288]{2,1,0:T(8,128)(2,1)}) custom-call(bf16[1728,2048]{1,0:T(8,128)(2,1)} %get-tuple-element.19.refs_0_, bf16[2304,2048]{1,0:T(8,128)(2,1)} %all-gather.5.cloned.1.call-done.x_ref.refs_1_, bf16[1728,2304]{1,0:T(8,128)(2,1)} %bitcast.42, ...), custom_call_target="tpu_custom_call" | custom-call | tf_op jit(solution)/shard_map/layer_two_backward/pallas_call | solution.py:720
  436.3 197.7 %layer_one_backward.1 = (bf16[6,288,2304]{2,1,0:T(8,128)(2,1)}, bf16[2,128,2304]{2,1,0:T(8,128)(2,1)}) custom-call(bf16[1728,2048]{1,0:T(8,128)(2,1)} %get-tuple-element.24.refs_0_, bf16[2048,2304]{1,0:T(8,128)(2,1)} %bitcast.40, bf16[1728,2304]{1,0:T(8,128)(2,1)} %bitcast.44), custom_call_target="tpu_custom_call" | custom-call | tf_op jit(solution)/shard_map/layer_one_backward/pallas_call | solution.py:720
  634.1 2.3 copy.54
  636.4 2.1 reshape.82
  638.5 1.4 copy.61
  639.8 0.2 reduce.1
  640.0 0.2 reduce
  640.2 9.9 %psum.7 = f32[2,288]{1,0:T(2,128)S(1)} all-reduce(f32[2,288]{1,0:T(2,128)S(1)} %maximum_reduce_fusion), channel_id=1, replica_groups=mesh['seq'=4,'tm'=8] {'seq'}, use_global_device_ids=true, to_apply=%region_2.3 | all-reduce | flops 576 | bytes 4608 | tf_op jit(solution)/shard_map/psum | solution.py:774
  650.1 0.6 slice_reduce_fusion
  650.8 10.7 %convert.2 = f32[2,3,288,2304]{3,2,1,0:T(8,128)} convert(bf16[2,3,288,2304]{3,2,1,0:T(8,128)(2,1)} %bitcast.48) | non-fusion elementwise | flops 3981312 | bytes 23887872 | tf_op jit(solution)/shard_map/reshape | solution.py:776
  661.4 7.3 %convert.3 = f32[2,3,288,2304]{3,2,1,0:T(8,128)} convert(bf16[2,3,288,2304]{3,2,1,0:T(8,128)(2,1)S(1)} %bitcast.47) | non-fusion elementwise | flops 3981312 | bytes 23887872 | tf_op jit(solution)/shard_map/reshape | solution.py:776
  (23 shorter events, 0.1 us)
Async XLA Ops:
  7.2 64.9 %all-gather.3.cloned.1.call-start = ((), (), s32[]{:S(2)}) async-start(), calls=%async_computation.1 | async-start | bytes 10616832 | tf_op jit(solution)/shard_map/all_gather | solution.py:751
  7.2 2.6 copy-start.5
  9.7 172.4 %all-gather.5.cloned.1.call-start = ((), (), s32[]{:S(2)}) async-start(), calls=%async_computation.2 | async-start | bytes 10616832 | tf_op jit(solution)/shard_map/all_gather | solution.py:753
  72.0 34.3 %copy-start.4 = (s32[2,4]{1,0:T(2,128)S(1)}, s32[2,4]{1,0:T(2,128)}, u32[]{:S(2)}) copy-start(s32[2,4]{1,0:T(2,128)} %param.13) | copy-start | bytes 100
  106.3 1.3 copy-start
  111.6 4.1 copy-start.6
  111.6 35.9 %all-to-all-start = ((bf16[2,16,8,8,288]{4,2,1,0,3:T(8,128)(2,1)}), bf16[2,16,8,8,288]{4,2,1,0,3:T(8,128)(2,1)S(1)}, u32[]{:S(2)}, u32[]{:S(2)}) async-start(bf16[2,16,8,8,288]{4,2,1,0,3:T(8,128)(2,1)} %copy.48), calls=%async_computation | async-start | bytes 3145728 | tf_op jit(solution)/shard_map/all_to_all | solution.py:747
  636.4 2.1 copy-start.1
  638.5 1.4 copy-start.2
  638.5 1.5 copy-start.3
  650.7 10.7 %slice-start = ((s8[7962624]{0:T(1024)(128)(4,1)}), s8[4194304]{0:T(1024)(128)(4,1)S(1)}, s32[]{:S(2)}) async-start(s8[7962624]{0:T(1024)(128)(4,1)} %bitcast.45), calls=%async_computation.3 | async-start | bytes 8388608
  650.7 10.7 %slice-start.1 = ((s8[7962624]{0:T(1024)(128)(4,1)}), s8[3768320]{0:T(1024)(128)(4,1)S(1)}, s32[]{:S(2)}) async-start(s8[7962624]{0:T(1024)(128)(4,1)} %bitcast.45), calls=%async_computation.4 | async-start | bytes 7536640
Sparse Core Ops, SparseCore 0:
  10.5 61.5 all-gather.2
  106.4 75.6 all-gather.4

commit v3 on v2

--- a/solution.py
+++ b/solution.py
@@ -50,7 +50,7 @@
     return value
 
 
-def pool_forward(first, p_ref, b_ref, pre_ref, cell_ref, h_ref, factor_ref, edge_ref, hidden, groups):
+def pool_forward(first, p_ref, b_ref, pre_ref, cell_ref, target, h_ref, factor_ref, edge_ref, hidden, groups):
     lane = lax.broadcasted_iota(jnp.int32, (ROWS, LANES), 1)
 
     def at(j, start=0):
@@ -100,7 +100,7 @@
             cell = cell_ref[rows, at(j, first)] + factor_ref[rows, at(j)] * edge
             cell_ref[rows, at(j, first)] = cell
             outgate = sigmoid(pre_ref[pl.ds(2 * hidden + r, ROWS), at(j, first)].astype(F32))
-            h_ref[rows, at(j, first)] = (outgate * cell).astype(BF16)
+            h_ref[rows, at(j, target)] = (outgate * cell).astype(BF16)
 
     tiles(hidden, ROWS, finish)
 
@@ -178,7 +178,7 @@
         p_ref[:, cols] = dot(w_ref[...], x_ref[cols, :], NT)
 
     tiles(length, 512, strip)
-    pool_forward(0, p_ref, b_ref, pre_ref, cell_ref, h_ref, work_ref, edge_ref, hidden, length // LANES)
+    pool_forward(0, p_ref, b_ref, pre_ref, cell_ref, 0, h_ref, work_ref, edge_ref, hidden, length // LANES)
 
 
 def second_kernel(
@@ -190,7 +190,7 @@
 
     tiles(length, 512, strip)
     groups = length // LANES
-    pool_forward(0, p_ref, b_ref, pre_ref, cell_ref, h_ref, work_ref.at[0], edge_ref.at[0], hidden, groups)
+    pool_forward(0, p_ref, b_ref, pre_ref, cell_ref, 0, h_ref, work_ref.at[0], edge_ref.at[0], hidden, groups)
     pool_backward(0, g_ref, pre_ref, cell_ref, 0, d_ref, db_ref.at[0], work_ref, edge_ref, hidden, groups)
 
 
@@ -307,10 +307,8 @@
     pl.semaphore_signal(sem, inc=1, device_id=target, device_id_type=MESH)
 
 
-def meet(here, everyone):
+def meet(targets):
     barrier = pltpu.get_barrier_semaphore()
-    near = here.peers if everyone else [here.core, here.across_x, here.across_y]
-    targets = near + [here.pair, here.middle]
     for target in targets:
         signal(barrier, target)
     pl.semaphore_wait(barrier, len(targets))
@@ -573,7 +571,8 @@
     for copy in loads[1:]:
         copy.start()
     rhs(1).start()
-    meet(here, second)
+    near = here.peers if second else [here.core, here.across_x, here.across_y]
+    meet(near + [here.pair, here.middle])
     spread = []
     if second:
         spread.append(pltpu.make_async_copy(h_in.at[here.b], h_out.at[here.b], hsem.at[0, 0]))
@@ -728,6 +727,256 @@
     )(*operands)
 
 
+class Gather:
+    def __init__(self, here, own, region, sems):
+        h, b = here, here.b
+        bx, by = h.across_x["tm"], h.across_y["tm"]
+        bd = bx + 4 - 8 * h.y
+        plan = (
+            (own, region(b, None), h.across_x),
+            (own, region(b, None), h.across_y),
+            (own, region(b, None), h.core),
+            (region(bx, 1), region(bx, 1), h.across_y),
+            (region(by, 0), region(by, 0), h.across_x),
+            (region(bx, None), region(bx, None), h.core),
+            (region(by, None), region(by, None), h.core),
+            (region(bd, 0), region(bd, 0), h.core),
+            (region(bd, 1), region(bd, 1), h.core),
+        )
+        self.copies = [remote(src, dst, sems.at[k, 0], sems.at[k, 1], to) for k, (src, dst, to) in enumerate(plan)]
+
+    def start(self):
+        for k in (0, 1, 2):
+            self.copies[k].start()
+
+    def relay(self):
+        self.copies[0].wait_recv()
+        self.copies[3].start()
+        self.copies[1].wait_recv()
+        self.copies[4].start()
+        self.copies[5].start()
+        self.copies[6].start()
+
+    def share(self):
+        self.copies[4].wait_recv()
+        self.copies[7].start()
+        self.copies[3].wait_recv()
+        self.copies[8].start()
+        for k in (2, 5, 6, 7, 8):
+            self.copies[k].wait_recv()
+
+    def drain(self):
+        for copy in self.copies:
+            copy.wait_send()
+
+
+def forward_kernel(seqs, hidden, length, width, *refs):
+    x_in, w1_in, w2_in, seed_in, b1, b2, starts = refs[:7]
+    x_out, h1_out, pre_out, cell_out, h2_out, d_out, db_out = refs[7:14]
+    xg, hg, w, p, pre, cell, work, edge, dv, seed, grad, hv, h2t, xsem, hsem, ssem, lsem = refs[14:]
+    here = Here()
+    groups = length // LANES
+    piece = LANES // 8
+
+    def columns_of(s):
+        return pl.ds(s * length, length)
+
+    def x_region(s):
+        def region(b, half):
+            js = pl.ds(0, groups) if half is None else pl.ds(half * (groups // 2), groups // 2)
+            return xg.at[s, js, b]
+
+        return region
+
+    def h_region(s):
+        def region(b, half):
+            rows = pl.ds(0, hidden) if half is None else pl.ds(half * (hidden // 2), hidden // 2)
+            return hg.at[b, rows, columns_of(s)]
+
+        return region
+
+    def load(src, dst, k):
+        return pltpu.make_async_copy(src, dst, lsem.at[k])
+
+    load_w1 = load(w1_in, w, 0)
+    load_w2 = load(w2_in, w, 0)
+    mine = [load(x_in.at[s], xg.at[s, :, here.b], 1 + s) for s in range(seqs)]
+    store_x = [load(xg.at[s], x_out.at[s], 3 + s) for s in range(seqs)]
+    store_h = [load(hg.at[:, :, columns_of(s)], h1_out.at[:, :, columns_of(s)], 5 + s) for s in range(seqs)]
+    store_p = [load(pre.at[:, columns_of(s)], pre_out.at[:, columns_of(s)], 7 + s) for s in range(seqs)]
+    store_c = [load(cell.at[:, columns_of(s)], cell_out.at[:, columns_of(s)], 9 + s) for s in range(seqs)]
+    store_d = [load(dv.at[s], d_out.at[:, columns_of(s)], 11 + s) for s in range(seqs)]
+    store_o = load(h2t, h2_out, 13)
+
+    load_w1.start()
+    for copy in mine:
+        copy.start()
+    meet(here.peers)
+    xs = [Gather(here, x_in.at[s], x_region(s), xsem.at[s]) for s in range(seqs)]
+    hs = [Gather(here, h_region(s)(here.b, None), h_region(s), hsem.at[s]) for s in range(seqs)]
+
+    late = [
+        (remote(seed_in.at[peer["tm"]], seed.at[:, :, here.b], ssem.at[d, 0], ssem.at[d, 1], peer), peer)
+        for d, peer in enumerate(here.peers, 1)
+    ]
+
+    def first_products(s):
+        for i in range(2):
+            js = pl.ds(i * (groups // 2), groups // 2)
+            rhs = xg[s, js].reshape(length // 2, width)
+            p[:, pl.ds(i * (length // 2), length // 2)] = dot(w[...], rhs, NT)
+
+    def second_products(s):
+        for i in range(2):
+            cols = pl.ds(s * length + i * (length // 2), length // 2)
+            rhs = hg[:, :, cols].reshape(width, length // 2)
+            p[:, pl.ds(i * (length // 2), length // 2)] = dot(w[...], rhs, NN)
+
+    def first_pool(s):
+        first = s * length
+        pool_forward(first, p, b1, pre, cell, first, hg.at[here.b], work.at[0], edge.at[0], hidden, groups)
+
+    def second_pool(s):
+        pool_forward(s * length, p, b2, pre, cell, 0, hv, work.at[0], edge.at[0], hidden, groups)
+        rows = lax.broadcasted_iota(jnp.int32, (LANES, LANES), 0)
+        cols = lax.broadcasted_iota(jnp.int32, (LANES, LANES), 1)
+        eye = (rows == cols).astype(BF16)
+        for j in range(groups):
+            turned = dot(eye, hv[:, pl.ds(j * LANES, LANES)], NT).astype(BF16)
+            at = pl.ds((s * groups + j) * piece, piece)
+            h2t[:, at, :] = turned.reshape(8, piece, hidden)
+
+    def incoming(s):
+        rows = lax.broadcasted_iota(jnp.int32, (hidden, hidden), 0)
+        cols = lax.broadcasted_iota(jnp.int32, (hidden, hidden), 1)
+        eye = (rows == cols).astype(BF16)
+        lane = lax.broadcasted_iota(jnp.int32, (1, LANES), 1)
+        for j in range(groups):
+            block = seed[s, j].reshape(LANES, hidden)
+            turned = dot(eye, block, NT)
+            step = lane * groups + j
+            keep = jnp.zeros((1, LANES), jnp.bool_)
+            for k in range(starts.shape[1]):
+                begin = starts[s, k]
+                keep = jnp.logical_or(keep, jnp.logical_and(step >= begin, step < begin + CLUSTER))
+            keep = jnp.broadcast_to(keep, (hidden, LANES))
+            grad[:, pl.ds(s * length + j * LANES, LANES)] = jnp.where(keep, turned, 0.0).astype(BF16)
+
+    def pool_back(s):
+        pool_backward(s * length, grad, pre, cell, 0, dv.at[s], db_out.at[s], work, edge, hidden, groups)
+        store_d[s].start()
+
+    xs[0].start()
+    seed[:, :, pl.ds(0, 4)] = jnp.zeros((seqs, groups, 4, piece, hidden), BF16)
+    xs[0].relay()
+    xs[1].start()
+    xs[0].share()
+    mine[0].wait()
+    store_x[0].start()
+    load_w1.wait()
+    first_products(0)
+    xs[1].relay()
+    first_pool(0)
+    hs[0].start()
+    store_p[0].start()
+    store_c[0].start()
+    xs[1].share()
+    mine[1].wait()
+    store_x[1].start()
+    first_products(1)
+    load_w2.start()
+    hs[0].relay()
+    first_pool(1)
+    hs[1].start()
+    store_p[1].start()
+    store_c[1].start()
+
+    @pl.when(here.y == 1)
+    def _():
+        pltpu.make_async_copy(seed_in.at[here.b], seed.at[:, :, here.b], ssem.at[0, 0]).start()
+        for copy, _ in late:
+            copy.start()
+
+    hs[0].share()
+    store_h[0].start()
+    load_w2.wait()
+    second_products(0)
+    hs[1].relay()
+    store_p[0].wait()
+    store_c[0].wait()
+    second_pool(0)
+    hs[1].share()
+    store_h[1].start()
+    second_products(1)
+    store_p[1].wait()
+    store_c[1].wait()
+    second_pool(1)
+    store_o.start()
+
+    @pl.when(here.y == 1)
+    def _():
+        pltpu.make_async_copy(seed_in.at[here.b], seed.at[:, :, here.b], ssem.at[0, 0]).wait()
+        for copy, _ in late:
+            copy.wait_send()
+
+    for d, (copy, _) in enumerate(late, 1):
+        source = lax.rem(here.b + 8 - d, 8)
+
+        @pl.when(source >= 4)
+        def _(copy=copy):
+            copy.wait_recv()
+
+    for s in range(seqs):
+        incoming(s)
+        pool_back(s)
+    for gather in xs + hs:
+        gather.drain()
+    for copy in store_x + store_h + store_d + [store_o]:
+        copy.wait()
+
+
+def run_forward(x, w1, b1, w2, b2, seed, starts):
+    seqs, groups, piece, width = x.shape
+    hidden, length = w1.shape[0] // 6, groups * LANES
+    total = seqs * length
+    vmem = pl.BlockSpec(memory_space=pltpu.VMEM)
+    return pl.pallas_call(
+        functools.partial(forward_kernel, seqs, hidden, length, width),
+        name="forward",
+        in_specs=[ANY, ANY, ANY, ANY, vmem, vmem, pl.BlockSpec(memory_space=pltpu.SMEM)],
+        out_specs=[ANY, ANY, ANY, ANY, ANY, ANY, vmem],
+        out_shape=[
+            shape((seqs, groups, 8, piece, width), BF16),
+            shape((8, hidden, total), BF16),
+            shape((3 * hidden, total), BF16),
+            shape((hidden, total), F32),
+            shape((8, seqs * groups * piece, hidden), BF16),
+            shape((6 * hidden, total), BF16),
+            shape((seqs, hidden, 1), F32),
+        ],
+        scratch_shapes=[
+            pltpu.VMEM((seqs, groups, 8, piece, width), BF16),
+            pltpu.VMEM((8, hidden, total), BF16),
+            pltpu.VMEM((6 * hidden, width), BF16),
+            pltpu.VMEM((6 * hidden, length), F32),
+            pltpu.VMEM((3 * hidden, total), BF16),
+            pltpu.VMEM((hidden, total), F32),
+            pltpu.VMEM((2, hidden, length), F32),
+            pltpu.VMEM((2, hidden, LANES), F32),
+            pltpu.VMEM((seqs, 6 * hidden, length), BF16),
+            pltpu.VMEM((seqs, groups, 8, piece, hidden), BF16),
+            pltpu.VMEM((hidden, total), BF16),
+            pltpu.VMEM((hidden, length), BF16),
+            pltpu.VMEM((8, seqs * groups * piece, hidden), BF16),
+            pltpu.SemaphoreType.DMA((seqs, 9, 2)),
+            pltpu.SemaphoreType.DMA((seqs, 9, 2)),
+            pltpu.SemaphoreType.DMA((8, 2)),
+            pltpu.SemaphoreType.DMA((14,)),
+        ],
+        compiler_params=params(collective_id=0, has_side_effects=True),
+    )(x, w1, w2, seed, b1, b2, starts)
+
+
 def per_device(line, inputs, weight_one, fbias_one, weight_two, fbias_two, cotangent, cluster_starts):
     seqs, span, width = inputs.shape
     count = lax.axis_size("tm")
@@ -739,28 +988,29 @@
     w1 = weight_one.reshape(6 * hidden, width)
     w2 = weight_two.reshape(6 * hidden, width)
 
-    steps = lax.axis_index("tm") * span + jnp.arange(span, dtype=jnp.int32)
-    starts = cluster_starts[:, :, None]
-    keep = jnp.any((steps >= starts) & (steps < starts + CLUSTER), axis=1)
-    seed = jnp.where(keep[:, :, None], cotangent, jnp.zeros_like(cotangent))
-    seed = seed.reshape(seqs, piece, groups, count, hidden)
-    seed = lax.all_to_all(seed, "tm", split_axis=3, concat_axis=1, tiled=True)
-    seed = seed.reshape(seqs, LANES, groups, hidden).transpose(3, 0, 2, 1).reshape(hidden, total)
-
     x = inputs.reshape(seqs, piece, groups, width).transpose(0, 2, 1, 3)
-    x = lax.all_gather(x, "tm", axis=2, tiled=True).reshape(total, width)
-    pre1, cell1, h1 = run_first(seqs, w1, fbias_one[:, None], x)
-    h1 = lax.all_gather(h1, "tm", axis=0, tiled=True)
-    h2, d2, db2 = run_second(seqs, w2, fbias_two[:, None], h1, seed)
-
-    h2 = h2.reshape(hidden, seqs, groups, count, piece)
+    bias1, bias2 = fbias_one[:, None], fbias_two[:, None]
+    seed = cotangent.reshape(seqs, piece, groups, count, hidden)
     if line:
-        h2 = h2.transpose(3, 1, 2, 4, 0).reshape(count, seqs * groups * piece, hidden)
+        seed = seed.transpose(3, 0, 2, 1, 4)
+        x, h1, pre1, cell1, h2, d2, db2 = run_forward(x, w1, bias1, w2, bias2, seed, cluster_starts)
+        x, h1 = x.reshape(total, width), h1.reshape(width, total)
         gw2, d1, db1, h2 = run_backward(seqs, d2, h1, w2, (pre1, cell1, h2))
         h2 = h2.reshape(count, seqs, groups, piece, hidden).transpose(1, 3, 2, 0, 4)
         gw1, gx1 = run_backward(seqs, d1, x, w1)
         gx1 = gx1.reshape(seqs, groups, piece, width)
     else:
+        steps = lax.axis_index("tm") * span + jnp.arange(span, dtype=jnp.int32)
+        starts = cluster_starts[:, :, None]
+        keep = jnp.any((steps >= starts) & (steps < starts + CLUSTER), axis=1)
+        seed = jnp.where(keep.reshape(seqs, piece, groups, 1, 1), seed, jnp.zeros_like(seed))
+        seed = lax.all_to_all(seed, "tm", split_axis=3, concat_axis=1, tiled=True)
+        seed = seed.reshape(seqs, LANES, groups, hidden).transpose(3, 0, 2, 1).reshape(hidden, total)
+        x = lax.all_gather(x, "tm", axis=2, tiled=True).reshape(total, width)
+        pre1, cell1, h1 = run_first(seqs, w1, bias1, x)
+        h1 = lax.all_gather(h1, "tm", axis=0, tiled=True)
+        h2, d2, db2 = run_second(seqs, w2, bias2, h1, seed)
+        h2 = h2.reshape(hidden, seqs, groups, count, piece)
         h2 = lax.all_to_all(h2, "tm", split_axis=3, concat_axis=0, tiled=True)
         h2 = h2.reshape(width, seqs, groups, piece).transpose(1, 3, 2, 0)
         gw2 = lax.psum(dot(d2, h1, NT).astype(BF16), "seq")

time: 681 us -> 597 us (0.88)
  waiting for transfers between devices: 124 us -> 0 us
  Pallas kernels: 483 us -> 540 us
  between operations: 14.4 us -> 1.16 us
    all_gather x2 -> x0, waiting for transfers between devices: 93.1 us -> none  [the longest x1 61.5 us: per_device(): x = lax.all_gather(x, 'tm', axis=2, tiled=True).reshape(total, width)]
    pallas_call x2 -> x1, Pallas kernels: 80.8 us -> 135 us  [run_forward(): pl.pallas_call(functools.partial(forward_kernel, seqs, hidden, length, wi...]
    all_to_all x1 -> x0, waiting for transfers between devices: 31.1 us -> none  [per_device(): seed = lax.all_to_all(seed, 'tm', split_axis=3, concat_axis=1, tiled=True)]
  transfers between devices with their start and end apart: 3 -> 0, of which waited for: 3 -> 0; matrix products, arithmetic and copies ran while one was open for 1% -> 0% of each run, Pallas kernels for 0% -> 0%
where the time goes in v3:
time: 597 us; the launch traced here: 590 us
  Pallas kernels  540 us (90%)
  other arithmetic  21.5 us (4%)
  local copies, waits for them, and re-layouts  16.4 us (3%)
  blocking collectives  10.7 us (2%)
    pallas_call x2, Pallas kernels, run_backward(): pl.pallas_call(functools.partial(backward_kernel, second, seqs, hidden, l...  405 us
    pallas_call x1, Pallas kernels, run_forward(): pl.pallas_call(functools.partial(forward_kernel, seqs, hidden, length, wi...  135 us

profile of v3, /device:TPU:0, one launch (start us, length us, event | category | flops | bytes accessed | tf_op | source)
XLA Modules:
  0.0 589.7 jit_solution(3457023152906755587)
XLA Ops:
  0.6 0.0 copy-start.1
  0.6 1.5 broadcast_in_dim.8.refs_4_
  2.2 1.4 broadcast_in_dim.9.refs_5_
  3.6 2.5 copy.26
  6.1 0.0 copy-done.1
  6.1 2.4 reshape.57
  8.5 2.1 copy.24
  10.6 134.5 %forward.1 = (bf16[2,8,8,16,2304]{4,3,2,1,0:T(8,128)(2,1)}, bf16[8,288,2048]{2,1,0:T(8,128)(2,1)}, bf16[864,2048]{1,0:T(8,128)(2,1)}, f32[288,2048]{1,0:T(8,128)...) custom-call(bf16[2,8,16,2304]{3,2,1,0:T(8,128)(2,1)} %bitcast.37, ...), custom_call_target="tpu_custom_call" | custom-call | tf_op jit(solution)/shard_map/forward/pallas_call | solution.py:943
  145.1 206.2 %layer_two_backward.1 = (bf16[6,288,2304]{2,1,0:T(8,128)(2,1)}, bf16[1728,2048]{1,0:T(8,128)(2,1)}, f32[2,288,1]{2,1,0:T(8,128)}, bf16[8,256,288]{2,1,0:T(8,128)(2,1)}) custom-call(bf16[1728,2048]{1,0:T(8,128)(2,1)} %get-tuple-element.19.refs_0_, bf16[2304,2048]{1,0:T(8,128)(2,1)} %bitcast.32, bf16[1728,2304]{1,0:T(8,128)(2,1)} %bitcast.29, ...), custom_call_target="tpu_custom_call" | custom-call | tf_op jit(solution)/shard_map/layer_two_backward/pallas_call | solution.py:719
  351.3 199.3 %layer_one_backward.1 = (bf16[6,288,2304]{2,1,0:T(8,128)(2,1)}, bf16[2,128,2304]{2,1,0:T(8,128)(2,1)}) custom-call(bf16[1728,2048]{1,0:T(8,128)(2,1)} %get-tuple-element.25.refs_0_, bf16[2048,2304]{1,0:T(8,128)(2,1)} %bitcast.33, bf16[1728,2304]{1,0:T(8,128)(2,1)} %bitcast.31), custom_call_target="tpu_custom_call" | custom-call | tf_op jit(solution)/shard_map/layer_one_backward/pallas_call | solution.py:719
  550.7 0.0 copy-start
  550.7 2.4 copy.19
  553.1 0.0 copy-start.3
  553.1 0.0 copy-start.2
  553.1 2.1 reshape.60
  555.2 0.0 copy-done
  555.2 1.4 copy.25
  556.5 0.0 copy-done.3
  556.5 0.2 reduce
  556.7 0.0 copy-done.2
  556.7 0.2 reduce.1
  556.9 10.7 %psum.7 = f32[2,288]{1,0:T(2,128)S(1)} all-reduce(f32[2,288]{1,0:T(2,128)S(1)} %maximum_reduce_fusion), channel_id=1, replica_groups=mesh['seq'=4,'tm'=8] {'seq'}, use_global_device_ids=true, to_apply=%region_1.0 | all-reduce | flops 576 | bytes 4608 | tf_op jit(solution)/shard_map/psum | solution.py:1024
  567.6 0.6 slice_reduce_fusion
  568.2 10.5 %convert.2 = f32[2,3,288,2304]{3,2,1,0:T(8,128)} convert(bf16[2,3,288,2304]{3,2,1,0:T(8,128)(2,1)} %bitcast.35) | non-fusion elementwise | flops 3981312 | bytes 23887872 | tf_op jit(solution)/shard_map/reshape | solution.py:1026
  578.8 10.5 %convert.3 = f32[2,3,288,2304]{3,2,1,0:T(8,128)} convert(bf16[2,3,288,2304]{3,2,1,0:T(8,128)(2,1)} %bitcast.34) | non-fusion elementwise | flops 3981312 | bytes 23887872 | tf_op jit(solution)/shard_map/reshape | solution.py:1026
  (1 shorter events, 0.0 us)
Async XLA Ops:
  0.6 5.5 copy-start.1
  550.7 4.5 copy-start
  553.1 3.4 copy-start.3
  553.1 3.6 copy-start.2

commit v4 on v3

--- a/solution.py
+++ b/solution.py
@@ -105,7 +105,33 @@
     tiles(hidden, ROWS, finish)
 
 
-def pool_backward(first, g_ref, pre_ref, cell_ref, target, d_ref, db_ref, work_ref, edge_ref, hidden, groups):
+def put_gate(d_ref, g, r, j, v, target, lane, hidden, groups):
+    d_ref[pl.ds(g * hidden + r, ROWS), pl.ds(target + j * LANES, LANES)] = v
+    tap = pl.ds((3 + g) * hidden + r, ROWS)
+    if j:
+        d_ref[tap, pl.ds(target + (j - 1) * LANES, LANES)] = v
+    else:
+        moved = shift_lanes(v.astype(F32), -1, lane, 0.0).astype(BF16)
+        d_ref[tap, pl.ds(target + (groups - 1) * LANES, LANES)] = moved
+
+
+def outgate_backward(first, g_ref, pre_ref, cell_ref, d_ref, hidden, groups):
+    lane = lax.broadcasted_iota(jnp.int32, (ROWS, LANES), 1)
+
+    def body(r):
+        rows = pl.ds(r, ROWS)
+        for j in range(groups):
+            at = pl.ds(first + j * LANES, LANES)
+            outgate = sigmoid(pre_ref[pl.ds(2 * hidden + r, ROWS), at].astype(F32))
+            v = g_ref[rows, at].astype(F32) * cell_ref[rows, at] * outgate * (1.0 - outgate)
+            put_gate(d_ref, 2, r, j, v.astype(BF16), 0, lane, hidden, groups)
+
+    tiles(hidden, ROWS, body)
+
+
+def pool_backward(
+    first, g_ref, pre_ref, cell_ref, target, d_ref, db_ref, work_ref, edge_ref, hidden, groups, carried_only=False
+):
     lane = lax.broadcasted_iota(jnp.int32, (ROWS, LANES), 1)
 
     def at(j, start=0):
@@ -148,25 +174,18 @@
             carried = work_ref[0, rows, at(j)] + work_ref[1, rows, at(j)] * edge
             candidate = jnp.tanh(gate(0, r, j))
             forget = sigmoid(gate(1, r, j))
-            outgate = sigmoid(gate(2, r, j))
             cell = cell_ref[rows, at(j, first)]
             keep = carried * (1.0 - forget)
-            got = (
-                keep * (1.0 - candidate * candidate),
-                keep * forget * (before - candidate),
-                g_ref[rows, at(j, first)].astype(F32) * cell * outgate * (1.0 - outgate),
-            )
+            got = [keep * (1.0 - candidate * candidate), keep * forget * (before - candidate)]
+            if not carried_only:
+                outgate = sigmoid(gate(2, r, j))
+                got.append(g_ref[rows, at(j, first)].astype(F32) * cell * outgate * (1.0 - outgate))
             before = cell
             for g, v in enumerate(got):
                 v = v.astype(BF16)
                 if g == 1:
                     total = total + v.astype(F32)
-                d_ref[pl.ds(g * hidden + r, ROWS), at(j, target)] = v
-                tap = pl.ds((3 + g) * hidden + r, ROWS)
-                if j:
-                    d_ref[tap, at(j - 1, target)] = v
-                else:
-                    d_ref[tap, at(groups - 1, target)] = shift_lanes(v.astype(F32), -1, lane, 0.0).astype(BF16)
+                put_gate(d_ref, g, r, j, v, target, lane, hidden, groups)
         db_ref[rows, :] = jnp.sum(total, axis=1, keepdims=True)
 
     tiles(hidden, ROWS, finish)
@@ -268,10 +287,10 @@
     )(grad, pre, cell)
 
 
-UNITS = 18
 THIRDS = 3
-SLOTS = 6
-AHEAD = 4
+PIECES = 3
+SLOTS = 12
+AHEAD = 6
 
 
 class Here:
@@ -286,6 +305,7 @@
         self.across_y = dict(seq=self.z, tm=self.b + 4 - 8 * self.y)
         self.pair = dict(seq=self.z + 1 - 2 * lax.rem(self.z, 2), tm=self.b)
         self.middle = dict(seq=3 - self.z, tm=self.b)
+        self.line = [dict(seq=lax.rem(self.z + d, 4), tm=self.b) for d in range(1, 4)]
         self.peers = [dict(seq=self.z, tm=lax.rem(self.b + d, 8)) for d in range(1, 8)]
         self.is_end = jnp.logical_or(self.z == 0, self.z == 3)
         self.is_centre = jnp.logical_and(self.z > 0, self.z < 3)
@@ -315,35 +335,48 @@
 
 
 class SeqSum:
-    def __init__(self, here, hidden, third, own, ring_in, ring_mid, total, out, sems, credits):
-        self.here, self.hidden, self.third = here, hidden, third
+    def __init__(self, here, gates, hidden, third, own, ring_in, ring_mid, total, out, sems, credits):
+        self.here, self.third, self.rows = here, third, hidden // PIECES
+        self.gates, self.blocks = gates, 2 * gates * THIRDS
+        self.units = self.blocks * PIECES
         self.own, self.ring_in, self.ring_mid, self.total, self.out = own, ring_in, ring_mid, total, out
         self.sems = sems
         self.credit_in, self.credit_mid, self.credit_out = credits
 
+    def rows_of(self, u):
+        return pl.ds(pl.multiple_of(lax.rem(u, PIECES) * self.rows, 16), self.rows)
+
+    def mine(self, u):
+        return self.own.at[u // PIECES, self.rows_of(u)]
+
     def inward(self, u):
         i = lax.rem(u, SLOTS)
-        return remote(self.own.at[u], self.ring_in.at[i], self.sems.at[0, i], self.sems.at[1, i], self.here.pair)
+        return remote(self.mine(u), self.ring_in.at[i], self.sems.at[0, i], self.sems.at[1, i], self.here.pair)
 
     def across(self, u):
         i = lax.rem(u, SLOTS)
-        return remote(self.own.at[u], self.ring_mid.at[i], self.sems.at[2, i], self.sems.at[3, i], self.here.middle)
+        return remote(self.mine(u), self.ring_mid.at[i], self.sems.at[2, i], self.sems.at[3, i], self.here.middle)
 
     def outward(self, u):
         i = lax.rem(u, SLOTS)
         return remote(self.total.at[i], self.ring_in.at[i], self.sems.at[4, i], self.sems.at[5, i], self.here.pair)
 
     def store(self, u, ring):
-        i = lax.rem(u, SLOTS)
-        cols = pl.ds(pl.multiple_of((u // 6) * self.third, LANES), self.third)
-        return pltpu.make_async_copy(ring.at[i], self.out.at[lax.rem(u, 6), :, cols], self.sems.at[6, i])
-
-    def add(self, dst, i, a, ia, b, ib):
+        i, block = lax.rem(u, SLOTS), u // PIECES
+        cols = pl.ds(pl.multiple_of((block // (2 * self.gates)) * self.third, LANES), self.third)
+        to = self.out.at[self.product(block), self.rows_of(u), cols]
+        return pltpu.make_async_copy(ring.at[i], to, self.sems.at[6, i])
+
+    def product(self, block):
+        k = lax.rem(block, 2 * self.gates)
+        return k if self.gates == 3 else (k // 2) * 3 + lax.rem(k, 2)
+
+    def add(self, dst, a, b):
         def rows(r):
             at = pl.ds(r, ROWS)
-            dst[i, at, :] = a[ia, at, :] + b[ib, at, :]
-
-        tiles(self.hidden, ROWS, rows)
+            dst[at, :] = a[at, :] + b[at, :]
+
+        tiles(self.rows, ROWS, rows)
 
     def offer(self, u):
         @pl.when(self.here.is_end)
@@ -358,9 +391,9 @@
     def gather(self, u):
         i = lax.rem(u, SLOTS)
         self.inward(u).wait_recv()
-        self.add(self.own, u, self.own, u, self.ring_in, i)
-
-        @pl.when(u + SLOTS < UNITS)
+        self.add(self.mine(u), self.mine(u), self.ring_in.at[i])
+
+        @pl.when(u + SLOTS < self.units)
         def _():
             signal(self.credit_in, self.here.pair)
 
@@ -381,9 +414,9 @@
             self.outward(u - SLOTS).wait_send()
             self.store(u - SLOTS, self.total).wait()
 
-        self.add(self.total, i, self.own, u, self.ring_mid, i)
-
-        @pl.when(u + SLOTS < UNITS)
+        self.add(self.total.at[i], self.mine(u), self.ring_mid.at[i])
+
+        @pl.when(u + SLOTS < self.units)
         def _():
             signal(self.credit_mid, self.here.middle)
 
@@ -398,22 +431,22 @@
         def _():
             self.store(u - 1, self.ring_in).wait()
 
-            @pl.when(u - 1 + SLOTS < UNITS)
+            @pl.when(u - 1 + SLOTS < self.units)
             def _():
                 signal(self.credit_out, self.here.pair)
 
     def tick(self, n):
         @pl.when(self.here.is_centre)
         def _():
-            @pl.when(n < UNITS)
+            @pl.when(n < self.units)
             def _():
                 self.gather(n)
 
-            @pl.when(both(n >= 1, n <= UNITS))
+            @pl.when(both(n >= 1, n <= self.units))
             def _():
                 self.finish(n - 1)
 
-        @pl.when(n + AHEAD < UNITS)
+        @pl.when(n + AHEAD < self.units)
         def _():
             self.offer(n + AHEAD)
 
@@ -426,16 +459,16 @@
     def drain(self):
         @pl.when(self.here.is_centre)
         def _():
-            for u in range(UNITS - SLOTS, UNITS):
+            for u in range(self.units - SLOTS, self.units):
                 self.across(u).wait_send()
                 self.outward(u).wait_send()
                 self.store(u, self.total).wait()
 
         @pl.when(self.here.is_end)
         def _():
-            for u in range(UNITS - SLOTS, UNITS):
+            for u in range(self.units - SLOTS, self.units):
                 self.inward(u).wait_send()
-            self.store(UNITS - 1, self.ring_in).wait()
+            self.store(self.units - 1, self.ring_in).wait()
 
 
 class RankSum:
@@ -516,10 +549,10 @@
 
 def sum_scratch(seqs, hidden, third, rows, cols):
     return [
-        pltpu.VMEM((UNITS, hidden, third), BF16),
-        pltpu.VMEM((SLOTS, hidden, third), BF16),
-        pltpu.VMEM((SLOTS, hidden, third), BF16),
-        pltpu.VMEM((SLOTS, hidden, third), BF16),
+        pltpu.VMEM((18, hidden, third), BF16),
+        pltpu.VMEM((SLOTS, hidden // PIECES, third), BF16),
+        pltpu.VMEM((SLOTS, hidden // PIECES, third), BF16),
+        pltpu.VMEM((SLOTS, hidden // PIECES, third), BF16),
         pltpu.SemaphoreType.DMA((7, SLOTS)),
         pltpu.SemaphoreType.REGULAR,
         pltpu.SemaphoreType.REGULAR,
@@ -531,26 +564,28 @@
         pltpu.VMEM((seqs, rows // 2, cols), BF16),
         pltpu.VMEM((seqs, rows // 2, cols), BF16),
         pltpu.SemaphoreType.DMA((seqs, 5, 2)),
-        pltpu.SemaphoreType.DMA((8,)),
+        pltpu.SemaphoreType.DMA((17,)),
     ]
 
 
 def backward_kernel(second, seqs, hidden, length, width, *refs):
     third = width // THIRDS
     if second:
-        d_in, r_in, w_in, pre_in, cell_in, h_in, gw_out, d_out, db_out, h_out = refs[:10]
-        dv, wv, rv, pre, cell, work, edge, grad, hsem = refs[10:19]
-        rest = refs[19:]
+        d_in, r_in, w_in, pre_in, cell_in, h_in, sel_in, dsel_in = refs[:8]
+        gw_out, d_out, db_out, h_out, sel_out = refs[8:13]
+        dv, wv, rv, pre, cell, work, edge, grad, picked, dsel, hsem, psem = refs[13:25]
+        rest = refs[25:]
     else:
-        d_in, r_in, w_in, gw_out, gx_out = refs[:5]
-        dv, wv, rv, gxv = refs[5:9]
-        rest = refs[9:]
+        d_in, r_in, w_in, db1_in, db2_in, gw_out, gx_out, db_out = refs[:8]
+        dv, wv, rv, gxv, dbv, dsem = refs[8:14]
+        rest = refs[14:]
     own, ring_in, ring_mid, total, zsem, *credits = rest[:8]
     rank_refs, lsem = rest[8:15], rest[15]
     here = Here()
-    ar = SeqSum(here, hidden, third, own, ring_in, ring_mid, total, gw_out, zsem, credits)
+    gates = 2 if second else 3
+    ar = SeqSum(here, gates, hidden, third, own, ring_in, ring_mid, total, gw_out, zsem, credits)
     rs = RankSum(here, *rank_refs)
-    groups = length // LANES
+    groups, piece = length // LANES, LANES // 8
 
     def columns_of(s):
         return pl.ds(s * length, length)
@@ -571,27 +606,61 @@
     for copy in loads[1:]:
         copy.start()
     rhs(1).start()
-    near = here.peers if second else [here.core, here.across_x, here.across_y]
-    meet(near + [here.pair, here.middle])
-    spread = []
     if second:
-        spread.append(pltpu.make_async_copy(h_in.at[here.b], h_out.at[here.b], hsem.at[0, 0]))
+        meet(here.peers + [here.pair, here.middle])
+        loads.append(pltpu.make_async_copy(dsel_in, dsel, lsem.at[8]))
+        loads[-1].start()
+
+        def halves(start, half):
+            size = hidden if half is None else hidden // 2
+            return pl.ds(start + (half or 0) * size, size)
+
+        gather = Gather(
+            here,
+            lambda b, half: sel_out.at[:, halves(b * hidden, half)],
+            psem,
+            lambda half: sel_in.at[:, halves(0, half)],
+        )
+        keep = pltpu.make_async_copy(sel_in, sel_out.at[:, pl.ds(here.b * hidden, hidden)], lsem.at[9])
+        keep.start()
+        others = [pltpu.make_async_copy(h_in.at[here.b], h_out.at[here.b], hsem.at[0, 0])]
         for d, peer in enumerate(here.peers, 1):
-            spread.append(remote(h_in.at[peer["tm"]], h_out.at[here.b], hsem.at[d, 0], hsem.at[d, 1], peer))
-        for copy in spread:
+            others.append(remote(h_in.at[peer["tm"]], h_out.at[here.b], hsem.at[d, 0], hsem.at[d, 1], peer))
+    else:
+        meet([here.core, here.across_x, here.across_y] + here.line)
+        dbv[here.z] = jnp.zeros((8, hidden), F32)
+        for layer, db in enumerate((db1_in, db2_in)):
+            dbv[here.z, layer : layer + 1, :] = to_row(sum(db[s] for s in range(1, seqs)) + db[0])
+        others = []
+        for d, peer in enumerate(here.line, 1):
+            others.append(remote(dbv.at[here.z], dbv.at[here.z], dsem.at[d, 0], dsem.at[d, 1], peer))
+    if not second:
+        for copy in others:
             copy.start()
 
-    def units(t, ks):
-        for k in ks:
-            rows = pl.ds(k * hidden, hidden)
-            own[t * 6 + k] = dot(dv[rows, :], rv[t % 2], NT if second else NN).astype(BF16)
-            if t * 6 + k < AHEAD:
-                ar.offer(t * 6 + k)
-
-    def part(s, piece):
+    done = [0]
+
+    def units(t, low, high):
+        def unit(k, carry):
+            block = t * (2 * gates) + k
+            rows = pl.ds(pl.multiple_of(ar.product(block) * hidden, 16), hidden)
+            own[block] = dot(dv[rows, :], rv[t % 2], NT if second else NN).astype(BF16)
+            for i in range(PIECES):
+                u = block * PIECES + i
+
+                @pl.when(u < AHEAD)
+                def _(u=u):
+                    ar.offer(u)
+
+            return carry
+
+        lax.fori_loop(low, high, unit, 0)
+        done[0] = (t * 2 * gates + high) * PIECES
+
+    def strips(s, q):
         if second:
-            i, start = piece // 2, piece % 2 * (length // 2)
-            lhs = pl.ds(i * (width // 2), width // 2)
+            i, start = q // 2, lax.rem(q, 2) * (length // 2)
+            lhs = pl.ds(pl.multiple_of(i * (width // 2), LANES), width // 2)
 
             def strip(c):
                 cols = pl.ds(pl.multiple_of(start + c, 256), 256)
@@ -601,60 +670,82 @@
 
             tiles(length // 2, 256, strip)
         else:
-            rows = LANES // 8
-            low, high = (width // 256 * q // 4 * 256 for q in (piece, piece + 1))
-
-            def strip(c):
-                cols = pl.ds(pl.multiple_of(low + c, 256), 256)
+
+            def strip(c, carry):
+                cols = pl.ds(pl.multiple_of(c * 256, 256), 256)
                 got = dot(dv[:, columns_of(s)], wv[:, cols], TN).astype(BF16)
                 for j in range(groups):
-                    block = got[j * LANES : (j + 1) * LANES].reshape(2, 2, 2, rows, 256)
-                    rs.part[:, :, :, pl.ds(j * rows, rows), cols] = block
-
-            tiles(high - low, 256, strip)
-
-    ticks = iter(range(UNITS + 2))
-
-    def tick():
-        ar.tick(next(ticks))
+                    block = got[j * LANES : (j + 1) * LANES].reshape(2, 2, 2, piece, 256)
+                    rs.part[:, :, :, pl.ds(j * piece, piece), cols] = block
+                return carry
+
+            count = width // 256
+            lax.fori_loop(count * q // 4, count * (q + 1) // 4, strip, 0)
+
+    spent = [0]
+
+    def tick(count=1):
+        for _ in range(count):
+            assert spent[0] + AHEAD < min(done[0], ar.units) or done[0] == ar.units
+            ar.tick(spent[0])
+            spent[0] += 1
+
+    def input_grad(s):
+        first = spent[0]
+        assert first + 3 + AHEAD < done[0]
+
+        def quarter(q, carry):
+            strips(s, q)
+            ar.tick(first + q)
+            return carry
+
+        lax.fori_loop(0, 4, quarter, 0)
+        spent[0] += 4
 
     def settle(s):
-        rs.done(s, grad.at[:, columns_of(s)] if second else gxv.at[s])
-
+        if second:
+            rs.done(s, grad.at[:, columns_of(s)])
+        else:
+            rs.done(s, gxv.at[s])
+            gxv[s] = dot(reorder(piece, groups, True), gxv[s], NN).astype(BF16)
+
+    def outgate_load(t):
+        return pltpu.make_async_copy(sel_out.at[:, pl.ds(t * third, third)], picked, lsem.at[10])
+
+    def outgate_store(t, tap):
+        to = gw_out.at[2 + 3 * tap, :, pl.ds(t * third, third)]
+        return pltpu.make_async_copy(own.at[ar.blocks + 2 * t + tap], to, lsem.at[11 + 2 * t + tap])
+
+    count = 2 * gates
     loads[0].wait()
     rhs(0).wait()
-    units(0, range(6))
+    units(0, 0, count)
     rhs(2).start()
     loads[1].wait()
-    part(0, 0)
-    part(0, 1)
-    tick()
-    part(0, 2)
-    part(0, 3)
+    input_grad(0)
     rs.start(0)
     tick()
     rhs(1).wait()
-    units(1, range(3))
+    units(1, 0, 2)
     rs.cross(0)
-    tick()
-    part(1, 0)
-    part(1, 1)
-    part(1, 2)
-    tick()
-    part(1, 3)
+    tick(2)
+    units(1, 2, 4)
+    input_grad(1)
     rs.start(1)
-    units(1, range(3, 6))
-    tick()
+    units(1, 4, count)
     rs.turn(0)
     rhs(2).wait()
-    units(2, range(2))
+    tick(2)
+    units(2, 0, 2)
+    tick()
     rs.cross(1)
-    units(2, range(2, 4))
+    units(2, 2, 4)
     tick()
-    units(2, range(4, 6))
+    units(2, 4, count)
     settle(0)
+    tick(2)
     if second:
-        for copy in loads[2:]:
+        for copy in loads[2:4]:
             copy.wait()
         stores = [
             pltpu.make_async_copy(dv.at[:, columns_of(s)], d_out.at[:, columns_of(s)], lsem.at[6 + s])
@@ -666,16 +757,35 @@
             pool_backward(first, grad, pre, cell, first, dv, db_out.at[s], work, edge, hidden, groups)
             stores[s].start()
 
-        tick()
         pool(0)
-    else:
-        tick()
+    tick()
     rs.turn(1)
-    tick()
-    tick()
+    if second:
+        gather.start()
+    tick(3)
     settle(1)
     if second:
         pool(1)
+        tick(2)
+        gather.relay()
+        for copy in others:
+            copy.start()
+        tick(4)
+        gather.share()
+        keep.wait()
+        outgate_load(0).start()
+        loads[4].wait()
+        tick()
+        for t in range(THIRDS):
+            outgate_load(t).wait()
+            for tap in range(2):
+                own[ar.blocks + 2 * t + tap] = dot(dsel[...], picked[tap], NT).astype(BF16)
+                outgate_store(t, tap).start()
+            if t + 1 < THIRDS:
+                outgate_load(t + 1).start()
+            tick()
+        gather.drain()
+        stores += [outgate_store(t, tap) for t in range(THIRDS) for tap in range(2)]
     else:
         stores = [pltpu.make_async_copy(gxv, gx_out, lsem.at[6])]
         stores[0].start()
@@ -684,22 +794,25 @@
         ar.tick(n)
         return carry
 
-    lax.fori_loop(next(ticks), UNITS + 2, more, 0)
+    lax.fori_loop(spent[0], ar.units + 2, more, 0)
     ar.drain()
-    for copy in stores + spread:
+    for copy in stores + others:
         copy.wait()
-
-
-def run_backward(seqs, d, rhs, weight, layer_one=None):
-    second = layer_one is not None
+    if not second:
+        db_out[...] = dbv[0] + dbv[1] + dbv[2] + dbv[3]
+
+
+def run_backward(seqs, d, rhs, weight, second, more):
     (wide, width), total = weight.shape, d.shape[1]
     hidden, length = wide // 6, total // seqs
     third, span = width // THIRDS, length // 8
     outs = [shape((6, hidden, width), BF16)]
     scratch = [pltpu.VMEM((wide, total), BF16), pltpu.VMEM((wide, width), BF16)]
     if second:
-        outs += [shape((wide, total), BF16), shape((seqs, hidden, 1), F32), shape(layer_one[2].shape, BF16)]
-        specs = [ANY, ANY, pl.BlockSpec(memory_space=pltpu.VMEM), ANY]
+        outs += [shape((wide, total), BF16), shape((seqs, hidden, 1), F32), shape(more[2].shape, BF16)]
+        picked = more[3].shape[2]
+        outs += [shape((2, width, picked), BF16)]
+        specs = [ANY, ANY, pl.BlockSpec(memory_space=pltpu.VMEM), ANY, ANY]
         rows, cols = hidden, length
         scratch += [
             pltpu.VMEM((2, third, total), BF16),
@@ -708,18 +821,26 @@
             pltpu.VMEM((2, hidden, length), F32),
             pltpu.VMEM((2, hidden, LANES), F32),
             pltpu.VMEM((hidden, total), BF16),
+            pltpu.VMEM((2, third, picked), BF16),
+            pltpu.VMEM((hidden, picked), BF16),
             pltpu.SemaphoreType.DMA((8, 2)),
+            pltpu.SemaphoreType.DMA((11, 2)),
         ]
     else:
-        outs += [shape((seqs, span, width), BF16)]
-        specs = [ANY, ANY]
+        outs += [shape((seqs, span, width), BF16), shape((8, hidden), F32)]
+        specs = [ANY, ANY, pl.BlockSpec(memory_space=pltpu.VMEM)]
         rows, cols = span, width
-        scratch += [pltpu.VMEM((2, total, third), BF16), pltpu.VMEM((seqs, span, width), BF16)]
-    operands = (d, rhs, weight) + (layer_one or ())
+        scratch += [
+            pltpu.VMEM((2, total, third), BF16),
+            pltpu.VMEM((seqs, span, width), BF16),
+            pltpu.VMEM((4, 8, hidden), F32),
+            pltpu.SemaphoreType.DMA((4, 2)),
+        ]
+    operands = (d, rhs, weight) + more
     return pl.pallas_call(
         functools.partial(backward_kernel, second, seqs, hidden, length, width),
         name="layer_two_backward" if second else "layer_one_backward",
-        in_specs=[ANY] * len(operands),
+        in_specs=[ANY] * (3 + 5 * second) + [pl.BlockSpec(memory_space=pltpu.VMEM)] * (2 - 2 * second),
         out_specs=specs,
         out_shape=outs,
         scratch_shapes=scratch + sum_scratch(seqs, hidden, third, rows, cols),
@@ -727,42 +848,69 @@
     )(*operands)
 
 
+def reorder(piece, groups, back):
+    span = piece * groups
+    a = lax.broadcasted_iota(jnp.int32, (span, span), 1 if back else 0)
+    b = lax.broadcasted_iota(jnp.int32, (span, span), 0 if back else 1)
+    return (b == lax.rem(a, piece) * groups + a // piece).astype(BF16)
+
+
+def to_row(column):
+    n = column.shape[0]
+    same = lax.broadcasted_iota(jnp.int32, (n, n), 0) == lax.broadcasted_iota(jnp.int32, (n, n), 1)
+    return jnp.sum(jnp.where(same, column, 0.0), axis=0, keepdims=True)
+
+
+def to_column(row):
+    n = row.shape[1]
+    same = lax.broadcasted_iota(jnp.int32, (n, n), 0) == lax.broadcasted_iota(jnp.int32, (n, n), 1)
+    return jnp.sum(jnp.where(same, row, 0.0), axis=1, keepdims=True)
+
+
 class Gather:
-    def __init__(self, here, own, region, sems):
+    def __init__(self, here, region, sems, own=None):
         h, b = here, here.b
+        own = own or (lambda half: region(b, half))
         bx, by = h.across_x["tm"], h.across_y["tm"]
         bd = bx + 4 - 8 * h.y
         plan = (
-            (own, region(b, None), h.across_x),
-            (own, region(b, None), h.across_y),
-            (own, region(b, None), h.core),
-            (region(bx, 1), region(bx, 1), h.across_y),
-            (region(by, 0), region(by, 0), h.across_x),
-            (region(bx, None), region(bx, None), h.core),
-            (region(by, None), region(by, None), h.core),
-            (region(bd, 0), region(bd, 0), h.core),
-            (region(bd, 1), region(bd, 1), h.core),
+            (b, 1, h.across_x),
+            (b, 0, h.across_y),
+            (b, 0, h.across_x),
+            (b, 1, h.across_y),
+            (b, None, h.core),
+            (bx, 1, h.across_y),
+            (by, 0, h.across_x),
+            (bx, None, h.core),
+            (by, None, h.core),
+            (bd, 0, h.core),
+            (bd, 1, h.core),
         )
-        self.copies = [remote(src, dst, sems.at[k, 0], sems.at[k, 1], to) for k, (src, dst, to) in enumerate(plan)]
+        self.copies = []
+        for k, (block, half, to) in enumerate(plan):
+            src = own(half) if k < 5 else region(block, half)
+            self.copies.append(remote(src, region(block, half), sems.at[k, 0], sems.at[k, 1], to))
 
     def start(self):
-        for k in (0, 1, 2):
+        for k in range(5):
             self.copies[k].start()
 
     def relay(self):
         self.copies[0].wait_recv()
-        self.copies[3].start()
+        self.copies[5].start()
         self.copies[1].wait_recv()
-        self.copies[4].start()
-        self.copies[5].start()
         self.copies[6].start()
 
     def share(self):
-        self.copies[4].wait_recv()
+        self.copies[2].wait_recv()
         self.copies[7].start()
         self.copies[3].wait_recv()
         self.copies[8].start()
-        for k in (2, 5, 6, 7, 8):
+        self.copies[6].wait_recv()
+        self.copies[9].start()
+        self.copies[5].wait_recv()
+        self.copies[10].start()
+        for k in (4, 7, 8, 9, 10):
             self.copies[k].wait_recv()
 
     def drain(self):
@@ -771,9 +919,10 @@
 
 
 def forward_kernel(seqs, hidden, length, width, *refs):
-    x_in, w1_in, w2_in, seed_in, b1, b2, starts = refs[:7]
-    x_out, h1_out, pre_out, cell_out, h2_out, d_out, db_out = refs[7:14]
-    xg, hg, w, p, pre, cell, work, edge, dv, seed, grad, hv, h2t, xsem, hsem, ssem, lsem = refs[14:]
+    x_in, w1_in, w2_in, cot_in, b1_in, b2_in, starts = refs[:7]
+    x_out, h1_out, pre_out, cell_out, h2_out, d_out, db_out, sel_out, dsel_out = refs[7:16]
+    xg, hg, w, p, pre, cell, work, edge, dv, seed, grad, hv, h2t, raw, cot, sent, b1, b2, pick, sel, dsel = refs[16:37]
+    xsem, hsem, ssem, zsem, lsem = refs[37:]
     here = Here()
     groups = length // LANES
     piece = LANES // 8
@@ -800,7 +949,8 @@
 
     load_w1 = load(w1_in, w, 0)
     load_w2 = load(w2_in, w, 0)
-    mine = [load(x_in.at[s], xg.at[s, :, here.b], 1 + s) for s in range(seqs)]
+    load_x = [load(x_in.at[s], raw.at[s], 1 + s) for s in range(seqs)]
+    load_c = load(cot_in, cot, 14)
     store_x = [load(xg.at[s], x_out.at[s], 3 + s) for s in range(seqs)]
     store_h = [load(hg.at[:, :, columns_of(s)], h1_out.at[:, :, columns_of(s)], 5 + s) for s in range(seqs)]
     store_p = [load(pre.at[:, columns_of(s)], pre_out.at[:, columns_of(s)], 7 + s) for s in range(seqs)]
@@ -808,29 +958,50 @@
     store_d = [load(dv.at[s], d_out.at[:, columns_of(s)], 11 + s) for s in range(seqs)]
     store_o = load(h2t, h2_out, 13)
 
+    for copy in load_x:
+        copy.start()
     load_w1.start()
-    for copy in mine:
-        copy.start()
-    meet(here.peers)
-    xs = [Gather(here, x_in.at[s], x_region(s), xsem.at[s]) for s in range(seqs)]
-    hs = [Gather(here, h_region(s)(here.b, None), h_region(s), hsem.at[s]) for s in range(seqs)]
+    load_c.start()
+    meet(here.peers + here.line)
+    xs = [Gather(here, x_region(s), xsem.at[s]) for s in range(seqs)]
+    hs = [Gather(here, h_region(s), hsem.at[s]) for s in range(seqs)]
+    order = reorder(piece, groups, False)
+
+    def place(s):
+        load_x[s].wait()
+        xg[s, :, here.b] = dot(order, raw[s], NN).astype(BF16).reshape(groups, piece, width)
+        xs[s].start()
+
+    def prepare():
+        load_c.wait()
+        for s in range(seqs):
+            turned = dot(order, cot[s], NN).astype(BF16)
+            for b in range(8):
+                block = turned[:, b * hidden : (b + 1) * hidden]
+                sent[b, s] = block.reshape(groups, piece, hidden)
+        seed[:, :, pl.ds(0, 4)] = jnp.zeros((seqs, groups, 4, piece, hidden), BF16)
+        for s in range(seqs):
+            prepare_pick(s)
+        b1[...] = to_column(b1_in[...])
+        b2[...] = to_column(b2_in[...])
 
     late = [
-        (remote(seed_in.at[peer["tm"]], seed.at[:, :, here.b], ssem.at[d, 0], ssem.at[d, 1], peer), peer)
+        (remote(sent.at[peer["tm"]], seed.at[:, :, here.b], ssem.at[d, 0], ssem.at[d, 1], peer), peer)
         for d, peer in enumerate(here.peers, 1)
     ]
 
+    def products(rhs, dims):
+        def block(r):
+            rows = pl.ds(r, hidden)
+            p[rows, :] = dot(w[rows, :], rhs(), dims)
+
+        tiles(6 * hidden, hidden, block)
+
     def first_products(s):
-        for i in range(2):
-            js = pl.ds(i * (groups // 2), groups // 2)
-            rhs = xg[s, js].reshape(length // 2, width)
-            p[:, pl.ds(i * (length // 2), length // 2)] = dot(w[...], rhs, NT)
+        products(lambda: xg[s].reshape(length, width), NT)
 
     def second_products(s):
-        for i in range(2):
-            cols = pl.ds(s * length + i * (length // 2), length // 2)
-            rhs = hg[:, :, cols].reshape(width, length // 2)
-            p[:, pl.ds(i * (length // 2), length // 2)] = dot(w[...], rhs, NN)
+        products(lambda: hg[:, :, columns_of(s)].reshape(width, length), NN)
 
     def first_pool(s):
         first = s * length
@@ -863,15 +1034,58 @@
             grad[:, pl.ds(s * length + j * LANES, LANES)] = jnp.where(keep, turned, 0.0).astype(BF16)
 
     def pool_back(s):
-        pool_backward(s * length, grad, pre, cell, 0, dv.at[s], db_out.at[s], work, edge, hidden, groups)
+        pool_backward(s * length, grad, pre, cell, 0, dv.at[s], db_out.at[s], work, edge, hidden, groups, True)
         store_d[s].start()
 
-    xs[0].start()
-    seed[:, :, pl.ds(0, 4)] = jnp.zeros((seqs, groups, 4, piece, hidden), BF16)
+    def cluster_steps(s):
+        lane = lax.broadcasted_iota(jnp.int32, (1, LANES), 1)
+        step = lax.rem(lane, CLUSTER)
+        for k in range(starts.shape[1]):
+            step = step + jnp.where(lane // CLUSTER == k, starts[s, k], 0)
+        return lane, step
+
+    def prepare_pick(s):
+        _, step = cluster_steps(s)
+        for j in range(groups):
+            code = lax.broadcasted_iota(jnp.int32, (LANES, LANES), 0) * groups + j
+            at = pl.ds(j * LANES, LANES)
+            pick[s, at, pl.ds(0, LANES)] = (code == step).astype(BF16)
+            pick[s, at, pl.ds(LANES, LANES)] = (code == step - 1).astype(BF16)
+
+    def held(s, count):
+        start = here.z * (seqs * LANES) + s * LANES
+        return pl.ds(pl.multiple_of(start, LANES), count * LANES)
+
+    def pick_hidden(s):
+        got = dot(hg[here.b, :, columns_of(s)], pick[s], NN).astype(BF16)
+        for tap in range(2):
+            sel[tap, :, held(s, 1)] = got[:, tap * LANES : (tap + 1) * LANES]
+
+    def pick_grad(s):
+        lane, step = cluster_steps(s)
+        again = jnp.zeros((1, LANES), jnp.bool_)
+        for k in range(starts.shape[1] - 1):
+            begin = starts[s, k]
+            inside = jnp.logical_and(step >= begin, step < begin + CLUSTER)
+            again = jnp.logical_or(again, jnp.logical_and(inside, lane // CLUSTER > k))
+        got = dot(dv[s, pl.ds(2 * hidden, hidden), :], pick[s, :, pl.ds(0, LANES)], NN)
+        dsel[:, held(s, 1)] = jnp.where(jnp.broadcast_to(again, (hidden, LANES)), 0.0, got).astype(BF16)
+
+    spread_h = []
+    spread_d = []
+    for d, peer in enumerate(here.line, 1):
+        at = sel.at[:, :, held(0, seqs)]
+        spread_h.append(remote(at, at, zsem.at[d, 0], zsem.at[d, 1], peer))
+        at = dsel.at[:, held(0, seqs)]
+        spread_d.append(remote(at, at, zsem.at[d, 2], zsem.at[d, 3], peer))
+    store_s = load(sel, sel_out, 15)
+    store_e = load(dsel, dsel_out, 16)
+
+    place(0)
+    prepare()
     xs[0].relay()
-    xs[1].start()
+    place(1)
     xs[0].share()
-    mine[0].wait()
     store_x[0].start()
     load_w1.wait()
     first_products(0)
@@ -881,7 +1095,6 @@
     store_p[0].start()
     store_c[0].start()
     xs[1].share()
-    mine[1].wait()
     store_x[1].start()
     first_products(1)
     load_w2.start()
@@ -891,17 +1104,22 @@
     store_p[1].start()
     store_c[1].start()
 
-    @pl.when(here.y == 1)
-    def _():
-        pltpu.make_async_copy(seed_in.at[here.b], seed.at[:, :, here.b], ssem.at[0, 0]).start()
-        for copy, _ in late:
-            copy.start()
-
+    for s in range(seqs):
+        pick_hidden(s)
+    for copy in spread_h:
+        copy.start()
     hs[0].share()
     store_h[0].start()
     load_w2.wait()
     second_products(0)
     hs[1].relay()
+
+    @pl.when(here.y == 1)
+    def _():
+        pltpu.make_async_copy(sent.at[here.b], seed.at[:, :, here.b], ssem.at[0, 0]).start()
+        for copy, _ in late:
+            copy.start()
+
     store_p[0].wait()
     store_c[0].wait()
     second_pool(0)
@@ -915,7 +1133,7 @@
 
     @pl.when(here.y == 1)
     def _():
-        pltpu.make_async_copy(seed_in.at[here.b], seed.at[:, :, here.b], ssem.at[0, 0]).wait()
+        pltpu.make_async_copy(sent.at[here.b], seed.at[:, :, here.b], ssem.at[0, 0]).wait()
         for copy, _ in late:
             copy.wait_send()
 
@@ -928,23 +1146,36 @@
 
     for s in range(seqs):
         incoming(s)
+        outgate_backward(s * length, grad, pre, cell, dv.at[s], hidden, groups)
+        pick_grad(s)
+    for copy in spread_d:
+        copy.start()
+    for copy in spread_h:
+        copy.wait()
+    store_s.start()
+    for s in range(seqs):
         pool_back(s)
     for gather in xs + hs:
         gather.drain()
-    for copy in store_x + store_h + store_d + [store_o]:
+    for copy in spread_d:
         copy.wait()
-
-
-def run_forward(x, w1, b1, w2, b2, seed, starts):
-    seqs, groups, piece, width = x.shape
-    hidden, length = w1.shape[0] // 6, groups * LANES
-    total = seqs * length
+    store_e.start()
+    for copy in store_x + store_h + store_d + [store_o, store_s, store_e]:
+        copy.wait()
+
+
+def run_forward(x, w1, b1, w2, b2, cotangent, starts):
+    seqs, span, width = x.shape
+    hidden, length, piece = w1.shape[0] // 6, span * 8, LANES // 8
+    groups = length // LANES
+    total, picked = seqs * length, 4 * seqs * LANES
+    assert starts.shape[1] * CLUSTER == LANES
     vmem = pl.BlockSpec(memory_space=pltpu.VMEM)
     return pl.pallas_call(
         functools.partial(forward_kernel, seqs, hidden, length, width),
         name="forward",
         in_specs=[ANY, ANY, ANY, ANY, vmem, vmem, pl.BlockSpec(memory_space=pltpu.SMEM)],
-        out_specs=[ANY, ANY, ANY, ANY, ANY, ANY, vmem],
+        out_specs=[ANY, ANY, ANY, ANY, ANY, ANY, vmem, ANY, ANY],
         out_shape=[
             shape((seqs, groups, 8, piece, width), BF16),
             shape((8, hidden, total), BF16),
@@ -953,6 +1184,8 @@
             shape((8, seqs * groups * piece, hidden), BF16),
             shape((6 * hidden, total), BF16),
             shape((seqs, hidden, 1), F32),
+            shape((2, hidden, picked), BF16),
+            shape((hidden, picked), BF16),
         ],
         scratch_shapes=[
             pltpu.VMEM((seqs, groups, 8, piece, width), BF16),
@@ -968,13 +1201,22 @@
             pltpu.VMEM((hidden, total), BF16),
             pltpu.VMEM((hidden, length), BF16),
             pltpu.VMEM((8, seqs * groups * piece, hidden), BF16),
-            pltpu.SemaphoreType.DMA((seqs, 9, 2)),
-            pltpu.SemaphoreType.DMA((seqs, 9, 2)),
+            pltpu.VMEM((seqs, span, width), BF16),
+            pltpu.VMEM((seqs, span, width), BF16),
+            pltpu.VMEM((8, seqs, groups, piece, hidden), BF16),
+            pltpu.VMEM((hidden, 1), F32),
+            pltpu.VMEM((hidden, 1), F32),
+            pltpu.VMEM((seqs, length, 2 * LANES), BF16),
+            pltpu.VMEM((2, hidden, picked), BF16),
+            pltpu.VMEM((hidden, picked), BF16),
+            pltpu.SemaphoreType.DMA((seqs, 11, 2)),
+            pltpu.SemaphoreType.DMA((seqs, 11, 2)),
             pltpu.SemaphoreType.DMA((8, 2)),
-            pltpu.SemaphoreType.DMA((14,)),
+            pltpu.SemaphoreType.DMA((4, 4)),
+            pltpu.SemaphoreType.DMA((17,)),
         ],
         compiler_params=params(collective_id=0, has_side_effects=True),
-    )(x, w1, w2, seed, b1, b2, starts)
+    )(x, w1, w2, cotangent, b1, b2, starts)
 
 
 def per_device(line, inputs, weight_one, fbias_one, weight_two, fbias_two, cotangent, cluster_starts):
@@ -988,18 +1230,18 @@
     w1 = weight_one.reshape(6 * hidden, width)
     w2 = weight_two.reshape(6 * hidden, width)
 
-    x = inputs.reshape(seqs, piece, groups, width).transpose(0, 2, 1, 3)
-    bias1, bias2 = fbias_one[:, None], fbias_two[:, None]
-    seed = cotangent.reshape(seqs, piece, groups, count, hidden)
     if line:
-        seed = seed.transpose(3, 0, 2, 1, 4)
-        x, h1, pre1, cell1, h2, d2, db2 = run_forward(x, w1, bias1, w2, bias2, seed, cluster_starts)
+        x, h1, pre1, cell1, h2, d2, db2, *picked = run_forward(
+            inputs, w1, fbias_one[None], w2, fbias_two[None], cotangent, cluster_starts
+        )
         x, h1 = x.reshape(total, width), h1.reshape(width, total)
-        gw2, d1, db1, h2 = run_backward(seqs, d2, h1, w2, (pre1, cell1, h2))
+        gw2, d1, db1, h2, _ = run_backward(seqs, d2, h1, w2, True, (pre1, cell1, h2, *picked))
         h2 = h2.reshape(count, seqs, groups, piece, hidden).transpose(1, 3, 2, 0, 4)
-        gw1, gx1 = run_backward(seqs, d1, x, w1)
-        gx1 = gx1.reshape(seqs, groups, piece, width)
+        gw1, gx1, db = run_backward(seqs, d1, x, w1, False, (db1, db2))
     else:
+        x = inputs.reshape(seqs, piece, groups, width).transpose(0, 2, 1, 3)
+        bias1, bias2 = fbias_one[:, None], fbias_two[:, None]
+        seed = cotangent.reshape(seqs, piece, groups, count, hidden)
         steps = lax.axis_index("tm") * span + jnp.arange(span, dtype=jnp.int32)
         starts = cluster_starts[:, :, None]
         keep = jnp.any((steps >= starts) & (steps < starts + CLUSTER), axis=1)
@@ -1019,9 +1261,9 @@
         gw1 = lax.psum(dot(d1, x, NN).astype(BF16), "seq")
         gx1 = dot(d1, w1, TN).astype(BF16).reshape(seqs, groups, LANES, width)
         gx1 = lax.psum_scatter(gx1, "tm", scatter_dimension=2, tiled=True)
+        gx1 = gx1.transpose(0, 2, 1, 3).reshape(seqs, span, width)
+        db = lax.psum(jnp.stack([db1, db2]).sum(axis=(1, 3)), "seq")
     out = h2.reshape(seqs, span, width)
-    gx1 = gx1.transpose(0, 2, 1, 3).reshape(seqs, span, width)
-    db = lax.psum(jnp.stack([db1, db2]).sum(axis=(1, 3)), "seq")
     dims = weight_one.shape
     return (out, gx1, gw1.astype(F32).reshape(dims), db[0], gw2.astype(F32).reshape(dims), db[1])
 

time: 597 us -> 539 us (0.903)
  Pallas kernels: 540 us -> 502 us
  blocking collectives: 10.7 us -> 0 us
  local copies, waits for them, and re-layouts: 16.4 us -> 9.27 us
    pallas_call x2, Pallas kernels: 405 us -> 374 us  [run_backward(): pl.pallas_call(functools.partial(backward_kernel, second, seqs, hidden, l...]
    psum x1 -> x0, blocking collectives: 10.7 us -> none  [per_device(): db = lax.psum(jnp.stack([db1, db2]).sum(axis=(1, 3)), 'seq')]
    reshape x3 -> x0, local copies, waits for them, and re-layouts: 6.96 us -> none  [the longest x2 4.49 us: per_device(): seed = cotangent.reshape(seqs, piece, groups, count, hidden)]
    pallas_call x1, Pallas kernels: 135 us -> 128 us  [run_forward(): pl.pallas_call(functools.partial(forward_kernel, seqs, hidden, length, wi...]
where the time goes in v4:
time: 539 us; the launch traced here: 534 us
  Pallas kernels  502 us (93%)
  other arithmetic  21.2 us (4%)
  local copies, waits for them, and re-layouts  9.27 us (2%)
    pallas_call x2, Pallas kernels, run_backward(): pl.pallas_call(functools.partial(backward_kernel, second, seqs, hidden, l...  374 us
    pallas_call x1, Pallas kernels, run_forward(): pl.pallas_call(functools.partial(forward_kernel, seqs, hidden, length, wi...  128 us

profile of v4, /device:TPU:0, one launch (start us, length us, event | category | flops | bytes accessed | tf_op | source)
XLA Modules:
  0.0 533.9 jit_solution(8439574290676084640)
XLA Ops:
  0.6 1.2 broadcast_in_dim.6.refs_4_
  1.9 1.2 broadcast_in_dim.7.refs_5_
  3.1 127.9 %forward.1 = (bf16[2,8,8,16,2304]{4,3,2,1,0:T(8,128)(2,1)}, bf16[8,288,2048]{2,1,0:T(8,128)(2,1)}, bf16[864,2048]{1,0:T(8,128)(2,1)}, f32[288,2048]{1,0:T(8,128)...) custom-call(bf16[2,128,2304]{2,1,0:T(8,128)(2,1)} %refs_0_.1, ...), custom_call_target="tpu_custom_call" | custom-call | tf_op jit(solution)/shard_map/forward/pallas_call | solution.py:1174
  131.1 166.5 %layer_two_backward.1 = (bf16[6,288,2304]{2,1,0:T(8,128)(2,1)}, bf16[1728,2048]{1,0:T(8,128)(2,1)}, f32[2,288,1]{2,1,0:T(8,128)}, bf16[8,256,288]{2,1,0:T(8,128)(2,1)}, bf16[2,2304,1024]{2,1,0:T(8,128)(2,1)}) custom-call(bf16[1728,2048]{1,0:T(8,128)(2,1)} %get-tuple-element.22.refs_0_, bf16[2304,2048]{1,0:T(8,128)(2,1)} %bitcast.17, ...), custom_call_target="tpu_custom_call" | custom-call | tf_op jit(solution)/shard_map/layer_two_backward/pallas_call | solution.py:840
  297.6 207.9 %layer_one_backward.1 = (bf16[6,288,2304]{2,1,0:T(8,128)(2,1)}, bf16[2,128,2304]{2,1,0:T(8,128)(2,1)}, f32[8,288]{1,0:T(8,128)}) custom-call(bf16[1728,2048]{1,0:T(8,128)(2,1)} %get-tuple-element.30.refs_0_, bf16[2048,2304]{1,0:T(8,128)(2,1)} %bitcast.18, bf16[1728,2304]{1,0:T(8,128)(2,1)} %bitcast.16, f32[2,288,1]{2,1,0:T(8,128)} %get-tuple-element.32.refs_3_, ...), custom_call_target="tpu_custom_call" | custom-call | tf_op jit(solution)/shard_map/layer_one_backward/pallas_call | solution.py:840
  505.5 2.3 copy.13
  507.8 2.1 reshape.46
  509.9 1.4 slice_reduce_fusion
  511.2 10.5 %convert.2 = f32[2,3,288,2304]{3,2,1,0:T(8,128)} convert(bf16[2,3,288,2304]{3,2,1,0:T(8,128)(2,1)} %bitcast.20) | non-fusion elementwise | flops 3981312 | bytes 23887872 | tf_op jit(solution)/shard_map/reshape | solution.py:1268
  521.8 0.0 copy-start
  521.8 10.6 %convert.3 = f32[2,3,288,2304]{3,2,1,0:T(8,128)} convert(bf16[2,3,288,2304]{3,2,1,0:T(8,128)(2,1)} %bitcast.19) | non-fusion elementwise | flops 3981312 | bytes 23887872 | tf_op jit(solution)/shard_map/reshape | solution.py:1268
  532.4 0.0 copy-done
  532.4 1.0 copy.15
Async XLA Ops:
  521.8 10.6 %copy-start = (bf16[2,128,2304]{2,1,0:T(8,128)(2,1)S(1)}, bf16[2,128,2304]{2,1,0:T(8,128)(2,1)}, u32[]{:S(2)}) copy-start(bf16[2,128,2304]{2,1,0:T(8,128)(2,1)} %get-tuple-element.47) | copy-start | bytes 3538948

commit v5 on v4

--- a/solution.py
+++ b/solution.py
@@ -291,6 +291,7 @@
 PIECES = 3
 SLOTS = 12
 AHEAD = 6
+BEHIND = 2
 
 
 class Here:
@@ -442,19 +443,19 @@
             def _():
                 self.gather(n)
 
-            @pl.when(both(n >= 1, n <= self.units))
+            @pl.when(both(n >= BEHIND, n < self.units + BEHIND))
             def _():
-                self.finish(n - 1)
+                self.finish(n - BEHIND)
 
         @pl.when(n + AHEAD < self.units)
         def _():
             self.offer(n + AHEAD)
 
-        @pl.when(n >= 2)
+        @pl.when(n >= BEHIND + 2)
         def _():
             @pl.when(self.here.is_end)
             def _():
-                self.accept(n - 2)
+                self.accept(n - BEHIND - 2)
 
     def drain(self):
         @pl.when(self.here.is_centre)
@@ -571,14 +572,14 @@
 def backward_kernel(second, seqs, hidden, length, width, *refs):
     third = width // THIRDS
     if second:
-        d_in, r_in, w_in, pre_in, cell_in, h_in, sel_in, dsel_in = refs[:8]
-        gw_out, d_out, db_out, h_out, sel_out = refs[8:13]
-        dv, wv, rv, pre, cell, work, edge, grad, picked, dsel, hsem, psem = refs[13:25]
-        rest = refs[25:]
+        d_in, r_in, w_in, pre_in, cell_in, gw_out, d_out, db_out = refs[:8]
+        dv, wv, rv, pre, cell, work, edge, grad = refs[8:16]
+        rest = refs[16:]
     else:
-        d_in, r_in, w_in, db1_in, db2_in, gw_out, gx_out, db_out = refs[:8]
-        dv, wv, rv, gxv, dbv, dsem = refs[8:14]
-        rest = refs[14:]
+        d_in, r_in, w_in, h_in, sel_in, dsel_in, db1_in, db2_in = refs[:8]
+        gw_out, gx_out, h_out, sel_out, wo_out, db_out = refs[8:14]
+        dv, wv, rv, gxv, picked, dsel, wo, heard, hv, dbv, dsem, hsem, psem = refs[14:27]
+        rest = refs[27:]
     own, ring_in, ring_mid, total, zsem, *credits = rest[:8]
     rank_refs, lsem = rest[8:15], rest[15]
     here = Here()
@@ -607,9 +608,11 @@
         copy.start()
     rhs(1).start()
     if second:
-        meet(here.peers + [here.pair, here.middle])
-        loads.append(pltpu.make_async_copy(dsel_in, dsel, lsem.at[8]))
-        loads[-1].start()
+        meet([here.core, here.across_x, here.across_y, here.pair, here.middle])
+    else:
+        meet(here.peers + here.line)
+        load_e = pltpu.make_async_copy(dsel_in, dsel, lsem.at[8])
+        load_e.start()
 
         def halves(start, half):
             size = hidden if half is None else hidden // 2
@@ -621,22 +624,20 @@
             psem,
             lambda half: sel_in.at[:, halves(0, half)],
         )
+        gather.start()
         keep = pltpu.make_async_copy(sel_in, sel_out.at[:, pl.ds(here.b * hidden, hidden)], lsem.at[9])
         keep.start()
-        others = [pltpu.make_async_copy(h_in.at[here.b], h_out.at[here.b], hsem.at[0, 0])]
-        for d, peer in enumerate(here.peers, 1):
-            others.append(remote(h_in.at[peer["tm"]], h_out.at[here.b], hsem.at[d, 0], hsem.at[d, 1], peer))
-    else:
-        meet([here.core, here.across_x, here.across_y] + here.line)
         dbv[here.z] = jnp.zeros((8, hidden), F32)
         for layer, db in enumerate((db1_in, db2_in)):
             dbv[here.z, layer : layer + 1, :] = to_row(sum(db[s] for s in range(1, seqs)) + db[0])
-        others = []
+        biases = []
         for d, peer in enumerate(here.line, 1):
-            others.append(remote(dbv.at[here.z], dbv.at[here.z], dsem.at[d, 0], dsem.at[d, 1], peer))
-    if not second:
-        for copy in others:
+            biases.append(remote(dbv.at[here.z], dbv.at[here.z], dsem.at[d, 0], dsem.at[d, 1], peer))
+        for copy in biases:
             copy.start()
+        spread = [pltpu.make_async_copy(h_in.at[here.b], heard.at[here.b], hsem.at[0, 0])]
+        for d, peer in enumerate(here.peers, 1):
+            spread.append(remote(h_in.at[peer["tm"]], heard.at[here.b], hsem.at[d, 0], hsem.at[d, 1], peer))
 
     done = [0]
 
@@ -713,8 +714,17 @@
         return pltpu.make_async_copy(sel_out.at[:, pl.ds(t * third, third)], picked, lsem.at[10])
 
     def outgate_store(t, tap):
-        to = gw_out.at[2 + 3 * tap, :, pl.ds(t * third, third)]
-        return pltpu.make_async_copy(own.at[ar.blocks + 2 * t + tap], to, lsem.at[11 + 2 * t + tap])
+        return pltpu.make_async_copy(wo.at[tap], wo_out.at[tap, :, pl.ds(t * third, third)], lsem.at[11 + tap])
+
+    def outgate(t):
+        outgate_load(t).wait()
+        for tap in range(2):
+            if t:
+                outgate_store(t - 1, tap).wait()
+            wo[tap] = dot(dsel[...], picked[tap], NT).astype(BF16)
+            outgate_store(t, tap).start()
+        if t + 1 < THIRDS:
+            outgate_load(t + 1).start()
 
     count = 2 * gates
     loads[0].wait()
@@ -724,27 +734,25 @@
     loads[1].wait()
     input_grad(0)
     rs.start(0)
-    tick()
-    rhs(1).wait()
-    units(1, 0, 2)
-    rs.cross(0)
-    tick(2)
-    units(1, 2, 4)
-    input_grad(1)
-    rs.start(1)
-    units(1, 4, count)
-    rs.turn(0)
-    rhs(2).wait()
-    tick(2)
-    units(2, 0, 2)
-    tick()
-    rs.cross(1)
-    units(2, 2, 4)
-    tick()
-    units(2, 4, count)
-    settle(0)
-    tick(2)
     if second:
+        tick()
+        rhs(1).wait()
+        units(1, 0, 2)
+        rs.cross(0)
+        tick(2)
+        units(1, 2, 4)
+        input_grad(1)
+        rs.start(1)
+        rs.turn(0)
+        rhs(2).wait()
+        tick(2)
+        units(2, 0, 2)
+        tick()
+        rs.cross(1)
+        units(2, 2, 4)
+        tick(2)
+        settle(0)
+        tick(2)
         for copy in loads[2:4]:
             copy.wait()
         stores = [
@@ -758,47 +766,74 @@
             stores[s].start()
 
         pool(0)
-    tick()
-    rs.turn(1)
-    if second:
-        gather.start()
-    tick(3)
-    settle(1)
-    if second:
+        tick()
+        rs.turn(1)
+        tick(3)
+        settle(1)
         pool(1)
+    else:
+        gather.relay()
+        rhs(1).wait()
+        units(1, 0, 2)
+        tick()
+        units(1, 2, 4)
+        tick()
+        rs.cross(0)
+        tick()
+        input_grad(1)
+        rs.start(1)
+        units(1, 4, 6)
         tick(2)
-        gather.relay()
-        for copy in others:
+        gather.share()
+        rhs(2).wait()
+        units(2, 0, 2)
+        tick()
+        rs.cross(1)
+        tick()
+        rs.turn(0)
+        tick()
+        units(2, 2, 4)
+        tick()
+        units(2, 4, 6)
+        tick(6)
+        settle(0)
+        rs.turn(1)
+        keep.wait()
+        load_e.wait()
+        outgate_load(0).start()
+        tick(2)
+        for copy in spread:
             copy.start()
         tick(4)
-        gather.share()
-        keep.wait()
-        outgate_load(0).start()
-        loads[4].wait()
-        tick()
-        for t in range(THIRDS):
-            outgate_load(t).wait()
-            for tap in range(2):
-                own[ar.blocks + 2 * t + tap] = dot(dsel[...], picked[tap], NT).astype(BF16)
-                outgate_store(t, tap).start()
-            if t + 1 < THIRDS:
-                outgate_load(t + 1).start()
-            tick()
-        gather.drain()
-        stores += [outgate_store(t, tap) for t in range(THIRDS) for tap in range(2)]
-    else:
+        settle(1)
         stores = [pltpu.make_async_copy(gxv, gx_out, lsem.at[6])]
         stores[0].start()
+        for t in range(THIRDS):
+            tick(2)
+            outgate(t)
+        for copy in spread:
+            copy.wait()
+        back = reorder(piece, groups, True)
+        for s in range(seqs):
+            for b in range(8):
+                block = heard[b, pl.ds(s * LANES, LANES), :]
+                hv[s, :, b * hidden : (b + 1) * hidden] = dot(back, block, NN).astype(BF16)
+        stores += [outgate_store(THIRDS - 1, tap) for tap in range(2)]
+        stores.append(pltpu.make_async_copy(hv, h_out, lsem.at[13]))
+        stores[-1].start()
 
     def more(n, carry):
         ar.tick(n)
         return carry
 
-    lax.fori_loop(spent[0], ar.units + 2, more, 0)
+    lax.fori_loop(spent[0], ar.units + BEHIND + 2, more, 0)
     ar.drain()
-    for copy in stores + others:
+    for copy in stores:
         copy.wait()
     if not second:
+        gather.drain()
+        for copy in biases:
+            copy.wait()
         db_out[...] = dbv[0] + dbv[1] + dbv[2] + dbv[3]
 
 
@@ -808,11 +843,9 @@
     third, span = width // THIRDS, length // 8
     outs = [shape((6, hidden, width), BF16)]
     scratch = [pltpu.VMEM((wide, total), BF16), pltpu.VMEM((wide, width), BF16)]
+    vmem = pl.BlockSpec(memory_space=pltpu.VMEM)
     if second:
-        outs += [shape((wide, total), BF16), shape((seqs, hidden, 1), F32), shape(more[2].shape, BF16)]
-        picked = more[3].shape[2]
-        outs += [shape((2, width, picked), BF16)]
-        specs = [ANY, ANY, pl.BlockSpec(memory_space=pltpu.VMEM), ANY, ANY]
+        outs += [shape((wide, total), BF16), shape((seqs, hidden, 1), F32)]
         rows, cols = hidden, length
         scratch += [
             pltpu.VMEM((2, third, total), BF16),
@@ -821,27 +854,36 @@
             pltpu.VMEM((2, hidden, length), F32),
             pltpu.VMEM((2, hidden, LANES), F32),
             pltpu.VMEM((hidden, total), BF16),
-            pltpu.VMEM((2, third, picked), BF16),
-            pltpu.VMEM((hidden, picked), BF16),
-            pltpu.SemaphoreType.DMA((8, 2)),
-            pltpu.SemaphoreType.DMA((11, 2)),
         ]
     else:
-        outs += [shape((seqs, span, width), BF16), shape((8, hidden), F32)]
-        specs = [ANY, ANY, pl.BlockSpec(memory_space=pltpu.VMEM)]
+        picked = more[2].shape[1]
+        outs += [
+            shape((seqs, span, width), BF16),
+            shape((seqs, span, width), BF16),
+            shape((2, width, picked), BF16),
+            shape((2, hidden, width), BF16),
+            shape((8, hidden), F32),
+        ]
         rows, cols = span, width
         scratch += [
             pltpu.VMEM((2, total, third), BF16),
             pltpu.VMEM((seqs, span, width), BF16),
+            pltpu.VMEM((2, third, picked), BF16),
+            pltpu.VMEM((hidden, picked), BF16),
+            pltpu.VMEM((2, hidden, third), BF16),
+            pltpu.VMEM(more[0].shape, BF16),
+            pltpu.VMEM((seqs, span, width), BF16),
             pltpu.VMEM((4, 8, hidden), F32),
             pltpu.SemaphoreType.DMA((4, 2)),
+            pltpu.SemaphoreType.DMA((8, 2)),
+            pltpu.SemaphoreType.DMA((11, 2)),
         ]
     operands = (d, rhs, weight) + more
     return pl.pallas_call(
         functools.partial(backward_kernel, second, seqs, hidden, length, width),
         name="layer_two_backward" if second else "layer_one_backward",
-        in_specs=[ANY] * (3 + 5 * second) + [pl.BlockSpec(memory_space=pltpu.VMEM)] * (2 - 2 * second),
-        out_specs=specs,
+        in_specs=[ANY] * 5 if second else [ANY] * 6 + [vmem] * 2,
+        out_specs=[ANY] * (len(outs) - 1) + [vmem],
         out_shape=outs,
         scratch_shapes=scratch + sum_scratch(seqs, hidden, third, rows, cols),
         compiler_params=params(collective_id=1 if second else 2, has_side_effects=True),
@@ -901,17 +943,25 @@
         self.copies[1].wait_recv()
         self.copies[6].start()
 
-    def share(self):
+    def share_near(self):
         self.copies[2].wait_recv()
         self.copies[7].start()
+        self.copies[4].wait_recv()
+        self.copies[7].wait_recv()
+
+    def share_far(self):
         self.copies[3].wait_recv()
         self.copies[8].start()
         self.copies[6].wait_recv()
         self.copies[9].start()
         self.copies[5].wait_recv()
         self.copies[10].start()
-        for k in (4, 7, 8, 9, 10):
+        for k in (8, 9, 10):
             self.copies[k].wait_recv()
+
+    def share(self):
+        self.share_near()
+        self.share_far()
 
     def drain(self):
         for copy in self.copies:
@@ -982,26 +1032,32 @@
         seed[:, :, pl.ds(0, 4)] = jnp.zeros((seqs, groups, 4, piece, hidden), BF16)
         for s in range(seqs):
             prepare_pick(s)
-        b1[...] = to_column(b1_in[...])
-        b2[...] = to_column(b2_in[...])
+        b1[...] = to_column(b1_in[...][None, :])
+        b2[...] = to_column(b2_in[...][None, :])
 
     late = [
         (remote(sent.at[peer["tm"]], seed.at[:, :, here.b], ssem.at[d, 0], ssem.at[d, 1], peer), peer)
         for d, peer in enumerate(here.peers, 1)
     ]
 
-    def products(rhs, dims):
+    def first_products(s):
         def block(r):
             rows = pl.ds(r, hidden)
-            p[rows, :] = dot(w[rows, :], rhs(), dims)
+            p[rows, :] = dot(w[rows, :], xg[s].reshape(length, width), NT)
 
         tiles(6 * hidden, hidden, block)
 
-    def first_products(s):
-        products(lambda: xg[s].reshape(length, width), NT)
-
-    def second_products(s):
-        products(lambda: hg[:, :, columns_of(s)].reshape(width, length), NN)
+    def second_products(s, near):
+        y = here.y if near else 1 - here.y
+        depth = pl.ds(pl.multiple_of(y * (width // 2), LANES), width // 2)
+
+        def block(r):
+            rows = pl.ds(r, hidden)
+            rhs = hg[pl.ds(y * 4, 4), :, columns_of(s)].reshape(width // 2, length)
+            got = dot(w[rows, depth], rhs, NN)
+            p[rows, :] = got if near else p[rows, :] + got
+
+        tiles(6 * hidden, hidden, block)
 
     def first_pool(s):
         first = s * length
@@ -1108,10 +1164,12 @@
         pick_hidden(s)
     for copy in spread_h:
         copy.start()
-    hs[0].share()
+    hs[0].share_near()
+    load_w2.wait()
+    second_products(0, True)
+    hs[0].share_far()
     store_h[0].start()
-    load_w2.wait()
-    second_products(0)
+    second_products(0, False)
     hs[1].relay()
 
     @pl.when(here.y == 1)
@@ -1123,9 +1181,11 @@
     store_p[0].wait()
     store_c[0].wait()
     second_pool(0)
-    hs[1].share()
+    hs[1].share_near()
+    second_products(1, True)
+    hs[1].share_far()
     store_h[1].start()
-    second_products(1)
+    second_products(1, False)
     store_p[1].wait()
     store_c[1].wait()
     second_pool(1)
@@ -1219,6 +1279,37 @@
     )(x, w1, w2, cotangent, b1, b2, starts)
 
 
+def widen_kernel(one_ref, two_ref, outgate_ref, wide_one_ref, wide_two_ref):
+    wide_one_ref[...] = one_ref[...].astype(F32)
+    last = lax.rem(pl.program_id(0), 3) == 2
+
+    @pl.when(last)
+    def _():
+        wide_two_ref[...] = outgate_ref[...].astype(F32)
+
+    @pl.when(jnp.logical_not(last))
+    def _():
+        wide_two_ref[...] = two_ref[...].astype(F32)
+
+
+def widen(one, two, outgate):
+    _, hidden, width = one.shape
+    dims = (1, hidden, width)
+    return pl.pallas_call(
+        widen_kernel,
+        name="weight_gradients",
+        grid=(6,),
+        in_specs=[
+            pl.BlockSpec(dims, lambda k: (k, 0, 0)),
+            pl.BlockSpec(dims, lambda k: (k - k % 3 // 2, 0, 0)),
+            pl.BlockSpec(dims, lambda k: (k // 3, 0, 0)),
+        ],
+        out_specs=[pl.BlockSpec(dims, lambda k: (k, 0, 0))] * 2,
+        out_shape=[shape(one.shape, F32)] * 2,
+        compiler_params=params(),
+    )(one, two, outgate)
+
+
 def per_device(line, inputs, weight_one, fbias_one, weight_two, fbias_two, cotangent, cluster_starts):
     seqs, span, width = inputs.shape
     count = lax.axis_size("tm")
@@ -1232,12 +1323,12 @@
 
     if line:
         x, h1, pre1, cell1, h2, d2, db2, *picked = run_forward(
-            inputs, w1, fbias_one[None], w2, fbias_two[None], cotangent, cluster_starts
+            inputs, w1, fbias_one, w2, fbias_two, cotangent, cluster_starts
         )
         x, h1 = x.reshape(total, width), h1.reshape(width, total)
-        gw2, d1, db1, h2, _ = run_backward(seqs, d2, h1, w2, True, (pre1, cell1, h2, *picked))
-        h2 = h2.reshape(count, seqs, groups, piece, hidden).transpose(1, 3, 2, 0, 4)
-        gw1, gx1, db = run_backward(seqs, d1, x, w1, False, (db1, db2))
+        gw2, d1, db1 = run_backward(seqs, d2, h1, w2, True, (pre1, cell1))
+        gw1, gx1, h2, _, wo, db = run_backward(seqs, d1, x, w1, False, (h2, *picked, db1, db2))
+        gw1, gw2 = widen(gw1, gw2, wo)
     else:
         x = inputs.reshape(seqs, piece, groups, width).transpose(0, 2, 1, 3)
         bias1, bias2 = fbias_one[:, None], fbias_two[:, None]
@@ -1255,17 +1346,17 @@
         h2 = h2.reshape(hidden, seqs, groups, count, piece)
         h2 = lax.all_to_all(h2, "tm", split_axis=3, concat_axis=0, tiled=True)
         h2 = h2.reshape(width, seqs, groups, piece).transpose(1, 3, 2, 0)
-        gw2 = lax.psum(dot(d2, h1, NT).astype(BF16), "seq")
+        gw2 = lax.psum(dot(d2, h1, NT).astype(BF16), "seq").astype(F32)
         gx2 = lax.psum_scatter(dot(w2, d2, TN).astype(BF16), "tm", scatter_dimension=0, tiled=True)
         d1, db1 = run_back(seqs, gx2, pre1, cell1)
-        gw1 = lax.psum(dot(d1, x, NN).astype(BF16), "seq")
+        gw1 = lax.psum(dot(d1, x, NN).astype(BF16), "seq").astype(F32)
         gx1 = dot(d1, w1, TN).astype(BF16).reshape(seqs, groups, LANES, width)
         gx1 = lax.psum_scatter(gx1, "tm", scatter_dimension=2, tiled=True)
         gx1 = gx1.transpose(0, 2, 1, 3).reshape(seqs, span, width)
         db = lax.psum(jnp.stack([db1, db2]).sum(axis=(1, 3)), "seq")
     out = h2.reshape(seqs, span, width)
     dims = weight_one.shape
-    return (out, gx1, gw1.astype(F32).reshape(dims), db[0], gw2.astype(F32).reshape(dims), db[1])
+    return (out, gx1, gw1.reshape(dims), db[0], gw2.reshape(dims), db[1])
 
 
 def solution(mesh):

time: 539 us -> 494 us (0.917)
  other arithmetic: 21.2 us -> 0 us
  Pallas kernels: 502 us -> 482 us
    pallas_call x2, Pallas kernels: 374 us -> 340 us  [run_backward(): pl.pallas_call(functools.partial(backward_kernel, second, seqs, hidden, l...]
    reshape x2 -> x0, other arithmetic: 21.2 us -> none  [the longest x1 10.6 us: per_device(): gw2.astype(F32).reshape(dims)]
    pallas_call x0 -> x1, Pallas kernels: none -> 15.7 us  [widen(): pl.pallas_call(widen_kernel, name='weight_gradients', grid=(6,), in_specs...]
where the time goes in v5:
time: 494 us; the launch traced here: 489 us
  Pallas kernels  482 us (98%)
  local copies, waits for them, and re-layouts  6.1 us (1%)
    pallas_call x2, Pallas kernels, run_backward(): pl.pallas_call(functools.partial(backward_kernel, second, seqs, hidden, l...  340 us
    pallas_call x1, Pallas kernels, run_forward(): pl.pallas_call(functools.partial(forward_kernel, seqs, hidden, length, wi...  126 us
    pallas_call x1, Pallas kernels, widen(): pl.pallas_call(widen_kernel, name='weight_gradients', grid=(6,), in_specs...  15.7 us

profile of v5, /device:TPU:0, one launch (start us, length us, event | category | flops | bytes accessed | tf_op | source)
XLA Modules:
  0.0 488.8 jit_solution(13030890028884656542)
XLA Ops:
  0.6 125.9 %forward.1 = (bf16[2,8,8,16,2304]{4,3,2,1,0:T(8,128)(2,1)}, bf16[8,288,2048]{2,1,0:T(8,128)(2,1)}, bf16[864,2048]{1,0:T(8,128)(2,1)}, f32[288,2048]{1,0:T(8,128)...) custom-call(bf16[2,128,2304]{2,1,0:T(8,128)(2,1)} %refs_0_.1, ...), custom_call_target="tpu_custom_call" | custom-call | tf_op jit(solution)/shard_map/forward/pallas_call | solution.py:1234
  126.5 140.5 %layer_two_backward.1 = (bf16[6,288,2304]{2,1,0:T(8,128)(2,1)}, bf16[1728,2048]{1,0:T(8,128)(2,1)}, f32[2,288,1]{2,1,0:T(8,128)}) custom-call(bf16[1728,2048]{1,0:T(8,128)(2,1)} %get-tuple-element.25.refs_0_, bf16[2304,2048]{1,0:T(8,128)(2,1)} %bitcast.11, bf16[1728,2304]{1,0:T(8,128)(2,1)} %bitcast.7, bf16[864,2048]{1,0:T(8,128)(2,1)} %get-tuple-element.27.refs_3_, ...), custom_call_target="tpu_custom_call" | custom-call | tf_op jit(solution)/shard_map/layer_two_backward/pallas_call | solution.py:882
  267.1 199.4 %layer_one_backward.1 = (bf16[6,288,2304]{2,1,0:T(8,128)(2,1)}, bf16[2,128,2304]{2,1,0:T(8,128)(2,1)}, bf16[2,128,2304]{2,1,0:T(8,128)(2,1)}, bf16[2,2304,1024]{...) custom-call(bf16[1728,2048]{1,0:T(8,128)(2,1)} %get-tuple-element.29.refs_0_, ...), custom_call_target="tpu_custom_call" | custom-call | tf_op jit(solution)/shard_map/layer_one_backward/pallas_call | solution.py:882
  466.5 1.4 slice_reduce_fusion
  467.9 15.7 %weight_gradients.1 = (f32[6,288,2304]{2,1,0:T(8,128)}, f32[6,288,2304]{2,1,0:T(8,128)}) custom-call(bf16[6,288,2304]{2,1,0:T(8,128)(2,1)} %get-tuple-element.38.one_ref, bf16[6,288,2304]{2,1,0:T(8,128)(2,1)} %get-tuple-element.39.two_ref, bf16[2,288,2304]{2,1,0:T(8,128)(2,1)} %get-tuple-element.40.outgate_ref), custom_call_target="tpu_custom_call" | custom-call | tf_op jit(solution)/shard_map/weight_gradients/pallas_call | solution.py:1298
  483.6 2.4 copy.15
  486.0 2.4 copy.16

commit v6 on v5

--- a/solution.py
+++ b/solution.py
@@ -292,6 +292,9 @@
 SLOTS = 12
 AHEAD = 6
 BEHIND = 2
+LATER = 12
+BLOCKS = 30
+OWN = 18
 
 
 class Here:
@@ -335,11 +338,16 @@
     pl.semaphore_wait(barrier, len(targets))
 
 
+def pick(condition, a, b):
+    if isinstance(condition, bool):
+        return a if condition else b
+    return jnp.where(condition, a, b)
+
+
 class SeqSum:
-    def __init__(self, here, gates, hidden, third, own, ring_in, ring_mid, total, out, sems, credits):
+    def __init__(self, here, hidden, third, own, ring_in, ring_mid, total, out, sems, credits):
         self.here, self.third, self.rows = here, third, hidden // PIECES
-        self.gates, self.blocks = gates, 2 * gates * THIRDS
-        self.units = self.blocks * PIECES
+        self.units = BLOCKS * PIECES
         self.own, self.ring_in, self.ring_mid, self.total, self.out = own, ring_in, ring_mid, total, out
         self.sems = sems
         self.credit_in, self.credit_mid, self.credit_out = credits
@@ -348,7 +356,7 @@
         return pl.ds(pl.multiple_of(lax.rem(u, PIECES) * self.rows, 16), self.rows)
 
     def mine(self, u):
-        return self.own.at[u // PIECES, self.rows_of(u)]
+        return self.own.at[lax.rem(u // PIECES, OWN), self.rows_of(u)]
 
     def inward(self, u):
         i = lax.rem(u, SLOTS)
@@ -364,13 +372,16 @@
 
     def store(self, u, ring):
         i, block = lax.rem(u, SLOTS), u // PIECES
-        cols = pl.ds(pl.multiple_of((block // (2 * self.gates)) * self.third, LANES), self.third)
-        to = self.out.at[self.product(block), self.rows_of(u), cols]
+        second = block < LATER
+        t = pick(second, block // 4, (block - LATER) // 6)
+        cols = pl.ds(pl.multiple_of(t * self.third, LANES), self.third)
+        to = self.out.at[self.product(block) + pick(second, 6, 0), self.rows_of(u), cols]
         return pltpu.make_async_copy(ring.at[i], to, self.sems.at[6, i])
 
-    def product(self, block):
-        k = lax.rem(block, 2 * self.gates)
-        return k if self.gates == 3 else (k // 2) * 3 + lax.rem(k, 2)
+    @staticmethod
+    def product(block):
+        k = lax.rem(block, 4)
+        return pick(block < LATER, (k // 2) * 3 + lax.rem(k, 2), lax.rem(block, 6))
 
     def add(self, dst, a, b):
         def rows(r):
@@ -476,10 +487,9 @@
     def __init__(self, here, part, pairs, wide_x, wide_y, last_x, last_y, sems):
         self.here, self.part, self.pairs = here, part, pairs
         self.wide_x, self.wide_y, self.last_x, self.last_y, self.sems = wide_x, wide_y, last_x, last_y, sems
-        self.rows = part.shape[3]
-        self.upper = pl.ds(0, self.rows // 2)
-        self.lower = pl.ds(self.rows // 2, self.rows // 2)
-        self.step = 16
+        self.count = part.shape[3]
+        self.half = self.count // 2
+        self.upper, self.lower = pl.ds(0, self.half), pl.ds(self.half, self.half)
 
     def copy(self, k, s, src, dst, target):
         return remote(src, dst, self.sems.at[s, k, 0], self.sems.at[s, k, 1], target)
@@ -508,166 +518,154 @@
         h = self.here
         self.swap(s).wait()
 
-        def rows(r):
-            at = pl.ds(r, self.step)
+        def some(r):
+            at = pl.ds(r, 8)
             for y in range(2):
                 for x in range(2):
-                    self.pairs[s, y, x, at, :] = self.pairs[s, y, x, at, :] + self.part[y, x, h.c, at, :]
-
-        tiles(self.rows, self.step, rows)
+                    self.pairs[s, y, x, at] = self.pairs[s, y, x, at] + self.part[y, x, h.c, at]
+
+        tiles(self.count, 8, some)
         for copy in self.wide(s):
             copy.start()
 
     def turn(self, s):
         h = self.here
-        half = self.rows // 2
         for copy in self.wide(s):
             copy.wait()
 
-        def rows(r):
-            at, low = pl.ds(r, self.step), pl.ds(half + r, self.step)
+        def some(r):
+            at, low = pl.ds(r, 8), pl.ds(self.half + r, 8)
             for k in range(2):
-                self.pairs[s, k, h.x, at, :] = self.pairs[s, k, h.x, at, :] + self.wide_x[s, k, at, :]
-                self.pairs[s, h.y, k, low, :] = self.pairs[s, h.y, k, low, :] + self.wide_y[s, k, at, :]
-
-        tiles(half, self.step, rows)
+                self.pairs[s, k, h.x, at] = self.pairs[s, k, h.x, at] + self.wide_x[s, k, at]
+                self.pairs[s, h.y, k, low] = self.pairs[s, h.y, k, low] + self.wide_y[s, k, at]
+
+        tiles(self.half, 8, some)
         for copy in self.last(s):
             copy.start()
 
-    def done(self, s, out):
+    def done(self, s, down, put):
         h = self.here
-        half = self.rows // 2
         for copy in self.last(s):
             copy.wait()
 
-        def rows(r):
-            at, low = pl.ds(r, self.step), pl.ds(half + r, self.step)
-            out[at, :] = self.pairs[s, h.y, h.x, at, :] + self.last_y[s, at, :]
-            out[low, :] = self.pairs[s, h.y, h.x, low, :] + self.last_x[s, at, :]
-
-        tiles(half, self.step, rows)
-
-
-def sum_scratch(seqs, hidden, third, rows, cols):
-    return [
-        pltpu.VMEM((18, hidden, third), BF16),
-        pltpu.VMEM((SLOTS, hidden // PIECES, third), BF16),
-        pltpu.VMEM((SLOTS, hidden // PIECES, third), BF16),
-        pltpu.VMEM((SLOTS, hidden // PIECES, third), BF16),
-        pltpu.SemaphoreType.DMA((7, SLOTS)),
-        pltpu.SemaphoreType.REGULAR,
-        pltpu.SemaphoreType.REGULAR,
-        pltpu.SemaphoreType.REGULAR,
-        pltpu.VMEM((2, 2, 2, rows, cols), BF16),
-        pltpu.VMEM((seqs, 2, 2, rows, cols), BF16),
-        pltpu.VMEM((seqs, 2, rows // 2, cols), BF16),
-        pltpu.VMEM((seqs, 2, rows // 2, cols), BF16),
-        pltpu.VMEM((seqs, rows // 2, cols), BF16),
-        pltpu.VMEM((seqs, rows // 2, cols), BF16),
-        pltpu.SemaphoreType.DMA((seqs, 5, 2)),
-        pltpu.SemaphoreType.DMA((17,)),
-    ]
-
-
-def backward_kernel(second, seqs, hidden, length, width, *refs):
+        def some(r):
+            at, low = pl.ds(r, down), pl.ds(self.half + r, down)
+            first = pl.multiple_of(r // down * LANES, LANES)
+            put(first, (self.pairs[s, h.y, h.x, at] + self.last_y[s, at]).reshape(down * 16, LANES))
+            first = pl.multiple_of((self.half + r) // down * LANES, LANES)
+            put(first, (self.pairs[s, h.y, h.x, low] + self.last_x[s, at]).reshape(down * 16, LANES))
+
+        tiles(self.half, down, some)
+
+
+def backward_kernel(seqs, hidden, length, width, *refs):
     third = width // THIRDS
-    if second:
-        d_in, r_in, w_in, pre_in, cell_in, gw_out, d_out, db_out = refs[:8]
-        dv, wv, rv, pre, cell, work, edge, grad = refs[8:16]
-        rest = refs[16:]
-    else:
-        d_in, r_in, w_in, h_in, sel_in, dsel_in, db1_in, db2_in = refs[:8]
-        gw_out, gx_out, h_out, sel_out, wo_out, db_out = refs[8:14]
-        dv, wv, rv, gxv, picked, dsel, wo, heard, hv, dbv, dsem, hsem, psem = refs[14:27]
-        rest = refs[27:]
-    own, ring_in, ring_mid, total, zsem, *credits = rest[:8]
-    rank_refs, lsem = rest[8:15], rest[15]
+    d_in, h1_in, x_in, w2_in, w1_in, pre_in, cell_in, h_in, sel_in, dsel_in, db2 = refs[:11]
+    gw_out, gx_out, h_out, sel_out, wo_out, db_out = refs[11:17]
+    dv, wv, rh, rx, pre, cell, work, edge, grad, gxv, dsel, wo, heard, hv, db1, dbv = refs[17:33]
+    own, ring_in, ring_mid, total, part, pairs, wide_x, wide_y, last_x, last_y = refs[33:43]
+    zsem, rsem, dsem, hsem, psem, lsem, credit_in, credit_mid, credit_out, ready = refs[43:]
     here = Here()
-    gates = 2 if second else 3
-    ar = SeqSum(here, gates, hidden, third, own, ring_in, ring_mid, total, gw_out, zsem, credits)
-    rs = RankSum(here, *rank_refs)
+    ar = SeqSum(here, hidden, third, own, ring_in, ring_mid, total, gw_out, zsem, (credit_in, credit_mid, credit_out))
+    sums = {
+        layer: RankSum(here, part, pairs, wide_x, wide_y, last_x, last_y, rsem.at[layer - 1]) for layer in (1, 2)
+    }
     groups, piece = length // LANES, LANES // 8
+    half = width // 2
 
     def columns_of(s):
         return pl.ds(s * length, length)
 
-    def rhs(t):
-        if second:
-            src = r_in.at[pl.ds(t * third, third), :]
-        else:
-            src = r_in.at[:, pl.ds(t * third, third)]
-        return pltpu.make_async_copy(src, rv.at[t % 2], lsem.at[t % 2])
-
-    loads = [pltpu.make_async_copy(d_in, dv, lsem.at[2]), pltpu.make_async_copy(w_in, wv, lsem.at[3])]
-    if second:
-        loads.append(pltpu.make_async_copy(pre_in, pre, lsem.at[4]))
-        loads.append(pltpu.make_async_copy(cell_in, cell, lsem.at[5]))
-    loads[0].start()
-    rhs(0).start()
-    for copy in loads[1:]:
+    def load(src, dst, k):
+        return pltpu.make_async_copy(src, dst, lsem.at[k])
+
+    def load_d(k):
+        rows = pl.ds(k * hidden, hidden)
+        return load(d_in.at[rows], dv.at[rows], k)
+
+    def load_rhs(layer, t):
+        at = pl.ds(t * third, third)
+        return load(h1_in.at[at], rh, 6) if layer == 2 else load(x_in.at[:, at], rx, 7)
+
+    load_w = {2: load(w2_in, wv, 8), 1: load(w1_in, wv, 8)}
+    load_p, load_c, load_e = load(pre_in, pre, 9), load(cell_in, cell, 10), load(dsel_in, dsel, 11)
+    keep = load(sel_in, sel_out.at[:, pl.ds(here.b * hidden, hidden)], 12)
+    store_g = load(gxv, gx_out, 13)
+    store_h = load(hv, h_out, 14)
+    load_rhs(2, 0).start()
+    for k in range(6):
+        load_d(k).start()
+    load_w[2].start()
+    load_rhs(1, 0).start()
+    for copy in (load_p, load_c, load_e, keep):
         copy.start()
-    rhs(1).start()
-    if second:
-        meet([here.core, here.across_x, here.across_y, here.pair, here.middle])
-    else:
-        meet(here.peers + here.line)
-        load_e = pltpu.make_async_copy(dsel_in, dsel, lsem.at[8])
-        load_e.start()
-
-        def halves(start, half):
-            size = hidden if half is None else hidden // 2
-            return pl.ds(start + (half or 0) * size, size)
-
-        gather = Gather(
-            here,
-            lambda b, half: sel_out.at[:, halves(b * hidden, half)],
-            psem,
-            lambda half: sel_in.at[:, halves(0, half)],
-        )
-        gather.start()
-        keep = pltpu.make_async_copy(sel_in, sel_out.at[:, pl.ds(here.b * hidden, hidden)], lsem.at[9])
-        keep.start()
-        dbv[here.z] = jnp.zeros((8, hidden), F32)
-        for layer, db in enumerate((db1_in, db2_in)):
-            dbv[here.z, layer : layer + 1, :] = to_row(sum(db[s] for s in range(1, seqs)) + db[0])
-        biases = []
-        for d, peer in enumerate(here.line, 1):
-            biases.append(remote(dbv.at[here.z], dbv.at[here.z], dsem.at[d, 0], dsem.at[d, 1], peer))
-        for copy in biases:
-            copy.start()
-        spread = [pltpu.make_async_copy(h_in.at[here.b], heard.at[here.b], hsem.at[0, 0])]
-        for d, peer in enumerate(here.peers, 1):
-            spread.append(remote(h_in.at[peer["tm"]], heard.at[here.b], hsem.at[d, 0], hsem.at[d, 1], peer))
-
-    done = [0]
-
-    def units(t, low, high):
+    meet(here.peers + here.line)
+
+    def halves(start, i):
+        size = hidden if i is None else hidden // 2
+        return pl.ds(start + (i or 0) * size, size)
+
+    gather = Gather(
+        here,
+        lambda b, i: sel_out.at[:, halves(b * hidden, i)],
+        psem,
+        lambda i: sel_in.at[:, halves(0, i)],
+    )
+    biases = [
+        remote(dbv.at[here.z], dbv.at[here.z], dsem.at[d, 0], dsem.at[d, 1], peer)
+        for d, peer in enumerate(here.line, 1)
+    ]
+    spread = [pltpu.make_async_copy(h_in.at[here.b], heard.at[here.b], hsem.at[0, 0])]
+    for d, peer in enumerate(here.peers, 1):
+        spread.append(remote(h_in.at[peer["tm"]], heard.at[here.b], hsem.at[d, 0], hsem.at[d, 1], peer))
+
+    done, spent = [0], [0]
+
+    def units(layer, t, low, high):
+        start = t * 4 if layer == 2 else LATER + t * 6
+        assert start + high <= OWN or spent[0] > (start + high - OWN) * PIECES - 1 + SLOTS
+
         def unit(k, carry):
-            block = t * (2 * gates) + k
+            block = start + k
             rows = pl.ds(pl.multiple_of(ar.product(block) * hidden, 16), hidden)
-            own[block] = dot(dv[rows, :], rv[t % 2], NT if second else NN).astype(BF16)
-            for i in range(PIECES):
-                u = block * PIECES + i
-
-                @pl.when(u < AHEAD)
-                def _(u=u):
-                    ar.offer(u)
+            got = dot(dv[rows, :], rh[...], NT) if layer == 2 else dot(dv[rows, :], rx[...], NN)
+            own[lax.rem(block, OWN)] = got.astype(BF16)
+            if start == 0:
+                for i in range(PIECES):
+                    u = block * PIECES + i
+
+                    @pl.when(u < AHEAD)
+                    def _(u=u):
+                        ar.offer(u)
 
             return carry
 
         lax.fori_loop(low, high, unit, 0)
-        done[0] = (t * 2 * gates + high) * PIECES
-
-    def strips(s, q):
-        if second:
+        done[0] = (start + high) * PIECES
+
+    def tick(count=1):
+        first = spent[0]
+        spent[0] += count
+        assert spent[0] - 1 + AHEAD < done[0] or done[0] == ar.units
+
+        def step(n, carry):
+            ar.tick(n)
+            return carry
+
+        lax.fori_loop(first, spent[0], step, 0)
+
+    def strips(layer, s, q):
+        if layer == 2:
             i, start = q // 2, lax.rem(q, 2) * (length // 2)
-            lhs = pl.ds(pl.multiple_of(i * (width // 2), LANES), width // 2)
+            down = hidden // 16
+            lhs = pl.ds(pl.multiple_of(i * half, LANES), half)
 
             def strip(c):
-                cols = pl.ds(pl.multiple_of(start + c, 256), 256)
                 src = pl.ds(pl.multiple_of(s * length + start + c, 256), 256)
                 got = dot(wv[:, lhs], dv[:, src], TN).astype(BF16)
-                rs.part[i, :, :, :, cols] = got.reshape(2, 2, hidden, 256)
+                for n in range(2):
+                    at = pl.ds(((start + c) // LANES + n) * down, down)
+                    part[i, :, :, at] = got[:, n * LANES : (n + 1) * LANES].reshape(2, 2, down, 16, LANES)
 
             tiles(length // 2, 256, strip)
         else:
@@ -676,151 +674,172 @@
                 cols = pl.ds(pl.multiple_of(c * 256, 256), 256)
                 got = dot(dv[:, columns_of(s)], wv[:, cols], TN).astype(BF16)
                 for j in range(groups):
-                    block = got[j * LANES : (j + 1) * LANES].reshape(2, 2, 2, piece, 256)
-                    rs.part[:, :, :, pl.ds(j * piece, piece), cols] = block
+                    for n in range(2):
+                        block = got[j * LANES : (j + 1) * LANES, n * LANES : (n + 1) * LANES]
+                        part[:, :, :, (c * 2 + n) * groups + j] = block.reshape(2, 2, 2, piece, LANES)
                 return carry
 
             count = width // 256
             lax.fori_loop(count * q // 4, count * (q + 1) // 4, strip, 0)
 
-    spent = [0]
-
-    def tick(count=1):
-        for _ in range(count):
-            assert spent[0] + AHEAD < min(done[0], ar.units) or done[0] == ar.units
-            ar.tick(spent[0])
-            spent[0] += 1
-
-    def input_grad(s):
+    def input_grad(layer, s):
         first = spent[0]
-        assert first + 3 + AHEAD < done[0]
+        spent[0] += 4
+        assert spent[0] - 1 + AHEAD < done[0]
 
         def quarter(q, carry):
-            strips(s, q)
+            strips(layer, s, q)
             ar.tick(first + q)
             return carry
 
         lax.fori_loop(0, 4, quarter, 0)
-        spent[0] += 4
-
-    def settle(s):
-        if second:
-            rs.done(s, grad.at[:, columns_of(s)])
+
+    def settle(layer, s):
+        if layer == 2:
+
+            def put(first, v):
+                grad[:, pl.ds(s * length + first, LANES)] = v
+
+            sums[2].done(s, hidden // 16, put)
         else:
-            rs.done(s, gxv.at[s])
+
+            def put(first, v):
+                gxv[s, :, pl.ds(first, LANES)] = v
+
+            sums[1].done(s, groups, put)
             gxv[s] = dot(reorder(piece, groups, True), gxv[s], NN).astype(BF16)
 
-    def outgate_load(t):
-        return pltpu.make_async_copy(sel_out.at[:, pl.ds(t * third, third)], picked, lsem.at[10])
-
-    def outgate_store(t, tap):
-        return pltpu.make_async_copy(wo.at[tap], wo_out.at[tap, :, pl.ds(t * third, third)], lsem.at[11 + tap])
+    def pool(s):
+        first = s * length
+        pool_backward(first, grad, pre, cell, first, dv, db1.at[s], work, edge, hidden, groups)
+
+    def load_picked(t):
+        at = pl.ds(t * third, third)
+        size = rh.shape[1] // 2
+        return [load(sel_out.at[tap, at], rh.at[:, pl.ds(tap * size, size)], 15 + tap) for tap in range(2)]
+
+    def store_o(t, tap):
+        return load(wo.at[tap], wo_out.at[tap, :, pl.ds(t * third, third)], 17 + tap)
 
     def outgate(t):
-        outgate_load(t).wait()
-        for tap in range(2):
+        size = rh.shape[1] // 2
+        for tap, copy in enumerate(load_picked(t)):
+            copy.wait()
             if t:
-                outgate_store(t - 1, tap).wait()
-            wo[tap] = dot(dsel[...], picked[tap], NT).astype(BF16)
-            outgate_store(t, tap).start()
+                store_o(t - 1, tap).wait()
+            wo[tap] = dot(dsel[...], rh[:, pl.ds(tap * size, size)], NT).astype(BF16)
+            store_o(t, tap).start()
         if t + 1 < THIRDS:
-            outgate_load(t + 1).start()
-
-    count = 2 * gates
-    loads[0].wait()
-    rhs(0).wait()
-    units(0, 0, count)
-    rhs(2).start()
-    loads[1].wait()
-    input_grad(0)
-    rs.start(0)
-    if second:
-        tick()
-        rhs(1).wait()
-        units(1, 0, 2)
-        rs.cross(0)
+            for copy in load_picked(t + 1):
+                copy.start()
+
+    load_rhs(2, 0).wait()
+    load_d(0).wait()
+    load_d(1).wait()
+    units(2, 0, 0, 2)
+    for k in range(2, 6):
+        load_d(k).wait()
+    units(2, 0, 2, 4)
+    load_rhs(2, 1).start()
+    load_w[2].wait()
+    input_grad(2, 0)
+    sums[2].start(0)
+    tick()
+    load_rhs(2, 1).wait()
+    units(2, 1, 0, 2)
+    sums[2].cross(0)
+    tick(2)
+    units(2, 1, 2, 4)
+    load_rhs(2, 2).start()
+    input_grad(2, 1)
+    load_w[1].start()
+    sums[2].start(1)
+    sums[2].turn(0)
+    load_rhs(2, 2).wait()
+    tick(2)
+    units(2, 2, 0, 2)
+    tick()
+    sums[2].cross(1)
+    units(2, 2, 2, 4)
+    tick(2)
+    settle(2, 0)
+    tick(2)
+    load_p.wait()
+    load_c.wait()
+    pool(0)
+    tick()
+    sums[2].turn(1)
+    gather.start()
+    tick(3)
+    settle(2, 1)
+    for target in (here.core, here.across_x, here.across_y):
+        signal(ready, target)
+    pool(1)
+    tick(2)
+    load_rhs(1, 0).wait()
+    units(1, 0, 0, 3)
+    tick()
+    gather.relay()
+    units(1, 0, 3, 6)
+    load_rhs(1, 1).start()
+    dbv[here.z] = jnp.zeros((8, hidden), F32)
+    for row, db in enumerate((db1, db2)):
+        dbv[here.z, row : row + 1, :] = to_row(sum(db[s] for s in range(1, seqs)) + db[0])
+    for copy in biases:
+        copy.start()
+    tick(2)
+    load_w[1].wait()
+    pl.semaphore_wait(ready, 3)
+    input_grad(1, 0)
+    sums[1].start(0)
+    load_rhs(1, 1).wait()
+    units(1, 1, 0, 2)
+    tick()
+    units(1, 1, 2, 4)
+    tick()
+    sums[1].cross(0)
+    tick()
+    input_grad(1, 1)
+    sums[1].start(1)
+    units(1, 1, 4, 6)
+    load_rhs(1, 2).start()
+    tick(2)
+    gather.share()
+    tick()
+    sums[1].cross(1)
+    tick()
+    sums[1].turn(0)
+    tick(2)
+    load_rhs(1, 2).wait()
+    units(1, 2, 0, 2)
+    tick(2)
+    units(1, 2, 2, 4)
+    tick(3)
+    units(1, 2, 4, 6)
+    tick(4)
+    settle(1, 0)
+    sums[1].turn(1)
+    keep.wait()
+    load_e.wait()
+    for copy in load_picked(0):
+        copy.start()
+    tick(2)
+    for copy in spread:
+        copy.start()
+    tick(4)
+    settle(1, 1)
+    store_g.start()
+    for t in range(THIRDS):
         tick(2)
-        units(1, 2, 4)
-        input_grad(1)
-        rs.start(1)
-        rs.turn(0)
-        rhs(2).wait()
-        tick(2)
-        units(2, 0, 2)
-        tick()
-        rs.cross(1)
-        units(2, 2, 4)
-        tick(2)
-        settle(0)
-        tick(2)
-        for copy in loads[2:4]:
-            copy.wait()
-        stores = [
-            pltpu.make_async_copy(dv.at[:, columns_of(s)], d_out.at[:, columns_of(s)], lsem.at[6 + s])
-            for s in range(seqs)
-        ]
-
-        def pool(s):
-            first = s * length
-            pool_backward(first, grad, pre, cell, first, dv, db_out.at[s], work, edge, hidden, groups)
-            stores[s].start()
-
-        pool(0)
-        tick()
-        rs.turn(1)
-        tick(3)
-        settle(1)
-        pool(1)
-    else:
-        gather.relay()
-        rhs(1).wait()
-        units(1, 0, 2)
-        tick()
-        units(1, 2, 4)
-        tick()
-        rs.cross(0)
-        tick()
-        input_grad(1)
-        rs.start(1)
-        units(1, 4, 6)
-        tick(2)
-        gather.share()
-        rhs(2).wait()
-        units(2, 0, 2)
-        tick()
-        rs.cross(1)
-        tick()
-        rs.turn(0)
-        tick()
-        units(2, 2, 4)
-        tick()
-        units(2, 4, 6)
-        tick(6)
-        settle(0)
-        rs.turn(1)
-        keep.wait()
-        load_e.wait()
-        outgate_load(0).start()
-        tick(2)
-        for copy in spread:
-            copy.start()
-        tick(4)
-        settle(1)
-        stores = [pltpu.make_async_copy(gxv, gx_out, lsem.at[6])]
-        stores[0].start()
-        for t in range(THIRDS):
-            tick(2)
-            outgate(t)
-        for copy in spread:
-            copy.wait()
-        back = reorder(piece, groups, True)
-        for s in range(seqs):
-            for b in range(8):
-                block = heard[b, pl.ds(s * LANES, LANES), :]
-                hv[s, :, b * hidden : (b + 1) * hidden] = dot(back, block, NN).astype(BF16)
-        stores += [outgate_store(THIRDS - 1, tap) for tap in range(2)]
-        stores.append(pltpu.make_async_copy(hv, h_out, lsem.at[13]))
-        stores[-1].start()
+        outgate(t)
+    for copy in spread:
+        copy.wait()
+    back = reorder(piece, groups, True)
+    for s in range(seqs):
+        for b in range(8):
+            block = heard[b, pl.ds(s * LANES, LANES), :]
+            hv[s, :, b * hidden : (b + 1) * hidden] = dot(back, block, NN).astype(BF16)
+    store_h.start()
 
     def more(n, carry):
         ar.tick(n)
@@ -828,66 +847,69 @@
 
     lax.fori_loop(spent[0], ar.units + BEHIND + 2, more, 0)
     ar.drain()
-    for copy in stores:
+    gather.drain()
+    for copy in [store_g, store_h] + [store_o(THIRDS - 1, tap) for tap in range(2)] + biases:
         copy.wait()
-    if not second:
-        gather.drain()
-        for copy in biases:
-            copy.wait()
-        db_out[...] = dbv[0] + dbv[1] + dbv[2] + dbv[3]
-
-
-def run_backward(seqs, d, rhs, weight, second, more):
-    (wide, width), total = weight.shape, d.shape[1]
+    db_out[...] = dbv[0] + dbv[1] + dbv[2] + dbv[3]
+
+
+def run_backward(d, h1, x, w2, w1, pre, cell, h, sel, dsel, db):
+    (wide, width), total, seqs = w1.shape, d.shape[1], db.shape[0]
     hidden, length = wide // 6, total // seqs
-    third, span = width // THIRDS, length // 8
-    outs = [shape((6, hidden, width), BF16)]
-    scratch = [pltpu.VMEM((wide, total), BF16), pltpu.VMEM((wide, width), BF16)]
+    third, span, picked = width // THIRDS, length // 8, dsel.shape[1]
+    rows, count = hidden // PIECES, length // 16 * hidden // LANES
+    assert picked == length and length == 8 * LANES
     vmem = pl.BlockSpec(memory_space=pltpu.VMEM)
-    if second:
-        outs += [shape((wide, total), BF16), shape((seqs, hidden, 1), F32)]
-        rows, cols = hidden, length
-        scratch += [
-            pltpu.VMEM((2, third, total), BF16),
-            pltpu.VMEM((3 * hidden, total), BF16),
-            pltpu.VMEM((hidden, total), F32),
-            pltpu.VMEM((2, hidden, length), F32),
-            pltpu.VMEM((2, hidden, LANES), F32),
-            pltpu.VMEM((hidden, total), BF16),
-        ]
-    else:
-        picked = more[2].shape[1]
-        outs += [
+    scratch = [
+        pltpu.VMEM((wide, total), BF16),
+        pltpu.VMEM((wide, width), BF16),
+        pltpu.VMEM((third, total), BF16),
+        pltpu.VMEM((total, third), BF16),
+        pltpu.VMEM((3 * hidden, total), BF16),
+        pltpu.VMEM((hidden, total), F32),
+        pltpu.VMEM((2, hidden, length), F32),
+        pltpu.VMEM((2, hidden, LANES), F32),
+        pltpu.VMEM((hidden, total), BF16),
+        pltpu.VMEM((seqs, span, width), BF16),
+        pltpu.VMEM((hidden, picked), BF16),
+        pltpu.VMEM((2, hidden, third), BF16),
+        pltpu.VMEM(h.shape, BF16),
+        pltpu.VMEM((seqs, span, width), BF16),
+        pltpu.VMEM((seqs, hidden, 1), F32),
+        pltpu.VMEM((4, 8, hidden), F32),
+        pltpu.VMEM((OWN, hidden, third), BF16),
+        pltpu.VMEM((SLOTS, rows, third), BF16),
+        pltpu.VMEM((SLOTS, rows, third), BF16),
+        pltpu.VMEM((SLOTS, rows, third), BF16),
+        pltpu.VMEM((2, 2, 2, count, 16, LANES), BF16),
+        pltpu.VMEM((seqs, 2, 2, count, 16, LANES), BF16),
+        pltpu.VMEM((seqs, 2, count // 2, 16, LANES), BF16),
+        pltpu.VMEM((seqs, 2, count // 2, 16, LANES), BF16),
+        pltpu.VMEM((seqs, count // 2, 16, LANES), BF16),
+        pltpu.VMEM((seqs, count // 2, 16, LANES), BF16),
+        pltpu.SemaphoreType.DMA((7, SLOTS)),
+        pltpu.SemaphoreType.DMA((2, seqs, 5, 2)),
+        pltpu.SemaphoreType.DMA((4, 2)),
+        pltpu.SemaphoreType.DMA((8, 2)),
+        pltpu.SemaphoreType.DMA((11, 2)),
+        pltpu.SemaphoreType.DMA((19,)),
+    ]
+    return pl.pallas_call(
+        functools.partial(backward_kernel, seqs, hidden, length, width),
+        name="backward",
+        in_specs=[ANY] * 10 + [vmem],
+        out_specs=[ANY] * 5 + [vmem],
+        out_shape=[
+            shape((12, hidden, width), BF16),
             shape((seqs, span, width), BF16),
             shape((seqs, span, width), BF16),
             shape((2, width, picked), BF16),
             shape((2, hidden, width), BF16),
             shape((8, hidden), F32),
-        ]
-        rows, cols = span, width
-        scratch += [
-            pltpu.VMEM((2, total, third), BF16),
-            pltpu.VMEM((seqs, span, width), BF16),
-            pltpu.VMEM((2, third, picked), BF16),
-            pltpu.VMEM((hidden, picked), BF16),
-            pltpu.VMEM((2, hidden, third), BF16),
-            pltpu.VMEM(more[0].shape, BF16),
-            pltpu.VMEM((seqs, span, width), BF16),
-            pltpu.VMEM((4, 8, hidden), F32),
-            pltpu.SemaphoreType.DMA((4, 2)),
-            pltpu.SemaphoreType.DMA((8, 2)),
-            pltpu.SemaphoreType.DMA((11, 2)),
-        ]
-    operands = (d, rhs, weight) + more
-    return pl.pallas_call(
-        functools.partial(backward_kernel, second, seqs, hidden, length, width),
-        name="layer_two_backward" if second else "layer_one_backward",
-        in_specs=[ANY] * 5 if second else [ANY] * 6 + [vmem] * 2,
-        out_specs=[ANY] * (len(outs) - 1) + [vmem],
-        out_shape=outs,
-        scratch_shapes=scratch + sum_scratch(seqs, hidden, third, rows, cols),
-        compiler_params=params(collective_id=1 if second else 2, has_side_effects=True),
-    )(*operands)
+        ],
+        scratch_shapes=scratch + [pltpu.SemaphoreType.REGULAR] * 4,
+        compiler_params=params(collective_id=1, has_side_effects=True),
+    )(d, h1, x, w2, w1, pre, cell, h, sel, dsel, db)
 
 
 def reorder(piece, groups, back):
@@ -971,7 +993,7 @@
 def forward_kernel(seqs, hidden, length, width, *refs):
     x_in, w1_in, w2_in, cot_in, b1_in, b2_in, starts = refs[:7]
     x_out, h1_out, pre_out, cell_out, h2_out, d_out, db_out, sel_out, dsel_out = refs[7:16]
-    xg, hg, w, p, pre, cell, work, edge, dv, seed, grad, hv, h2t, raw, cot, sent, b1, b2, pick, sel, dsel = refs[16:37]
+    xg, hg, w, p, pre, cell, work, edge, dv, seed, grad, hv, h2t, raw, cot, sent, b1, b2, chosen, sel, dsel = refs[16:37]
     xsem, hsem, ssem, zsem, lsem = refs[37:]
     here = Here()
     groups = length // LANES
@@ -1105,15 +1127,15 @@
         for j in range(groups):
             code = lax.broadcasted_iota(jnp.int32, (LANES, LANES), 0) * groups + j
             at = pl.ds(j * LANES, LANES)
-            pick[s, at, pl.ds(0, LANES)] = (code == step).astype(BF16)
-            pick[s, at, pl.ds(LANES, LANES)] = (code == step - 1).astype(BF16)
+            chosen[s, at, pl.ds(0, LANES)] = (code == step).astype(BF16)
+            chosen[s, at, pl.ds(LANES, LANES)] = (code == step - 1).astype(BF16)
 
     def held(s, count):
         start = here.z * (seqs * LANES) + s * LANES
         return pl.ds(pl.multiple_of(start, LANES), count * LANES)
 
     def pick_hidden(s):
-        got = dot(hg[here.b, :, columns_of(s)], pick[s], NN).astype(BF16)
+        got = dot(hg[here.b, :, columns_of(s)], chosen[s], NN).astype(BF16)
         for tap in range(2):
             sel[tap, :, held(s, 1)] = got[:, tap * LANES : (tap + 1) * LANES]
 
@@ -1124,7 +1146,7 @@
             begin = starts[s, k]
             inside = jnp.logical_and(step >= begin, step < begin + CLUSTER)
             again = jnp.logical_or(again, jnp.logical_and(inside, lane // CLUSTER > k))
-        got = dot(dv[s, pl.ds(2 * hidden, hidden), :], pick[s, :, pl.ds(0, LANES)], NN)
+        got = dot(dv[s, pl.ds(2 * hidden, hidden), :], chosen[s, :, pl.ds(0, LANES)], NN)
         dsel[:, held(s, 1)] = jnp.where(jnp.broadcast_to(again, (hidden, LANES)), 0.0, got).astype(BF16)
 
     spread_h = []
@@ -1279,9 +1301,12 @@
     )(x, w1, w2, cotangent, b1, b2, starts)
 
 
-def widen_kernel(one_ref, two_ref, outgate_ref, wide_one_ref, wide_two_ref):
+def finish_kernel(
+    one_ref, two_ref, outgate_ref, h_ref, gx_ref, db_ref, wide_one_ref, wide_two_ref, h_out, gx_out, db1_out, db2_out
+):
+    i = pl.program_id(0)
     wide_one_ref[...] = one_ref[...].astype(F32)
-    last = lax.rem(pl.program_id(0), 3) == 2
+    last = lax.rem(i, 3) == 2
 
     @pl.when(last)
     def _():
@@ -1291,23 +1316,36 @@
     def _():
         wide_two_ref[...] = two_ref[...].astype(F32)
 
-
-def widen(one, two, outgate):
-    _, hidden, width = one.shape
+    h_out[...] = h_ref[...]
+    gx_out[...] = gx_ref[...]
+    db1_out[...] = db_ref[0]
+    db2_out[...] = db_ref[1]
+
+
+def finish(gw, outgate, h, gx, db):
+    _, hidden, width = gw.shape
+    total = h.shape[0] * h.shape[1]
     dims = (1, hidden, width)
+    small = (total // 4, width)
+    weights = pl.BlockSpec(dims, lambda i: (i, 0, 0))
+    tokens = pl.BlockSpec(small, lambda i: (jnp.minimum(i, 3), 0))
+    bias = pl.BlockSpec((hidden,), lambda i: (0,))
     return pl.pallas_call(
-        widen_kernel,
-        name="weight_gradients",
+        finish_kernel,
+        name="results",
         grid=(6,),
         in_specs=[
-            pl.BlockSpec(dims, lambda k: (k, 0, 0)),
-            pl.BlockSpec(dims, lambda k: (k - k % 3 // 2, 0, 0)),
-            pl.BlockSpec(dims, lambda k: (k // 3, 0, 0)),
+            weights,
+            pl.BlockSpec(dims, lambda i: (6 + i - i % 3 // 2, 0, 0)),
+            pl.BlockSpec(dims, lambda i: (i // 3, 0, 0)),
+            tokens,
+            tokens,
+            pl.BlockSpec(db.shape, lambda i: (0, 0)),
         ],
-        out_specs=[pl.BlockSpec(dims, lambda k: (k, 0, 0))] * 2,
-        out_shape=[shape(one.shape, F32)] * 2,
+        out_specs=[weights, weights, tokens, tokens, bias, bias],
+        out_shape=[shape((6, hidden, width), F32)] * 2 + [shape((total, width), BF16)] * 2 + [shape((hidden,), F32)] * 2,
         compiler_params=params(),
-    )(one, two, outgate)
+    )(gw, gw, outgate, h.reshape(total, width), gx.reshape(total, width), db)
 
 
 def per_device(line, inputs, weight_one, fbias_one, weight_two, fbias_two, cotangent, cluster_starts):
@@ -1326,9 +1364,8 @@
             inputs, w1, fbias_one, w2, fbias_two, cotangent, cluster_starts
         )
         x, h1 = x.reshape(total, width), h1.reshape(width, total)
-        gw2, d1, db1 = run_backward(seqs, d2, h1, w2, True, (pre1, cell1))
-        gw1, gx1, h2, _, wo, db = run_backward(seqs, d1, x, w1, False, (h2, *picked, db1, db2))
-        gw1, gw2 = widen(gw1, gw2, wo)
+        gw, gx1, h2, _, wo, db = run_backward(d2, h1, x, w2, w1, pre1, cell1, h2, *picked, db2)
+        gw1, gw2, h2, gx1, *db = finish(gw, wo, h2, gx1, db)
     else:
         x = inputs.reshape(seqs, piece, groups, width).transpose(0, 2, 1, 3)
         bias1, bias2 = fbias_one[:, None], fbias_two[:, None]
@@ -1354,7 +1391,7 @@
         gx1 = lax.psum_scatter(gx1, "tm", scatter_dimension=2, tiled=True)
         gx1 = gx1.transpose(0, 2, 1, 3).reshape(seqs, span, width)
         db = lax.psum(jnp.stack([db1, db2]).sum(axis=(1, 3)), "seq")
-    out = h2.reshape(seqs, span, width)
+    out, gx1 = h2.reshape(seqs, span, width), gx1.reshape(seqs, span, width)
     dims = weight_one.shape
     return (out, gx1, gw1.reshape(dims), db[0], gw2.reshape(dims), db[1])
 

time: 494 us -> 467 us (0.945)
  Pallas kernels: 482 us -> 461 us
  local copies, waits for them, and re-layouts: 6.1 us -> 0 us
    pallas_call x3 -> x2, Pallas kernels: 356 us -> 335 us  [the longest x1 317 us: run_backward(): pl.pallas_call(functools.partial(backward_kernel, seqs, hidden, length, w...]
where the time goes in v6:
time: 467 us; the launch traced here: 462 us
  Pallas kernels  461 us (99%)
    pallas_call x1, Pallas kernels, run_backward(): pl.pallas_call(functools.partial(backward_kernel, seqs, hidden, length, w...  317 us
    pallas_call x1, Pallas kernels, run_forward(): pl.pallas_call(functools.partial(forward_kernel, seqs, hidden, length, wi...  126 us
    pallas_call x1, Pallas kernels, finish(): pl.pallas_call(finish_kernel, name='results', grid=(6,), in_specs=[weight...  17.6 us

profile of v6, /device:TPU:0, one launch (start us, length us, event | category | flops | bytes accessed | tf_op | source)
XLA Modules:
  0.0 461.8 jit_solution(10397316040920885022)
XLA Ops:
  0.6 125.8 %forward.1 = (bf16[2,8,8,16,2304]{4,3,2,1,0:T(8,128)(2,1)}, bf16[8,288,2048]{2,1,0:T(8,128)(2,1)}, bf16[864,2048]{1,0:T(8,128)(2,1)}, f32[288,2048]{1,0:T(8,128)...) custom-call(bf16[2,128,2304]{2,1,0:T(8,128)(2,1)} %refs_0_.1, ...), custom_call_target="tpu_custom_call" | custom-call | tf_op jit(solution)/shard_map/forward/pallas_call | solution.py:1256
  126.5 317.3 %backward.1 = (bf16[12,288,2304]{2,1,0:T(8,128)(2,1)}, bf16[2,128,2304]{2,1,0:T(8,128)(2,1)}, bf16[2,128,2304]{2,1,0:T(8,128)(2,1)}, bf16[2,2304,1024]{2,1,0:T(8...) custom-call(bf16[1728,2048]{1,0:T(8,128)(2,1)} %get-tuple-element.26.refs_0_, bf16[2304,2048]{1,0:T(8,128)(2,1)} %bitcast.15, ...), custom_call_target="tpu_custom_call" | custom-call | tf_op jit(solution)/shard_map/backward/pallas_call | solution.py:897
  443.7 17.6 %results.1 = (f32[6,288,2304]{2,1,0:T(8,128)}, f32[6,288,2304]{2,1,0:T(8,128)}, bf16[256,2304]{1,0:T(8,128)(2,1)}, bf16[256,2304]{1,0:T(8,128)(2,1)}, f32[288]{0:T(512)}, /*index=5*/f32[288]{0:T(512)}) custom-call(bf16[12,288,2304]{2,1,0:T(8,128)(2,1)} %get-tuple-element.35.one_ref.two_ref, bf16[12,288,2304]{2,1,0:T(8,128)(2,1)} %get-tuple-element.35.one_ref.two_ref, ...), custom_call_target="tpu_custom_call" | custom-call | tf_op jit(solution)/shard_map/results/pallas_call | solution.py:1333

commit v7 on v6

--- a/solution.py
+++ b/solution.py
@@ -331,10 +331,12 @@
     pl.semaphore_signal(sem, inc=1, device_id=target, device_id_type=MESH)
 
 
-def meet(targets):
+def meet(targets, between=None):
     barrier = pltpu.get_barrier_semaphore()
     for target in targets:
         signal(barrier, target)
+    if between is not None:
+        between()
     pl.semaphore_wait(barrier, len(targets))
 
 
@@ -581,6 +583,8 @@
 
     def load_d(k):
         rows = pl.ds(k * hidden, hidden)
+        if not isinstance(k, int):
+            rows = pl.ds(pl.multiple_of(k * hidden, 16), hidden)
         return load(d_in.at[rows], dv.at[rows], k)
 
     def load_rhs(layer, t):
@@ -621,13 +625,18 @@
 
     done, spent = [0], [0]
 
-    def units(layer, t, low, high):
-        start = t * 4 if layer == 2 else LATER + t * 6
-        assert start + high <= OWN or spent[0] > (start + high - OWN) * PIECES - 1 + SLOTS
+    def units(layer, t):
+        count = 4 if layer == 2 else 6
+        start = t * count + (LATER if layer == 1 else 0)
+        assert start + count <= OWN or spent[0] > (start + count - OWN) * PIECES - 1 + SLOTS
+        first = spent[0]
 
         def unit(k, carry):
             block = start + k
-            rows = pl.ds(pl.multiple_of(ar.product(block) * hidden, 16), hidden)
+            product = ar.product(block)
+            if start == 0:
+                load_d(product).wait()
+            rows = pl.ds(pl.multiple_of(product * hidden, 16), hidden)
             got = dot(dv[rows, :], rh[...], NT) if layer == 2 else dot(dv[rows, :], rx[...], NN)
             own[lax.rem(block, OWN)] = got.astype(BF16)
             if start == 0:
@@ -638,10 +647,19 @@
                     def _(u=u):
                         ar.offer(u)
 
+            else:
+
+                @pl.when(lax.rem(k, 2) == 1)
+                def _():
+                    ar.tick(first + k // 2)
+
             return carry
 
-        lax.fori_loop(low, high, unit, 0)
-        done[0] = (start + high) * PIECES
+        lax.fori_loop(0, count, unit, 0)
+        done[0] = (start + count) * PIECES
+        if start:
+            spent[0] += count // 2
+            assert first + AHEAD < (start + 2) * PIECES and spent[0] - 1 + AHEAD < done[0]
 
     def tick(count=1):
         first = spent[0]
@@ -713,125 +731,123 @@
         first = s * length
         pool_backward(first, grad, pre, cell, first, dv, db1.at[s], work, edge, hidden, groups)
 
-    def load_picked(t):
-        at = pl.ds(t * third, third)
-        size = rh.shape[1] // 2
-        return [load(sel_out.at[tap, at], rh.at[:, pl.ds(tap * size, size)], 15 + tap) for tap in range(2)]
+    size = rh.shape[1] // 2
+
+    def third_of(t):
+        return pl.ds(pl.multiple_of(t * third, LANES), third)
+
+    def load_picked(t, tap):
+        return load(sel_out.at[tap, third_of(t)], rh.at[:, pl.ds(pl.multiple_of(tap * size, LANES), size)], 15 + tap)
 
     def store_o(t, tap):
-        return load(wo.at[tap], wo_out.at[tap, :, pl.ds(t * third, third)], 17 + tap)
-
-    def outgate(t):
-        size = rh.shape[1] // 2
-        for tap, copy in enumerate(load_picked(t)):
-            copy.wait()
-            if t:
+        return load(wo.at[tap], wo_out.at[tap, :, third_of(t)], 17 + tap)
+
+    def outgate():
+        first = spent[0]
+        spent[0] += 6
+
+        def step(i, carry):
+            t, tap = i // 2, lax.rem(i, 2)
+            load_picked(t, tap).wait()
+
+            @pl.when(t > 0)
+            def _():
                 store_o(t - 1, tap).wait()
-            wo[tap] = dot(dsel[...], rh[:, pl.ds(tap * size, size)], NT).astype(BF16)
+
+            values = rh[:, pl.ds(pl.multiple_of(tap * size, LANES), size)]
+            wo[tap] = dot(dsel[...], values, NT).astype(BF16)
             store_o(t, tap).start()
-        if t + 1 < THIRDS:
-            for copy in load_picked(t + 1):
-                copy.start()
+
+            @pl.when(t + 1 < THIRDS)
+            def _():
+                load_picked(t + 1, tap).start()
+
+            ar.tick(first + i)
+            return carry
+
+        lax.fori_loop(0, 2 * THIRDS, step, 0)
 
     load_rhs(2, 0).wait()
-    load_d(0).wait()
-    load_d(1).wait()
-    units(2, 0, 0, 2)
-    for k in range(2, 6):
-        load_d(k).wait()
-    units(2, 0, 2, 4)
+    units(2, 0)
     load_rhs(2, 1).start()
+    load_d(2).wait()
+    load_d(5).wait()
     load_w[2].wait()
     input_grad(2, 0)
     sums[2].start(0)
     tick()
     load_rhs(2, 1).wait()
-    units(2, 1, 0, 2)
+    units(2, 1)
+    load_rhs(2, 2).start()
     sums[2].cross(0)
-    tick(2)
-    units(2, 1, 2, 4)
-    load_rhs(2, 2).start()
+    tick()
     input_grad(2, 1)
     load_w[1].start()
     sums[2].start(1)
+    tick()
     sums[2].turn(0)
+    tick()
     load_rhs(2, 2).wait()
-    tick(2)
-    units(2, 2, 0, 2)
+    units(2, 2)
+    sums[2].cross(1)
     tick()
-    sums[2].cross(1)
-    units(2, 2, 2, 4)
-    tick(2)
     settle(2, 0)
     tick(2)
     load_p.wait()
     load_c.wait()
     pool(0)
-    tick()
+    tick(2)
     sums[2].turn(1)
     gather.start()
-    tick(3)
+    tick(2)
     settle(2, 1)
     for target in (here.core, here.across_x, here.across_y):
         signal(ready, target)
     pool(1)
     tick(2)
     load_rhs(1, 0).wait()
-    units(1, 0, 0, 3)
-    tick()
+    units(1, 0)
     gather.relay()
-    units(1, 0, 3, 6)
     load_rhs(1, 1).start()
     dbv[here.z] = jnp.zeros((8, hidden), F32)
     for row, db in enumerate((db1, db2)):
         dbv[here.z, row : row + 1, :] = to_row(sum(db[s] for s in range(1, seqs)) + db[0])
     for copy in biases:
         copy.start()
-    tick(2)
     load_w[1].wait()
     pl.semaphore_wait(ready, 3)
     input_grad(1, 0)
     sums[1].start(0)
     load_rhs(1, 1).wait()
-    units(1, 1, 0, 2)
-    tick()
-    units(1, 1, 2, 4)
-    tick()
+    units(1, 1)
+    load_rhs(1, 2).start()
     sums[1].cross(0)
     tick()
     input_grad(1, 1)
     sums[1].start(1)
-    units(1, 1, 4, 6)
-    load_rhs(1, 2).start()
-    tick(2)
+    tick()
     gather.share()
     tick()
     sums[1].cross(1)
     tick()
     sums[1].turn(0)
+    tick(5)
+    load_rhs(1, 2).wait()
+    units(1, 2)
     tick(2)
-    load_rhs(1, 2).wait()
-    units(1, 2, 0, 2)
-    tick(2)
-    units(1, 2, 2, 4)
-    tick(3)
-    units(1, 2, 4, 6)
-    tick(4)
     settle(1, 0)
     sums[1].turn(1)
     keep.wait()
     load_e.wait()
-    for copy in load_picked(0):
-        copy.start()
+    for tap in range(2):
+        load_picked(0, tap).start()
     tick(2)
     for copy in spread:
         copy.start()
     tick(4)
     settle(1, 1)
     store_g.start()
-    for t in range(THIRDS):
-        tick(2)
-        outgate(t)
+    outgate()
     for copy in spread:
         copy.wait()
     back = reorder(piece, groups, True)
@@ -1034,15 +1050,16 @@
         copy.start()
     load_w1.start()
     load_c.start()
-    meet(here.peers + here.line)
+    order = reorder(piece, groups, False)
+
+    def place():
+        for s in range(seqs):
+            load_x[s].wait()
+            xg[s, :, here.b] = dot(order, raw[s], NN).astype(BF16).reshape(groups, piece, width)
+
+    meet(here.peers + here.line, place)
     xs = [Gather(here, x_region(s), xsem.at[s]) for s in range(seqs)]
     hs = [Gather(here, h_region(s), hsem.at[s]) for s in range(seqs)]
-    order = reorder(piece, groups, False)
-
-    def place(s):
-        load_x[s].wait()
-        xg[s, :, here.b] = dot(order, raw[s], NN).astype(BF16).reshape(groups, piece, width)
-        xs[s].start()
 
     def prepare():
         load_c.wait()
@@ -1159,10 +1176,10 @@
     store_s = load(sel, sel_out, 15)
     store_e = load(dsel, dsel_out, 16)
 
-    place(0)
+    xs[0].start()
     prepare()
     xs[0].relay()
-    place(1)
+    xs[1].start()
     xs[0].share()
     store_x[0].start()
     load_w1.wait()

time: 467 us -> 463 us (level); the launches traced: 462 us -> 463 us
  no operation moved by 1% of the time
where the time goes in v7:
time: 463 us
  Pallas kernels  462 us (100%)
    pallas_call x1, Pallas kernels, run_backward(): pl.pallas_call(functools.partial(backward_kernel, seqs, hidden, length, w...  319 us
    pallas_call x1, Pallas kernels, run_forward(): pl.pallas_call(functools.partial(forward_kernel, seqs, hidden, length, wi...  125 us
    pallas_call x1, Pallas kernels, finish(): pl.pallas_call(finish_kernel, name='results', grid=(6,), in_specs=[weight...  17.6 us

profile of v7, /device:TPU:0, one launch (start us, length us, event | category | flops | bytes accessed | tf_op | source)
XLA Modules:
  0.0 463.0 jit_solution(6262314798190997008)
XLA Ops:
  0.6 125.5 %forward.1 = (bf16[2,8,8,16,2304]{4,3,2,1,0:T(8,128)(2,1)}, bf16[8,288,2048]{2,1,0:T(8,128)(2,1)}, bf16[864,2048]{1,0:T(8,128)(2,1)}, f32[288,2048]{1,0:T(8,128)...) custom-call(bf16[2,128,2304]{2,1,0:T(8,128)(2,1)} %refs_0_.1, ...), custom_call_target="tpu_custom_call" | custom-call | tf_op jit(solution)/shard_map/forward/pallas_call | solution.py:1273
  126.1 319.1 %backward.1 = (bf16[12,288,2304]{2,1,0:T(8,128)(2,1)}, bf16[2,128,2304]{2,1,0:T(8,128)(2,1)}, bf16[2,128,2304]{2,1,0:T(8,128)(2,1)}, bf16[2,2304,1024]{2,1,0:T(8...) custom-call(bf16[1728,2048]{1,0:T(8,128)(2,1)} %get-tuple-element.26.refs_0_, bf16[2304,2048]{1,0:T(8,128)(2,1)} %bitcast.15, ...), custom_call_target="tpu_custom_call" | custom-call | tf_op jit(solution)/shard_map/backward/pallas_call | solution.py:913
  445.2 17.6 %results.1 = (f32[6,288,2304]{2,1,0:T(8,128)}, f32[6,288,2304]{2,1,0:T(8,128)}, bf16[256,2304]{1,0:T(8,128)(2,1)}, bf16[256,2304]{1,0:T(8,128)(2,1)}, f32[288]{0:T(512)}, /*index=5*/f32[288]{0:T(512)}) custom-call(bf16[12,288,2304]{2,1,0:T(8,128)(2,1)} %get-tuple-element.35.one_ref.two_ref, bf16[12,288,2304]{2,1,0:T(8,128)(2,1)} %get-tuple-element.35.one_ref.two_ref, ...), custom_call_target="tpu_custom_call" | custom-call | tf_op jit(solution)/shard_map/results/pallas_call | solution.py:1350

commit v8 on v7

--- a/solution.py
+++ b/solution.py
@@ -35,6 +35,14 @@
     lax.fori_loop(0, count // rows, step, 0)
 
 
+def aligned(start):
+    return start if isinstance(start, int) else pl.multiple_of(start, LANES)
+
+
+def stretch(hidden):
+    return 96 if hidden % 96 == 0 else ROWS
+
+
 def shift_lanes(v, amount, lane, fill):
     moved = pltpu.roll(v, amount % LANES, axis=1)
     gone = lane < amount if amount > 0 else lane >= LANES + amount
@@ -51,19 +59,20 @@
 
 
 def pool_forward(first, p_ref, b_ref, pre_ref, cell_ref, target, h_ref, factor_ref, edge_ref, hidden, groups):
-    lane = lax.broadcasted_iota(jnp.int32, (ROWS, LANES), 1)
+    size = stretch(hidden)
+    lane = lax.broadcasted_iota(jnp.int32, (size, LANES), 1)
 
     def at(j, start=0):
         return pl.ds(start + j * LANES, LANES)
 
     def gates(r):
-        rows = pl.ds(r, ROWS)
+        rows = pl.ds(r, size)
         value = factor = None
         for j in range(groups):
             got = []
             for g in range(3):
-                now = p_ref[pl.ds(g * hidden + r, ROWS), at(j)]
-                tap = pl.ds((3 + g) * hidden + r, ROWS)
+                now = p_ref[pl.ds(g * hidden + r, size), at(j)]
+                tap = pl.ds((3 + g) * hidden + r, size)
                 if j:
                     past = p_ref[tap, at(j - 1)]
                 else:
@@ -72,7 +81,7 @@
                 if g == 1:
                     total = total + b_ref[rows, :]
                 total = total.astype(BF16)
-                pre_ref[pl.ds(g * hidden + r, ROWS), at(j, first)] = total
+                pre_ref[pl.ds(g * hidden + r, size), at(j, first)] = total
                 got.append(total.astype(F32))
             forget = sigmoid(got[1])
             fresh = (1.0 - forget) * jnp.tanh(got[0])
@@ -84,30 +93,28 @@
             cell_ref[rows, at(j, first)] = value
             factor_ref[rows, at(j)] = factor
 
-    tiles(hidden, ROWS, gates)
-
-    def chain(r):
-        rows = pl.ds(r, ROWS)
-        value = lane_chain(factor_ref[rows, at(groups - 1)], cell_ref[rows, at(groups - 1, first)], lane, 1)
-        edge_ref[rows, :] = shift_lanes(value, 1, lane, 0.0)
-
-    tiles(hidden, ROWS, chain)
+    tiles(hidden, size, gates)
+
+    everywhere = lax.broadcasted_iota(jnp.int32, (hidden, LANES), 1)
+    value = lane_chain(factor_ref[:, at(groups - 1)], cell_ref[:, at(groups - 1, first)], everywhere, 1)
+    edge_ref[...] = shift_lanes(value, 1, everywhere, 0.0)
 
     def finish(r):
-        rows = pl.ds(r, ROWS)
+        rows = pl.ds(r, size)
         edge = edge_ref[rows, :]
         for j in range(groups):
             cell = cell_ref[rows, at(j, first)] + factor_ref[rows, at(j)] * edge
             cell_ref[rows, at(j, first)] = cell
-            outgate = sigmoid(pre_ref[pl.ds(2 * hidden + r, ROWS), at(j, first)].astype(F32))
+            outgate = sigmoid(pre_ref[pl.ds(2 * hidden + r, size), at(j, first)].astype(F32))
             h_ref[rows, at(j, target)] = (outgate * cell).astype(BF16)
 
-    tiles(hidden, ROWS, finish)
+    tiles(hidden, size, finish)
 
 
 def put_gate(d_ref, g, r, j, v, target, lane, hidden, groups):
-    d_ref[pl.ds(g * hidden + r, ROWS), pl.ds(target + j * LANES, LANES)] = v
-    tap = pl.ds((3 + g) * hidden + r, ROWS)
+    rows = v.shape[0]
+    d_ref[pl.ds(g * hidden + r, rows), pl.ds(target + j * LANES, LANES)] = v
+    tap = pl.ds((3 + g) * hidden + r, rows)
     if j:
         d_ref[tap, pl.ds(target + (j - 1) * LANES, LANES)] = v
     else:
@@ -116,32 +123,34 @@
 
 
 def outgate_backward(first, g_ref, pre_ref, cell_ref, d_ref, hidden, groups):
-    lane = lax.broadcasted_iota(jnp.int32, (ROWS, LANES), 1)
+    size = stretch(hidden)
+    lane = lax.broadcasted_iota(jnp.int32, (size, LANES), 1)
 
     def body(r):
-        rows = pl.ds(r, ROWS)
+        rows = pl.ds(r, size)
         for j in range(groups):
             at = pl.ds(first + j * LANES, LANES)
-            outgate = sigmoid(pre_ref[pl.ds(2 * hidden + r, ROWS), at].astype(F32))
+            outgate = sigmoid(pre_ref[pl.ds(2 * hidden + r, size), at].astype(F32))
             v = g_ref[rows, at].astype(F32) * cell_ref[rows, at] * outgate * (1.0 - outgate)
             put_gate(d_ref, 2, r, j, v.astype(BF16), 0, lane, hidden, groups)
 
-    tiles(hidden, ROWS, body)
+    tiles(hidden, size, body)
 
 
 def pool_backward(
     first, g_ref, pre_ref, cell_ref, target, d_ref, db_ref, work_ref, edge_ref, hidden, groups, carried_only=False
 ):
-    lane = lax.broadcasted_iota(jnp.int32, (ROWS, LANES), 1)
+    size = stretch(hidden)
+    lane = lax.broadcasted_iota(jnp.int32, (size, LANES), 1)
 
     def at(j, start=0):
-        return pl.ds(start + j * LANES, LANES)
+        return pl.ds(aligned(start + j * LANES), LANES)
 
     def gate(g, r, j):
-        return pre_ref[pl.ds(g * hidden + r, ROWS), at(j, first)].astype(F32)
+        return pre_ref[pl.ds(g * hidden + r, size), at(j, first)].astype(F32)
 
     def start(r):
-        rows = pl.ds(r, ROWS)
+        rows = pl.ds(r, size)
         later = value = factor = None
         for j in reversed(range(groups)):
             own = g_ref[rows, at(j, first)].astype(F32) * sigmoid(gate(2, r, j))
@@ -156,19 +165,16 @@
         edge_ref[0, rows, :] = later * value
         edge_ref[1, rows, :] = later * factor
 
-    tiles(hidden, ROWS, start)
-
-    def chain(r):
-        rows = pl.ds(r, ROWS)
-        value = lane_chain(edge_ref[1, rows, :], edge_ref[0, rows, :], lane, -1)
-        edge_ref[0, rows, :] = shift_lanes(value, -1, lane, 0.0)
-
-    tiles(hidden, ROWS, chain)
+    tiles(hidden, size, start)
+
+    everywhere = lax.broadcasted_iota(jnp.int32, (hidden, LANES), 1)
+    value = lane_chain(edge_ref[1], edge_ref[0], everywhere, -1)
+    edge_ref[0] = shift_lanes(value, -1, everywhere, 0.0)
 
     def finish(r):
-        rows = pl.ds(r, ROWS)
+        rows = pl.ds(r, size)
         edge = edge_ref[0, rows, :]
-        total = jnp.zeros((ROWS, LANES), F32)
+        total = jnp.zeros((size, LANES), F32)
         before = shift_lanes(cell_ref[rows, at(groups - 1, first)], 1, lane, 0.0)
         for j in range(groups):
             carried = work_ref[0, rows, at(j)] + work_ref[1, rows, at(j)] * edge
@@ -188,7 +194,7 @@
                 put_gate(d_ref, g, r, j, v, target, lane, hidden, groups)
         db_ref[rows, :] = jnp.sum(total, axis=1, keepdims=True)
 
-    tiles(hidden, ROWS, finish)
+    tiles(hidden, size, finish)
 
 
 def first_kernel(hidden, length, w_ref, b_ref, x_ref, pre_ref, cell_ref, h_ref, p_ref, work_ref, edge_ref):
@@ -1016,7 +1022,7 @@
     piece = LANES // 8
 
     def columns_of(s):
-        return pl.ds(s * length, length)
+        return pl.ds(aligned(s * length), length)
 
     def x_region(s):
         def region(b, half):
@@ -1043,7 +1049,10 @@
     store_h = [load(hg.at[:, :, columns_of(s)], h1_out.at[:, :, columns_of(s)], 5 + s) for s in range(seqs)]
     store_p = [load(pre.at[:, columns_of(s)], pre_out.at[:, columns_of(s)], 7 + s) for s in range(seqs)]
     store_c = [load(cell.at[:, columns_of(s)], cell_out.at[:, columns_of(s)], 9 + s) for s in range(seqs)]
-    store_d = [load(dv.at[s], d_out.at[:, columns_of(s)], 11 + s) for s in range(seqs)]
+
+    def store_d(s):
+        return load(dv.at[s], d_out.at[:, columns_of(s)], 11 + s)
+
     store_o = load(h2t, h2_out, 13)
 
     for copy in load_x:
@@ -1130,7 +1139,7 @@
 
     def pool_back(s):
         pool_backward(s * length, grad, pre, cell, 0, dv.at[s], db_out.at[s], work, edge, hidden, groups, True)
-        store_d[s].start()
+        store_d(s).start()
 
     def cluster_steps(s):
         lane = lax.broadcasted_iota(jnp.int32, (1, LANES), 1)
@@ -1252,14 +1261,18 @@
     for copy in spread_h:
         copy.wait()
     store_s.start()
-    for s in range(seqs):
+
+    def back(s, carry):
         pool_back(s)
+        return carry
+
+    lax.fori_loop(0, seqs, back, 0)
     for gather in xs + hs:
         gather.drain()
     for copy in spread_d:
         copy.wait()
     store_e.start()
-    for copy in store_x + store_h + store_d + [store_o, store_s, store_e]:
+    for copy in store_x + store_h + [store_d(s) for s in range(seqs)] + [store_o, store_s, store_e]:
         copy.wait()
 
 

time: 463 us -> 454 us (0.981)
  Pallas kernels: 462 us -> 453 us
    pallas_call x1, Pallas kernels: 125 us -> 119 us  [run_forward(): pl.pallas_call(functools.partial(forward_kernel, seqs, hidden, length, wi...]
where the time goes in v8:
time: 454 us
  Pallas kernels  453 us (100%)
    pallas_call x1, Pallas kernels, run_backward(): pl.pallas_call(functools.partial(backward_kernel, seqs, hidden, length, w...  317 us
    pallas_call x1, Pallas kernels, run_forward(): pl.pallas_call(functools.partial(forward_kernel, seqs, hidden, length, wi...  119 us
    pallas_call x1, Pallas kernels, finish(): pl.pallas_call(finish_kernel, name='results', grid=(6,), in_specs=[weight...  17.6 us

profile of v8, /device:TPU:0, one launch (start us, length us, event | category | flops | bytes accessed | tf_op | source)
XLA Modules:
  0.0 453.8 jit_solution(9465733287309884135)
XLA Ops:
  0.6 118.8 %forward.1 = (bf16[2,8,8,16,2304]{4,3,2,1,0:T(8,128)(2,1)}, bf16[8,288,2048]{2,1,0:T(8,128)(2,1)}, bf16[864,2048]{1,0:T(8,128)(2,1)}, f32[288,2048]{1,0:T(8,128)...) custom-call(bf16[2,128,2304]{2,1,0:T(8,128)(2,1)} %refs_0_.1, ...), custom_call_target="tpu_custom_call" | custom-call | tf_op jit(solution)/shard_map/forward/pallas_call | solution.py:1286
  119.4 316.6 %backward.1 = (bf16[12,288,2304]{2,1,0:T(8,128)(2,1)}, bf16[2,128,2304]{2,1,0:T(8,128)(2,1)}, bf16[2,128,2304]{2,1,0:T(8,128)(2,1)}, bf16[2,2304,1024]{2,1,0:T(8...) custom-call(bf16[1728,2048]{1,0:T(8,128)(2,1)} %get-tuple-element.26.refs_0_, bf16[2304,2048]{1,0:T(8,128)(2,1)} %bitcast.15, ...), custom_call_target="tpu_custom_call" | custom-call | tf_op jit(solution)/shard_map/backward/pallas_call | solution.py:919
  436.0 17.6 %results.1 = (f32[6,288,2304]{2,1,0:T(8,128)}, f32[6,288,2304]{2,1,0:T(8,128)}, bf16[256,2304]{1,0:T(8,128)(2,1)}, bf16[256,2304]{1,0:T(8,128)(2,1)}, f32[288]{0:T(512)}, /*index=5*/f32[288]{0:T(512)}) custom-call(bf16[12,288,2304]{2,1,0:T(8,128)(2,1)} %get-tuple-element.35.one_ref.two_ref, bf16[12,288,2304]{2,1,0:T(8,128)(2,1)} %get-tuple-element.35.one_ref.two_ref, ...), custom_call_target="tpu_custom_call" | custom-call | tf_op jit(solution)/shard_map/results/pallas_call | solution.py:1363

commit v9 on v8

--- a/solution.py
+++ b/solution.py
@@ -295,7 +295,7 @@
 
 THIRDS = 3
 PIECES = 3
-SLOTS = 12
+SLOTS = 11
 AHEAD = 6
 BEHIND = 2
 LATER = 12
@@ -570,9 +570,9 @@
     third = width // THIRDS
     d_in, h1_in, x_in, w2_in, w1_in, pre_in, cell_in, h_in, sel_in, dsel_in, db2 = refs[:11]
     gw_out, gx_out, h_out, sel_out, wo_out, db_out = refs[11:17]
-    dv, wv, rh, rx, pre, cell, work, edge, grad, gxv, dsel, wo, heard, hv, db1, dbv = refs[17:33]
-    own, ring_in, ring_mid, total, part, pairs, wide_x, wide_y, last_x, last_y = refs[33:43]
-    zsem, rsem, dsem, hsem, psem, lsem, credit_in, credit_mid, credit_out, ready = refs[43:]
+    dv, wv, rh, rx, pre, cell, work, edge, grad, gxv, dsel, wo, heard, hv, db1, dbv, told = refs[17:34]
+    own, ring_in, ring_mid, total, part, pairs, wide_x, wide_y, last_x, last_y = refs[34:44]
+    zsem, rsem, dsem, hsem, psem, lsem, credit_in, credit_mid, credit_out, ready = refs[44:]
     here = Here()
     ar = SeqSum(here, hidden, third, own, ring_in, ring_mid, total, gw_out, zsem, (credit_in, credit_mid, credit_out))
     sums = {
@@ -625,9 +625,10 @@
         remote(dbv.at[here.z], dbv.at[here.z], dsem.at[d, 0], dsem.at[d, 1], peer)
         for d, peer in enumerate(here.line, 1)
     ]
-    spread = [pltpu.make_async_copy(h_in.at[here.b], heard.at[here.b], hsem.at[0, 0])]
+    load_h = load(h_in, grad, 19)
+    spread = [pltpu.make_async_copy(told.at[here.b], heard.at[here.b], hsem.at[0, 0])]
     for d, peer in enumerate(here.peers, 1):
-        spread.append(remote(h_in.at[peer["tm"]], heard.at[here.b], hsem.at[d, 0], hsem.at[d, 1], peer))
+        spread.append(remote(told.at[peer["tm"]], heard.at[here.b], hsem.at[d, 0], hsem.at[d, 1], peer))
 
     done, spent = [0], [0]
 
@@ -810,6 +811,7 @@
     for target in (here.core, here.across_x, here.across_y):
         signal(ready, target)
     pool(1)
+    load_h.start()
     tick(2)
     load_rhs(1, 0).wait()
     units(1, 0)
@@ -848,6 +850,11 @@
     for tap in range(2):
         load_picked(0, tap).start()
     tick(2)
+    load_h.wait()
+    eye = identity(LANES)
+    for n in range(seqs * groups):
+        turned = dot(eye, grad[:, pl.ds(n * LANES, LANES)], NT).astype(BF16)
+        told[:, pl.ds(n * piece, piece), :] = turned.reshape(8, piece, hidden)
     for copy in spread:
         copy.start()
     tick(4)
@@ -895,10 +902,11 @@
         pltpu.VMEM((seqs, span, width), BF16),
         pltpu.VMEM((hidden, picked), BF16),
         pltpu.VMEM((2, hidden, third), BF16),
-        pltpu.VMEM(h.shape, BF16),
+        pltpu.VMEM((8, total // 8, hidden), BF16),
         pltpu.VMEM((seqs, span, width), BF16),
         pltpu.VMEM((seqs, hidden, 1), F32),
         pltpu.VMEM((4, 8, hidden), F32),
+        pltpu.VMEM((8, total // 8, hidden), BF16),
         pltpu.VMEM((OWN, hidden, third), BF16),
         pltpu.VMEM((SLOTS, rows, third), BF16),
         pltpu.VMEM((SLOTS, rows, third), BF16),
@@ -914,7 +922,7 @@
         pltpu.SemaphoreType.DMA((4, 2)),
         pltpu.SemaphoreType.DMA((8, 2)),
         pltpu.SemaphoreType.DMA((11, 2)),
-        pltpu.SemaphoreType.DMA((19,)),
+        pltpu.SemaphoreType.DMA((20,)),
     ]
     return pl.pallas_call(
         functools.partial(backward_kernel, seqs, hidden, length, width),
@@ -939,6 +947,11 @@
     a = lax.broadcasted_iota(jnp.int32, (span, span), 1 if back else 0)
     b = lax.broadcasted_iota(jnp.int32, (span, span), 0 if back else 1)
     return (b == lax.rem(a, piece) * groups + a // piece).astype(BF16)
+
+
+def identity(n):
+    rows, cols = (lax.broadcasted_iota(jnp.int32, (n, n), axis) for axis in range(2))
+    return (rows == cols).astype(BF16)
 
 
 def to_row(column):
@@ -1015,8 +1028,8 @@
 def forward_kernel(seqs, hidden, length, width, *refs):
     x_in, w1_in, w2_in, cot_in, b1_in, b2_in, starts = refs[:7]
     x_out, h1_out, pre_out, cell_out, h2_out, d_out, db_out, sel_out, dsel_out = refs[7:16]
-    xg, hg, w, p, pre, cell, work, edge, dv, seed, grad, hv, h2t, raw, cot, sent, b1, b2, chosen, sel, dsel = refs[16:37]
-    xsem, hsem, ssem, zsem, lsem = refs[37:]
+    xg, hg, w, p, pre, cell, work, edge, dv, seed, grad, hv, raw, cot, sent, b1, b2, chosen, sel, dsel = refs[16:36]
+    xsem, hsem, ssem, zsem, lsem = refs[36:]
     here = Here()
     groups = length // LANES
     piece = LANES // 8
@@ -1053,7 +1066,7 @@
     def store_d(s):
         return load(dv.at[s], d_out.at[:, columns_of(s)], 11 + s)
 
-    store_o = load(h2t, h2_out, 13)
+    store_o = load(hv, h2_out, 13)
 
     for copy in load_x:
         copy.start()
@@ -1084,9 +1097,13 @@
         b2[...] = to_column(b2_in[...][None, :])
 
     late = [
-        (remote(sent.at[peer["tm"]], seed.at[:, :, here.b], ssem.at[d, 0], ssem.at[d, 1], peer), peer)
-        for d, peer in enumerate(here.peers, 1)
+        [
+            remote(sent.at[peer["tm"], s], seed.at[s, :, here.b], ssem.at[d, s, 0], ssem.at[d, s, 1], peer)
+            for d, peer in enumerate(here.peers, 1)
+        ]
+        for s in range(seqs)
     ]
+    early = pltpu.make_async_copy(sent.at[here.b], seed.at[:, :, here.b], ssem.at[0, 0, 0])
 
     def first_products(s):
         def block(r):
@@ -1112,23 +1129,14 @@
         pool_forward(first, p, b1, pre, cell, first, hg.at[here.b], work.at[0], edge.at[0], hidden, groups)
 
     def second_pool(s):
-        pool_forward(s * length, p, b2, pre, cell, 0, hv, work.at[0], edge.at[0], hidden, groups)
-        rows = lax.broadcasted_iota(jnp.int32, (LANES, LANES), 0)
-        cols = lax.broadcasted_iota(jnp.int32, (LANES, LANES), 1)
-        eye = (rows == cols).astype(BF16)
-        for j in range(groups):
-            turned = dot(eye, hv[:, pl.ds(j * LANES, LANES)], NT).astype(BF16)
-            at = pl.ds((s * groups + j) * piece, piece)
-            h2t[:, at, :] = turned.reshape(8, piece, hidden)
+        pool_forward(s * length, p, b2, pre, cell, s * length, hv, work.at[0], edge.at[0], hidden, groups)
 
     def incoming(s):
-        rows = lax.broadcasted_iota(jnp.int32, (hidden, hidden), 0)
-        cols = lax.broadcasted_iota(jnp.int32, (hidden, hidden), 1)
-        eye = (rows == cols).astype(BF16)
+        eye = identity(LANES)
         lane = lax.broadcasted_iota(jnp.int32, (1, LANES), 1)
         for j in range(groups):
             block = seed[s, j].reshape(LANES, hidden)
-            turned = dot(eye, block, NT)
+            turned = dot(block, eye, TN)
             step = lane * groups + j
             keep = jnp.zeros((1, LANES), jnp.bool_)
             for k in range(starts.shape[1]):
@@ -1176,12 +1184,13 @@
         dsel[:, held(s, 1)] = jnp.where(jnp.broadcast_to(again, (hidden, LANES)), 0.0, got).astype(BF16)
 
     spread_h = []
-    spread_d = []
+    spread_d = [[] for _ in range(seqs)]
     for d, peer in enumerate(here.line, 1):
         at = sel.at[:, :, held(0, seqs)]
         spread_h.append(remote(at, at, zsem.at[d, 0], zsem.at[d, 1], peer))
-        at = dsel.at[:, held(0, seqs)]
-        spread_d.append(remote(at, at, zsem.at[d, 2], zsem.at[d, 3], peer))
+        for s in range(seqs):
+            at = dsel.at[:, held(s, 1)]
+            spread_d[s].append(remote(at, at, zsem.at[d, 2 + 2 * s], zsem.at[d, 3 + 2 * s], peer))
     store_s = load(sel, sel_out, 15)
     store_e = load(dsel, dsel_out, 16)
 
@@ -1222,8 +1231,8 @@
 
     @pl.when(here.y == 1)
     def _():
-        pltpu.make_async_copy(sent.at[here.b], seed.at[:, :, here.b], ssem.at[0, 0]).start()
-        for copy, _ in late:
+        early.start()
+        for copy in late[0] + late[1]:
             copy.start()
 
     store_p[0].wait()
@@ -1241,23 +1250,20 @@
 
     @pl.when(here.y == 1)
     def _():
-        pltpu.make_async_copy(sent.at[here.b], seed.at[:, :, here.b], ssem.at[0, 0]).wait()
-        for copy, _ in late:
-            copy.wait_send()
-
-    for d, (copy, _) in enumerate(late, 1):
-        source = lax.rem(here.b + 8 - d, 8)
-
-        @pl.when(source >= 4)
-        def _(copy=copy):
-            copy.wait_recv()
+        early.wait()
 
     for s in range(seqs):
+        for d, copy in enumerate(late[s], 1):
+
+            @pl.when(lax.rem(here.b + 8 - d, 8) >= 4)
+            def _(copy=copy):
+                copy.wait_recv()
+
         incoming(s)
         outgate_backward(s * length, grad, pre, cell, dv.at[s], hidden, groups)
         pick_grad(s)
-    for copy in spread_d:
-        copy.start()
+        for copy in spread_d[s]:
+            copy.start()
     for copy in spread_h:
         copy.wait()
     store_s.start()
@@ -1267,9 +1273,14 @@
         return carry
 
     lax.fori_loop(0, seqs, back, 0)
+    @pl.when(here.y == 1)
+    def _():
+        for copy in late[0] + late[1]:
+            copy.wait_send()
+
     for gather in xs + hs:
         gather.drain()
-    for copy in spread_d:
+    for copy in spread_d[0] + spread_d[1]:
         copy.wait()
     store_e.start()
     for copy in store_x + store_h + [store_d(s) for s in range(seqs)] + [store_o, store_s, store_e]:
@@ -1293,7 +1304,7 @@
             shape((8, hidden, total), BF16),
             shape((3 * hidden, total), BF16),
             shape((hidden, total), F32),
-            shape((8, seqs * groups * piece, hidden), BF16),
+            shape((hidden, total), BF16),
             shape((6 * hidden, total), BF16),
             shape((seqs, hidden, 1), F32),
             shape((2, hidden, picked), BF16),
@@ -1311,8 +1322,7 @@
             pltpu.VMEM((seqs, 6 * hidden, length), BF16),
             pltpu.VMEM((seqs, groups, 8, piece, hidden), BF16),
             pltpu.VMEM((hidden, total), BF16),
-            pltpu.VMEM((hidden, length), BF16),
-            pltpu.VMEM((8, seqs * groups * piece, hidden), BF16),
+            pltpu.VMEM((hidden, total), BF16),
             pltpu.VMEM((seqs, span, width), BF16),
             pltpu.VMEM((seqs, span, width), BF16),
             pltpu.VMEM((8, seqs, groups, piece, hidden), BF16),
@@ -1323,8 +1333,8 @@
             pltpu.VMEM((hidden, picked), BF16),
             pltpu.SemaphoreType.DMA((seqs, 11, 2)),
             pltpu.SemaphoreType.DMA((seqs, 11, 2)),
-            pltpu.SemaphoreType.DMA((8, 2)),
-            pltpu.SemaphoreType.DMA((4, 4)),
+            pltpu.SemaphoreType.DMA((8, seqs, 2)),
+            pltpu.SemaphoreType.DMA((4, 2 + 2 * seqs)),
             pltpu.SemaphoreType.DMA((17,)),
         ],
         compiler_params=params(collective_id=0, has_side_effects=True),

time: 454 us -> 448 us (0.987)
  Pallas kernels: 453 us -> 447 us
where the time goes in v9:
time: 448 us
  Pallas kernels  447 us (100%)
    pallas_call x1, Pallas kernels, run_backward(): pl.pallas_call(functools.partial(backward_kernel, seqs, hidden, length, w...  314 us
    pallas_call x1, Pallas kernels, run_forward(): pl.pallas_call(functools.partial(forward_kernel, seqs, hidden, length, wi...  115 us
    pallas_call x1, Pallas kernels, finish(): pl.pallas_call(finish_kernel, name='results', grid=(6,), in_specs=[weight...  17.6 us

profile of v9, /device:TPU:0, one launch (start us, length us, event | category | flops | bytes accessed | tf_op | source)
XLA Modules:
  0.0 447.7 jit_solution(12229756972997069978)
XLA Ops:
  0.6 115.0 %forward.1 = (bf16[2,8,8,16,2304]{4,3,2,1,0:T(8,128)(2,1)}, bf16[8,288,2048]{2,1,0:T(8,128)(2,1)}, bf16[864,2048]{1,0:T(8,128)(2,1)}, f32[288,2048]{1,0:T(8,128)...) custom-call(bf16[2,128,2304]{2,1,0:T(8,128)(2,1)} %refs_0_.1, ...), custom_call_target="tpu_custom_call" | custom-call | tf_op jit(solution)/shard_map/forward/pallas_call | solution.py:1297
  115.6 314.2 %backward.1 = (bf16[12,288,2304]{2,1,0:T(8,128)(2,1)}, bf16[2,128,2304]{2,1,0:T(8,128)(2,1)}, bf16[2,128,2304]{2,1,0:T(8,128)(2,1)}, bf16[2,2304,1024]{2,1,0:T(8...) custom-call(bf16[1728,2048]{1,0:T(8,128)(2,1)} %get-tuple-element.26.refs_0_, bf16[2304,2048]{1,0:T(8,128)(2,1)} %bitcast.15, ...), custom_call_target="tpu_custom_call" | custom-call | tf_op jit(solution)/shard_map/backward/pallas_call | solution.py:927
  429.9 17.6 %results.1 = (f32[6,288,2304]{2,1,0:T(8,128)}, f32[6,288,2304]{2,1,0:T(8,128)}, bf16[256,2304]{1,0:T(8,128)(2,1)}, bf16[256,2304]{1,0:T(8,128)(2,1)}, f32[288]{0:T(512)}, /*index=5*/f32[288]{0:T(512)}) custom-call(bf16[12,288,2304]{2,1,0:T(8,128)(2,1)} %get-tuple-element.35.one_ref.two_ref, bf16[12,288,2304]{2,1,0:T(8,128)(2,1)} %get-tuple-element.35.one_ref.two_ref, ...), custom_call_target="tpu_custom_call" | custom-call | tf_op jit(solution)/shard_map/results/pallas_call | solution.py:1373

commit v10 on v9

--- a/solution.py
+++ b/solution.py
@@ -297,7 +297,7 @@
 PIECES = 3
 SLOTS = 11
 AHEAD = 6
-BEHIND = 2
+BEHIND = 3
 LATER = 12
 BLOCKS = 30
 OWN = 18

time: 448 us -> 449 us (level)
  no operation moved by 1% of the time
where the time goes in v10:
time: 449 us
  Pallas kernels  448 us (100%)
    pallas_call x1, Pallas kernels, run_backward(): pl.pallas_call(functools.partial(backward_kernel, seqs, hidden, length, w...  316 us
    pallas_call x1, Pallas kernels, run_forward(): pl.pallas_call(functools.partial(forward_kernel, seqs, hidden, length, wi...  115 us
    pallas_call x1, Pallas kernels, finish(): pl.pallas_call(finish_kernel, name='results', grid=(6,), in_specs=[weight...  17.6 us

profile of v10, /device:TPU:0, one launch (start us, length us, event | category | flops | bytes accessed | tf_op | source)
XLA Modules:
  0.0 449.1 jit_solution(9845643628377910916)
XLA Ops:
  0.6 115.0 %forward.1 = (bf16[2,8,8,16,2304]{4,3,2,1,0:T(8,128)(2,1)}, bf16[8,288,2048]{2,1,0:T(8,128)(2,1)}, bf16[864,2048]{1,0:T(8,128)(2,1)}, f32[288,2048]{1,0:T(8,128)...) custom-call(bf16[2,128,2304]{2,1,0:T(8,128)(2,1)} %refs_0_.1, ...), custom_call_target="tpu_custom_call" | custom-call | tf_op jit(solution)/shard_map/forward/pallas_call | solution.py:1297
  115.6 315.7 %backward.1 = (bf16[12,288,2304]{2,1,0:T(8,128)(2,1)}, bf16[2,128,2304]{2,1,0:T(8,128)(2,1)}, bf16[2,128,2304]{2,1,0:T(8,128)(2,1)}, bf16[2,2304,1024]{2,1,0:T(8...) custom-call(bf16[1728,2048]{1,0:T(8,128)(2,1)} %get-tuple-element.26.refs_0_, bf16[2304,2048]{1,0:T(8,128)(2,1)} %bitcast.15, ...), custom_call_target="tpu_custom_call" | custom-call | tf_op jit(solution)/shard_map/backward/pallas_call | solution.py:927
  431.3 17.6 %results.1 = (f32[6,288,2304]{2,1,0:T(8,128)}, f32[6,288,2304]{2,1,0:T(8,128)}, bf16[256,2304]{1,0:T(8,128)(2,1)}, bf16[256,2304]{1,0:T(8,128)(2,1)}, f32[288]{0:T(512)}, /*index=5*/f32[288]{0:T(512)}) custom-call(bf16[12,288,2304]{2,1,0:T(8,128)(2,1)} %get-tuple-element.35.one_ref.two_ref, bf16[12,288,2304]{2,1,0:T(8,128)(2,1)} %get-tuple-element.35.one_ref.two_ref, ...), custom_call_target="tpu_custom_call" | custom-call | tf_op jit(solution)/shard_map/results/pallas_call | solution.py:1373
